TPU v7x, 32 devices: a whole 2x2x4 slice. The times are simulated.
32 devices in a mesh: parts: 2 (over x), seq: 8 (over z, y), dp: 2 (over core).
Axes of the slice: x: 2, y: 2, z: 4, core: 2. Of those that a mesh axis runs over, the one named last changes fastest.
Arguments:
- activations: bfloat16 [8, 2048, 1024], P(('parts', 'dp'), 'seq'), parts along dimension 0, may hold values from -36 to 36, as said below
- cotangent: bfloat16 [8, 2048, 1024], P(('parts', 'dp'), 'seq'), parts along dimension 0, may hold values from -6 to 6
- conv_one: bfloat16 [1024, 3, 512], P(('seq', 'dp')), may hold values from -0.109375 to 0.109375
- mix_one: bfloat16 [512, 1024], P(('seq', 'dp')), may hold values from -0.25 to 0.25
- conv_two: bfloat16 [1024, 3, 512], P(('seq', 'dp')), may hold values from -0.109375 to 0.109375
- mix_two: bfloat16 [512, 1024], P(('seq', 'dp')), may hold values from -0.25 to 0.25
Outputs:
- input_grad: bfloat16 [8, 2048, 1024], P(('parts', 'dp'), 'seq'), parts along dimension 0
- grad_conv_one: float32 [2048, 3, 512], P(('parts', 'seq', 'dp')), parts along dimension 0
- grad_mix_one: float32 [1024, 1024], P(('parts', 'seq', 'dp')), parts along dimension 0
- grad_conv_two: float32 [2048, 3, 512], P(('parts', 'seq', 'dp')), parts along dimension 0
- grad_mix_two: float32 [1024, 1024], P(('parts', 'seq', 'dp')), parts along dimension 0
There are 2 independent parts, one for each index of `parts`. A program takes and returns all parts, laid end to end along the dimension named above; an argument that names none is the same for every part. Nothing has to cross between parts.
Inputs may be any that keep to these rules, and one draw needn't show every extreme that they name: activations of earlier layers.
All inputs are finite; a program needn't handle non-finite values.
Results may differ from a plain program's by a relative error of at most 0.007.
Values may be sent and summed in bfloat16 or wider, within the bound.
No kernel may reach another device: no remote copies, remote signals or barrier semaphores. Data moves between devices by JAX's collectives and lax.ppermute only.
A program may use at most 128 MiB of HBM per device.

v0:
```python
import jax
import jax.numpy as jnp
from jax import lax
from jax.sharding import PartitionSpec as P

DILATE_ONE = 64
DILATE_TWO = 128


def with_halo(block, sides, width):
    for axis, dim in sides:
        count = lax.axis_size(axis)
        forward = [(i, i + 1) for i in range(count - 1)]
        backward = [(target, source) for source, target in forward]
        low = lax.ppermute(
            lax.slice_in_dim(block, block.shape[dim] - width, None, axis=dim), axis, forward
        )
        high = lax.ppermute(lax.slice_in_dim(block, 0, width, axis=dim), axis, backward)
        block = jnp.concatenate([low, block, high], axis=dim)
    return block


def prenorm(values):
    scale = lax.rsqrt(jnp.mean(values * values, axis=-1, keepdims=True) + 1e-06)
    return jax.nn.gelu(values * scale)


def fetch(conv_w, mix_w):
    return (
        lax.all_gather(conv_w, ("seq", "dp"), axis=0, tiled=True),
        lax.all_gather(mix_w, ("seq", "dp"), axis=0, tiled=True),
    )


def extended(field, dilate):
    return with_halo(field, (("seq", 1),), dilate)


def views_of(padded, dilate, length):
    return [padded[:, tap * dilate : tap * dilate + length] for tap in range(3)]


def forward(inputs, full_conv, full_mix, dilate):
    width = inputs.shape[-1]
    length = inputs.shape[1]
    normed = prenorm(inputs.astype(jnp.float32)).astype(jnp.bfloat16)
    views = views_of(extended(normed, dilate), dilate, length)
    flat_views = [view.reshape(-1, width) for view in views]
    preact = jnp.dot(flat_views[0], full_conv[:, 0, :], preferred_element_type=jnp.float32)
    for tap in range(1, 3):
        preact = preact + jnp.dot(
            flat_views[tap], full_conv[:, tap, :], preferred_element_type=jnp.float32
        )
    hidden = jax.nn.gelu(preact).astype(jnp.bfloat16)
    mixed = inputs.reshape(-1, width).astype(jnp.float32) + jnp.dot(
        hidden, full_mix, preferred_element_type=jnp.float32
    )
    return (mixed.astype(jnp.bfloat16).reshape(inputs.shape), flat_views, preact, hidden)


def backward(
    inputs, flat_views, preact, hidden, upstream, full_conv, full_mix, conv_rows, mix_rows, dilate
):
    width = inputs.shape[-1]
    length = inputs.shape[1]
    middle = full_mix.shape[0]
    flat_up = upstream.reshape(-1, width)
    contract = (((0,), (0,)), ((), ()))
    dhidden = jnp.dot(flat_up, full_mix.T, preferred_element_type=jnp.float32)
    unused, pull = jax.vjp(jax.nn.gelu, preact)
    dpre = pull(dhidden)[0].astype(jnp.bfloat16)
    piece = hidden
    grad_mix = lax.psum_scatter(
        lax.dot_general(piece, flat_up, contract, preferred_element_type=jnp.float32),
        ("seq", "dp"),
        scatter_dimension=0,
        tiled=True,
    )
    terms = []
    for conv_tap in range(3):
        piece = flat_views[conv_tap]
        terms.append(lax.dot_general(piece, dpre, contract, preferred_element_type=jnp.float32))
    grad_conv = lax.psum_scatter(
        jnp.stack(terms, axis=1), ("seq", "dp"), scatter_dimension=0, tiled=True
    )
    dpre_field = dpre.reshape(inputs.shape[0], length, middle)
    back_views = views_of(extended(dpre_field, dilate), dilate, length)
    dnormed = jnp.dot(
        back_views[2].reshape(-1, middle), full_conv[:, 0, :].T, preferred_element_type=jnp.float32
    )
    for tap in range(1, 3):
        dnormed = dnormed + jnp.dot(
            back_views[2 - tap].reshape(-1, middle),
            full_conv[:, tap, :].T,
            preferred_element_type=jnp.float32,
        )
    unused_two, pull_norm = jax.vjp(prenorm, inputs.astype(jnp.float32))
    dinput = pull_norm(dnormed.reshape(inputs.shape))[0]
    result = (upstream.astype(jnp.float32) + dinput).astype(jnp.bfloat16)
    return (result, grad_conv, grad_mix)


def body(activations, cotangent, conv_one, mix_one, conv_two, mix_two):
    conv_full_one, mix_full_one = fetch(conv_one, mix_one)
    second_in, views_one, preact_one, hidden_one = forward(
        activations, conv_full_one, mix_full_one, DILATE_ONE
    )
    conv_full_two, mix_full_two = fetch(conv_two, mix_two)
    unused, views_two, preact_two, hidden_two = forward(
        second_in, conv_full_two, mix_full_two, DILATE_TWO
    )
    conv_back_two, mix_back_two = (conv_full_two, mix_full_two)
    upstream, grad_conv_two, grad_mix_two = backward(
        second_in,
        views_two,
        preact_two,
        hidden_two,
        cotangent,
        conv_back_two,
        mix_back_two,
        conv_two.shape[0],
        mix_two.shape[0],
        DILATE_TWO,
    )
    conv_back_one, mix_back_one = (conv_full_one, mix_full_one)
    input_grad, grad_conv_one, grad_mix_one = backward(
        activations,
        views_one,
        preact_one,
        hidden_one,
        upstream,
        conv_back_one,
        mix_back_one,
        conv_one.shape[0],
        mix_one.shape[0],
        DILATE_ONE,
    )
    return (input_grad, grad_conv_one, grad_mix_one, grad_conv_two, grad_mix_two)


def solution(mesh):
    in_specs = (
        P(("parts", "dp"), "seq", None),
        P(("parts", "dp"), "seq", None),
        P(("seq", "dp"), None, None),
        P(("seq", "dp"), None),
        P(("seq", "dp"), None, None),
        P(("seq", "dp"), None),
    )
    out_specs = (
        P(("parts", "dp"), "seq", None),
        P(("parts", "seq", "dp"), None, None),
        P(("parts", "seq", "dp"), None),
        P(("parts", "seq", "dp"), None, None),
        P(("parts", "seq", "dp"), None),
    )
    return jax.shard_map(body, mesh=mesh, in_specs=in_specs, out_specs=out_specs, check_vma=False)
```

profile of v0, /device:TPU:0, one launch (start us, length us, event | category | flops | bytes accessed | tf_op | source)
XLA Modules:
  0.0 512.4 jit_solution(3078574404284320583)
XLA Ops:
  12.4 4.9 collective-permute-start
  18.6 12.0 %collective-permute-done = bf16[2,64,1024]{2,1,0:T(8,128)(2,1)S(1)} collective-permute-done((bf16[2,64,1024]{2,1,0:T(8,128)(2,1)S(1)}, bf16[2,64,1024]{2,1,0:T(8,128)(2,1)S(1)}, u32[]{:S(2)}, u32[]{:S(2)}) %collective-permute-start) | collective-permute-done | bytes 262176 | tf_op jit(solution)/shard_map/ppermute | solution.py:15
  31.9 31.0 %all-gather.7.cloned.1.call-done = bf16[1024,3,512]{2,0,1:T(8,128)(2,1)} async-done(((bf16[64,3,512]{2,0,1:T(8,128)(2,1)}), bf16[1024,3,512]{2,0,1:T(8,128)(2,1)}) %all-gather.7.cloned.1.call-update) | async-done | bytes 3145744 | tf_op jit(solution)/shard_map/all_gather | solution.py:30
  62.9 2.1 fusion.60
  67.0 34.9 %all-gather.9.cloned.1.call-done = bf16[512,1024]{1,0:T(8,128)(2,1)} async-done(((bf16[32,1024]{1,0:T(8,128)(2,1)}), bf16[512,1024]{1,0:T(8,128)(2,1)}) %all-gather.9.cloned.1.call-update) | async-done | bytes 1048592 | tf_op jit(solution)/shard_map/all_gather | solution.py:31
  101.8 3.1 fusion.36
  105.0 3.4 fusion.39
  110.4 3.2 collective-permute-start.2
  114.9 28.7 %all-gather.5.cloned.1.call-done = bf16[512,1024]{1,0:T(8,128)(2,1)} async-done(((bf16[32,1024]{1,0:T(8,128)(2,1)}), bf16[512,1024]{1,0:T(8,128)(2,1)}) %all-gather.5.cloned.1.call-update) | async-done | bytes 1048592 | tf_op jit(solution)/shard_map/all_gather | solution.py:31
  143.6 2.9 fusion.84
  146.5 43.3 %all-gather.11.cloned.1.call-done = bf16[1024,3,512]{2,0,1:T(8,128)(2,1)} async-done(((bf16[64,3,512]{2,0,1:T(8,128)(2,1)}), bf16[1024,3,512]{2,0,1:T(8,128)(2,1)}) %all-gather.11.cloned.1.call-update) | async-done | bytes 3145744 | tf_op jit(solution)/shard_map/all_gather | solution.py:30
  189.9 2.6 fusion.63
  197.6 2.2 fusion.66
  199.9 2.5 collective-permute-start.5
  204.2 2.0 fusion.62
  206.1 2.2 collective-permute-done.5
  208.4 5.5 %collective-permute-done.4 = bf16[2,128,512]{2,1,0:T(8,128)(2,1)S(1)} collective-permute-done((bf16[2,128,512]{2,1,0:T(8,128)(2,1)S(1)}, bf16[2,128,512]{2,1,0:T(8,128)(2,1)S(1)}, u32[]{:S(2)}, u32[]{:S(2)}) %collective-permute-start.4) | collective-permute-done | bytes 262176 | tf_op jit(solution)/shard_map/ppermute | solution.py:18
  215.1 3.3 fusion.20
  218.5 3.8 fusion.22
  223.3 2.2 fusion.77
  225.6 2.2 convolution_bitcast_fusion
  230.3 3.4 pad_maximum_fusion.1
  233.8 3.2 fusion.48
  239.7 3.4 pad_maximum_fusion
  243.1 4.4 collective-permute-start.7
  249.3 2.0 fusion.57
  251.3 5.5 %collective-permute-done.6 = bf16[2,64,512]{2,1,0:T(8,128)(2,1)S(1)} collective-permute-done((bf16[2,64,512]{2,1,0:T(8,128)(2,1)S(1)}, bf16[2,64,512]{2,1,0:T(8,128)(2,1)S(1)}, u32[]{:S(2)}, u32[]{:S(2)}) %collective-permute-start.6) | collective-permute-done | bytes 131104 | tf_op jit(solution)/shard_map/ppermute | solution.py:18
  258.3 1.9 fusion.32
  260.3 3.0 fusion.24
  263.3 63.9 %reduce-scatter.7.cloned.1.call-done = f32[32,1024]{1,0:T(8,128)} async-done(((f32[512,1024]{1,0:T(8,128)}), f32[32,1024]{1,0:T(8,128)}) %reduce-scatter.7.cloned.1.call-update) | async-done | bytes 131088 | tf_op jit(solution)/shard_map/reduce_scatter | solution.py:73
  327.2 88.8 %reduce-scatter.9.cloned.1.call-done = f32[64,3,512]{2,0,1:T(8,128)} async-done(((f32[1024,3,512]{2,0,1:T(8,128)}), f32[64,3,512]{2,0,1:T(8,128)}) %reduce-scatter.9.cloned.1.call-update) | async-done | bytes 393232 | tf_op jit(solution)/shard_map/reduce_scatter | solution.py:83
  416.0 89.6 %reduce-scatter.5.cloned.1.call-done = f32[64,3,512]{2,0,1:T(8,128)} async-done(((f32[1024,3,512]{2,0,1:T(8,128)}), f32[64,3,512]{2,0,1:T(8,128)}) %reduce-scatter.5.cloned.1.call-update) | async-done | bytes 393232 | tf_op jit(solution)/shard_map/reduce_scatter | solution.py:83
  (100 shorter events, 30.9 us)
Async XLA Ops:
  7.2 4.4 copy-start
  7.2 55.7 %all-gather.7.cloned.1.call-start = ((), (), s32[]{:S(2)}) async-start(), calls=%async_computation.5 | async-start | bytes 3342336 | tf_op jit(solution)/shard_map/all_gather | solution.py:30
  7.9 93.9 %all-gather.9.cloned.1.call-start = ((), (), s32[]{:S(2)}) async-start(), calls=%async_computation.6 | async-start | bytes 1114112 | tf_op jit(solution)/shard_map/all_gather | solution.py:31
  8.7 134.9 %all-gather.5.cloned.1.call-start = ((), (), s32[]{:S(2)}) async-start(), calls=%async_computation.4 | async-start | bytes 1114112 | tf_op jit(solution)/shard_map/all_gather | solution.py:31
  9.4 180.5 %all-gather.11.cloned.1.call-start = ((), (), s32[]{:S(2)}) async-start(), calls=%async_computation.7 | async-start | bytes 3342336 | tf_op jit(solution)/shard_map/all_gather | solution.py:30
  10.0 253.3 %reduce-scatter.11.cloned.1.call-start = ((), (), s32[]{:S(2)}) async-start(), calls=%async_computation.11 | async-start | bytes 2228224 | tf_op jit(solution)/shard_map/reduce_scatter | solution.py:73
  12.4 18.2 %collective-permute-start = (bf16[2,64,1024]{2,1,0:T(8,128)(2,1)S(1)}, bf16[2,64,1024]{2,1,0:T(8,128)(2,1)S(1)}, u32[]{:S(2)}, u32[]{:S(2)}) collective-permute-start(bf16[2,64,1024]{2,1,0:T(8,128)(2,1)S(1)} %get-tuple-element.13), channel_id=1, source_target_pairs={{0,2},{2,4},{4,6},{6,8},{8,10},{10,12},{12,14},{1,3},{3,5},{5,7},{... | collective-permute-start | bytes 786440 | tf_op jit(solution)/shard_map/ppermute | solution.py:15
  17.3 13.3 %collective-permute-start.1 = (bf16[2,64,1024]{2,1,0:T(8,128)(2,1)S(1)}, bf16[2,64,1024]{2,1,0:T(8,128)(2,1)S(1)}, u32[]{:S(2)}, u32[]{:S(2)}) collective-permute-start(bf16[2,64,1024]{2,1,0:T(8,128)(2,1)S(1)} %get-tuple-element.14), channel_id=1, source_target_pairs={{2,0},{4,2},{6,4},{8,6},{10,8},{12,10},{14,12},{3,1},{5,3},{7,5},{... | collective-permute-start | bytes 786440 | tf_op jit(solution)/shard_map/ppermute | solution.py:18
  31.9 34.0 %copy-start.7 = (bf16[2,256,1024]{2,1,0:T(8,128)(2,1)}, bf16[2,256,1024]{2,1,0:T(8,128)(2,1)S(1)}, u32[]{:S(2)}) copy-start(bf16[2,256,1024]{2,1,0:T(8,128)(2,1)S(1)} %get-tuple-element.12) | copy-start | bytes 3145732
  62.9 2.2 copy-start.5
  66.9 38.0 %copy-start.16 = (f32[512,512]{1,0:T(8,128)}, f32[512,512]{1,0:T(8,128)S(1)}, u32[]{:S(2)}) copy-start(f32[512,512]{1,0:T(8,128)S(1)} %fusion.41) | copy-start | bytes 3145732
  108.3 35.3 %copy-start.18 = (bf16[2,256,1024]{2,1,0:T(8,128)(2,1)S(1)}, bf16[2,256,1024]{2,1,0:T(8,128)(2,1)}, u32[]{:S(2)}) copy-start(bf16[2,256,1024]{2,1,0:T(8,128)(2,1)} %param.7) | copy-start | bytes 3145732
  110.4 82.1 %collective-permute-start.2 = (bf16[2,128,1024]{2,1,0:T(8,128)(2,1)}, bf16[2,128,1024]{2,1,0:T(8,128)(2,1)}, u32[]{:S(2)}, u32[]{:S(2)}) collective-permute-start(bf16[2,128,1024]{2,1,0:T(8,128)(2,1)} %get-tuple-element.9), channel_id=1, source_target_pairs={{0,2},{2,4},{4,6},{6,8},{8,10},{10,12},{12,14},{1,3},{3,5},{5,7},{... | collective-permute-start | bytes 1572872 | tf_op jit(solution)/shard_map/ppermute | solution.py:15
  113.6 78.9 %collective-permute-start.3 = (bf16[2,128,1024]{2,1,0:T(8,128)(2,1)}, bf16[2,128,1024]{2,1,0:T(8,128)(2,1)}, u32[]{:S(2)}, u32[]{:S(2)}) collective-permute-start(bf16[2,128,1024]{2,1,0:T(8,128)(2,1)} %get-tuple-element.10), channel_id=1, source_target_pairs={{2,0},{4,2},{6,4},{8,6},{10,8},{12,10},{14,12},{3,1},{5,3},{7,5},{... | collective-permute-start | bytes 1572872 | tf_op jit(solution)/shard_map/ppermute | solution.py:18
  189.9 2.7 copy-start.4
  192.5 2.2 copy-start.14
  194.1 3.5 copy-start.9
  194.1 3.5 copy-start.11
  194.1 2.1 copy-start.22
  199.8 127.3 %reduce-scatter.7.cloned.1.call-start = ((), (), s32[]{:S(2)}) async-start(), calls=%async_computation.9 | async-start | bytes 2228224 | tf_op jit(solution)/shard_map/reduce_scatter | solution.py:73
  199.9 8.4 %collective-permute-start.5 = (bf16[2,128,512]{2,1,0:T(8,128)(2,1)S(1)}, bf16[2,128,512]{2,1,0:T(8,128)(2,1)S(1)}, u32[]{:S(2)}, u32[]{:S(2)}) collective-permute-start(bf16[2,128,512]{2,1,0:T(8,128)(2,1)S(1)} %get-tuple-element.21), channel_id=1, source_target_pairs={{0,2},{2,4},{4,6},{6,8},{8,10},{10,12},{12,14},{1,3},{3,5},{5,7},{... | collective-permute-start | bytes 786440 | tf_op jit(solution)/shard_map/ppermute | solution.py:15
  202.4 11.5 %copy-start.15 = (bf16[1024,3,512]{2,0,1:T(8,128)(2,1)S(1)}, bf16[1024,3,512]{2,0,1:T(8,128)(2,1)}, u32[]{:S(2)}) copy-start(bf16[1024,3,512]{2,0,1:T(8,128)(2,1)} %all-gather.11.cloned.1.call-done) | copy-start | bytes 9437188
  202.4 11.4 %collective-permute-start.4 = (bf16[2,128,512]{2,1,0:T(8,128)(2,1)S(1)}, bf16[2,128,512]{2,1,0:T(8,128)(2,1)S(1)}, u32[]{:S(2)}, u32[]{:S(2)}) collective-permute-start(bf16[2,128,512]{2,1,0:T(8,128)(2,1)S(1)} %get-tuple-element.22), channel_id=1, source_target_pairs={{2,0},{4,2},{6,4},{8,6},{10,8},{12,10},{14,12},{3,1},{5,3},{7,5},{... | collective-permute-start | bytes 786440 | tf_op jit(solution)/shard_map/ppermute | solution.py:18
  218.5 4.8 copy-start.17
  225.5 190.5 %reduce-scatter.9.cloned.1.call-start = ((), (), s32[]{:S(2)}) async-start(), calls=%async_computation.10 | async-start | bytes 6684672 | tf_op jit(solution)/shard_map/reduce_scatter | solution.py:83
  225.6 2.3 copy-start.10
  233.7 271.9 %reduce-scatter.5.cloned.1.call-start = ((), (), s32[]{:S(2)}) async-start(), calls=%async_computation.8 | async-start | bytes 6684672 | tf_op jit(solution)/shard_map/reduce_scatter | solution.py:83
  233.8 3.2 copy-start.8
  243.1 8.1 %collective-permute-start.7 = (bf16[2,64,512]{2,1,0:T(8,128)(2,1)S(1)}, bf16[2,64,512]{2,1,0:T(8,128)(2,1)S(1)}, u32[]{:S(2)}, u32[]{:S(2)}) collective-permute-start(bf16[2,64,512]{2,1,0:T(8,128)(2,1)S(1)} %get-tuple-element.17), channel_id=1, source_target_pairs={{0,2},{2,4},{4,6},{6,8},{8,10},{10,12},{12,14},{1,3},{3,5},{5,7},{... | collective-permute-start | bytes 393224 | tf_op jit(solution)/shard_map/ppermute | solution.py:15
  247.5 9.3 %copy-start.6 = (bf16[1024,3,512]{2,0,1:T(8,128)(2,1)S(1)}, bf16[1024,3,512]{2,0,1:T(8,128)(2,1)}, u32[]{:S(2)}) copy-start(bf16[1024,3,512]{2,0,1:T(8,128)(2,1)} %all-gather.7.cloned.1.call-done) | copy-start | bytes 9437188
  247.5 9.2 %collective-permute-start.6 = (bf16[2,64,512]{2,1,0:T(8,128)(2,1)S(1)}, bf16[2,64,512]{2,1,0:T(8,128)(2,1)S(1)}, u32[]{:S(2)}, u32[]{:S(2)}) collective-permute-start(bf16[2,64,512]{2,1,0:T(8,128)(2,1)S(1)} %get-tuple-element.18), channel_id=1, source_target_pairs={{2,0},{4,2},{6,4},{8,6},{10,8},{12,10},{14,12},{3,1},{5,3},{7,5},{... | collective-permute-start | bytes 393224 | tf_op jit(solution)/shard_map/ppermute | solution.py:18
  258.3 1.9 copy-start.13
  (7 other events, 8.4 us)
Sparse Core Ops, SparseCore 0:
  10.2 52.6 all-gather.6
  65.0 36.7 all-gather.8
  104.0 39.5 all-gather.4
  145.6 44.1 all-gather.10
  199.9 62.3 reduce-scatter.10
  266.9 60.1 reduce-scatter.6
  331.7 84.2 reduce-scatter.8
  421.0 84.4 reduce-scatter.4
where the time goes:
time: 513 us; the launch traced here: 512 us
  waiting for transfers between devices  408 us (80%)
  matrix products  37.7 us (7%)
  other arithmetic  24.2 us (5%)
  starting transfers between devices  21.4 us (4%)
  between operations  14.6 us (3%)
  local copies, waits for them, and re-layouts  6.65 us (1%)
    reduce_scatter x2, waiting for transfers between devices, backward(): lax.psum_scatter(jnp.stack(terms, axis=1), ('seq', 'dp'), scatter_dimensi...  178 us
    all_gather x2, waiting for transfers between devices, fetch(): lax.all_gather(conv_w, ('seq', 'dp'), axis=0, tiled=True)  74.3 us
    reduce_scatter x2, waiting for transfers between devices, backward(): lax.psum_scatter(lax.dot_general(piece, flat_up, contract, preferred_elem...  63.9 us
    all_gather x2, waiting for transfers between devices, fetch(): lax.all_gather(mix_w, ('seq', 'dp'), axis=0, tiled=True)  63.6 us
    ppermute x4, starting transfers between devices, with_halo(): lax.ppermute(lax.slice_in_dim(block, block.shape[dim] - width, None, axis...  15 us
    ppermute x4, waiting for transfers between devices, with_halo(): lax.ppermute(lax.slice_in_dim(block, block.shape[dim] - width, None, axis...  14.2 us
    ppermute x4, waiting for transfers between devices, with_halo(): lax.ppermute(lax.slice_in_dim(block, 0, width, axis=dim), axis, backward)  10.9 us
  transfers between devices with their start and end apart: 16, of which 11 were waited for; matrix products, arithmetic and copies ran while one was open for 11% of the time, Pallas kernels for 0%

commit v1 on v0

v1 whole, which is shorter than its diff:
```python
import functools
import math

import jax
import jax.numpy as jnp
from jax import lax
from jax.experimental import pallas as pl
from jax.experimental.pallas import tpu as pltpu
from jax.sharding import PartitionSpec as P

DILATE_ONE = 64
DILATE_TWO = 128
BF = jnp.bfloat16
F32 = jnp.float32
ROOT = math.sqrt(2.0 / math.pi)
CUBE = 0.044715
VMEM = pl.BlockSpec(memory_space=pltpu.VMEM)
ANY = pl.BlockSpec(memory_space=pl.ANY)
NT = (((1,), (1,)), ((), ()))
TN = (((0,), (0,)), ((), ()))


def gelu(v):
    return v * (0.5 * (1.0 + jnp.tanh(ROOT * (v + CUBE * (v * v * v)))))


def gelu_slope(v):
    t = jnp.tanh(ROOT * (v + CUBE * (v * v * v)))
    return 0.5 * (1.0 + t) + (0.5 * v) * (1.0 - t * t) * (ROOT * (1.0 + 3.0 * CUBE * (v * v)))


def norm_scale(v):
    return lax.rsqrt(jnp.mean(v * v, axis=-1, keepdims=True) + 1e-06)


def dot(a, b, dims=(((1,), (0,)), ((), ()))):
    return lax.dot_general(a, b, dims, preferred_element_type=F32)


def params():
    return pltpu.CompilerParams(vmem_limit_bytes=40 << 20)


def swap(value, axis, bit):
    count = lax.axis_size(axis)
    return lax.ppermute(value, axis, [(i, i ^ bit) for i in range(count)])


def step_orders(count):
    bits = [1 << i for i in reversed(range(count.bit_length() - 1))]
    assert math.prod([2] * len(bits)) == count
    return bits, bits[-1:] + bits[:-1]


def offset_of(index, steps):
    return sum(step for j, step in enumerate(steps) if (index >> j) & 1)


def place_of(offset, steps):
    place = 0
    for j, step in enumerate(steps):
        shift = step.bit_length() - 1
        place = place + (((offset >> shift) & 1) << j)
    return place


def gather_pair(first, second, orders):
    one, two = first[None], second[None]
    for left, right in zip(*orders):
        got_one = swap(one, "seq", left)
        got_two = swap(two, "seq", right)
        one = jnp.concatenate([one, got_one], axis=0)
        two = jnp.concatenate([two, got_two], axis=0)
    return one, swap(one, "dp", 1), two, swap(two, "dp", 1)


def scatter_sum(keep, send, steps):
    total = keep + swap(send, "dp", 1).astype(F32)
    for step in reversed(steps):
        half = total.shape[0] // 2
        got = swap(total[half:].astype(BF), "seq", step)
        total = total[:half] + got.astype(F32)
    return total[0]


def halo(first, last):
    count = lax.axis_size("seq")
    low = lax.ppermute(last, "seq", [(i, i + 1) for i in range(count - 1)])
    high = lax.ppermute(first, "seq", [(i + 1, i) for i in range(count - 1)])
    return low, high


def fetch_weights(orders, pieces, taps, rest, sem):
    here, core = lax.axis_index("seq"), lax.axis_index("dp")
    copies = []
    for which, (target, steps) in enumerate(((taps, orders[0]), (rest, orders[1]))):
        own, other = pieces[2 * which], pieces[2 * which + 1]
        for index in range(own.shape[0]):
            where = here ^ offset_of(index, steps)
            for piece, lane in ((own, core), (other, 1 - core)):
                copy = pltpu.make_async_copy(
                    piece.at[index], target.at[where, lane], sem.at[len(copies)]
                )
                copy.start()
                copies.append(copy)
    return copies


def weight_scratch(count, rows, width):
    return [
        pltpu.VMEM((count, 2, rows, width), BF),
        pltpu.VMEM((count, 2, rows, width), BF),
        pltpu.SemaphoreType.DMA((4 * count,)),
    ]


def conv_weights(taps, rest, middle):
    rows = taps.shape[0] * taps.shape[1] * taps.shape[2]
    return [
        taps[:, :, :, :middle].reshape(rows, middle),
        taps[:, :, :, middle:].reshape(rows, middle),
        rest[:, :, :, :middle].reshape(rows, middle),
    ]


def mix_halves(rest, middle):
    half = rest.shape[2] // 2
    return [
        rest[:, :, :half, middle:].reshape(middle, middle),
        rest[:, :, half:, middle:].reshape(middle, middle),
    ]


def norm_kernel(x_ref, low_ref, high_ref, ext_ref):
    dilate = low_ref.shape[1]
    length = x_ref.shape[1]
    for w in range(x_ref.shape[0]):
        for source, start, size in (
            (low_ref, 0, dilate),
            (x_ref, dilate, length),
            (high_ref, dilate + length, dilate),
        ):

            @pl.loop(0, size // 32)
            def _(i):
                rows = pl.multiple_of(i * 32, 32)
                v = source[w, pl.ds(rows, 32), :].astype(F32)
                ext_ref[w, pl.ds(start + rows, 32), :] = gelu(v * norm_scale(v)).astype(BF)


def norm_ext(x, low, high):
    windows, length, width = x.shape
    return pl.pallas_call(
        norm_kernel,
        out_shape=jax.ShapeDtypeStruct((windows, length + 2 * low.shape[1], width), BF),
        in_specs=[VMEM] * 3,
        out_specs=VMEM,
        compiler_params=params(),
        name="norm_ext",
    )(x, low, high)


def forward_kernel(
    orders, dilate, edge, ext, x_ref, a0, a1, b0, b1,
    pre_ref, hid_ref, x2_ref, first_ref, last_ref, taps, rest, sem,
):
    copies = fetch_weights(orders, (a0, a1, b0, b1), taps, rest, sem)
    for copy in copies:
        copy.wait()
    windows, length, width = x_ref.shape
    middle = hid_ref.shape[1]
    conv = conv_weights(taps, rest, middle)
    mix = mix_halves(rest, middle)
    for w in range(windows):
        pre = sum(dot(ext[w, k * dilate : k * dilate + length, :], conv[k]) for k in range(3))
        pre_ref[w * length : (w + 1) * length, :] = pre
        hid_ref[w * length : (w + 1) * length, :] = gelu(pre).astype(BF)
        hid = hid_ref[w * length : (w + 1) * length, :]
        for h in range(2):
            cols = slice(h * middle, (h + 1) * middle)
            x2_ref[w, :, cols] = (x_ref[w, :, cols].astype(F32) + dot(hid, mix[h])).astype(BF)
        for target, start in ((first_ref, 0), (last_ref, length - edge)):

            @pl.loop(0, edge // 32)
            def _(i):
                rows = pl.multiple_of(i * 32, 32)
                v = x2_ref[w, pl.ds(start + rows, 32), :].astype(F32)
                target[w, pl.ds(rows, 32), :] = gelu(v * norm_scale(v)).astype(BF)


def forward_block(ext, x, pieces, orders, dilate, edge):
    windows, length, width = x.shape
    count, rows, packed = pieces[0].shape
    middle = packed // 2
    flat = windows * length
    return pl.pallas_call(
        functools.partial(forward_kernel, orders, dilate, edge),
        out_shape=(
            jax.ShapeDtypeStruct((flat, middle), F32),
            jax.ShapeDtypeStruct((flat, middle), BF),
            jax.ShapeDtypeStruct(x.shape, BF),
            jax.ShapeDtypeStruct((windows, edge, width), BF),
            jax.ShapeDtypeStruct((windows, edge, width), BF),
        ),
        in_specs=[VMEM, VMEM] + [ANY] * 4,
        out_specs=(VMEM,) * 5,
        scratch_shapes=weight_scratch(count, rows, packed),
        compiler_params=params(),
        cost_estimate=pl.CostEstimate(
            flops=8 * flat * width * middle, bytes_accessed=16 << 20, transcendentals=0
        ),
        name="forward_block",
    )(ext, x, *pieces)


def turn_kernel(
    orders, dilate, first, last, low, high, e_ref, a0, a1, b0, b1,
    ext, hid_ref, dpre_ref, dfirst, dlast, taps, rest, sem,
):
    copies = fetch_weights(orders, (a0, a1, b0, b1), taps, rest, sem)
    windows, length, width = e_ref.shape
    edge = first.shape[1]
    middle = hid_ref.shape[1]
    for w in range(windows):
        for source, start in (
            (low, 0), (first, dilate), (last, dilate + length - edge), (high, dilate + length),
        ):
            ext[w, start : start + edge, :] = source[w]
    for copy in copies:
        copy.wait()
    conv = conv_weights(taps, rest, middle)
    mix = mix_halves(rest, middle)
    for w in range(windows):
        pre = sum(dot(ext[w, k * dilate : k * dilate + length, :], conv[k]) for k in range(3))
        dhid = dot(e_ref[w, :, :middle], mix[0], NT) + dot(e_ref[w, :, middle:], mix[1], NT)
        rows = slice(w * length, (w + 1) * length)
        hid_ref[rows, :] = gelu(pre).astype(BF)
        dpre_ref[rows, :] = (gelu_slope(pre) * dhid).astype(BF)
        dfirst[w] = dpre_ref[w * length : w * length + dilate, :]
        dlast[w] = dpre_ref[(w + 1) * length - dilate : (w + 1) * length, :]


def turn_block(first, last, low, high, e, pieces, orders, dilate):
    windows, length, width = e.shape
    count, rows, packed = pieces[0].shape
    middle = packed // 2
    flat = windows * length
    return pl.pallas_call(
        functools.partial(turn_kernel, orders, dilate),
        out_shape=(
            jax.ShapeDtypeStruct((windows, length + 2 * dilate, width), BF),
            jax.ShapeDtypeStruct((flat, middle), BF),
            jax.ShapeDtypeStruct((flat, middle), BF),
            jax.ShapeDtypeStruct((windows, dilate, middle), BF),
            jax.ShapeDtypeStruct((windows, dilate, middle), BF),
        ),
        in_specs=[VMEM] * 5 + [ANY] * 4,
        out_specs=(VMEM,) * 5,
        scratch_shapes=weight_scratch(count, rows, packed),
        compiler_params=params(),
        cost_estimate=pl.CostEstimate(
            flops=8 * flat * width * middle, bytes_accessed=16 << 20, transcendentals=0
        ),
        name="turn_block",
    )(first, last, low, high, e, *pieces)


def grads_kernel(orders, dilate, ext, hid, e_ref, dpre, keep_a, send_a, keep_b, send_b, full):
    here, core = lax.axis_index("seq"), lax.axis_index("dp")
    windows, length, width = e_ref.shape
    middle = hid.shape[1]
    count, rows, packed = keep_a.shape
    half = rows // 2
    for k in (2, 0, 1, 3):
        if k == 3:
            for h in range(2):
                e = jnp.concatenate(
                    [e_ref[w, :, h * middle : (h + 1) * middle] for w in range(windows)], axis=0
                )
                full[h * middle : (h + 1) * middle, :] = dot(hid[...], e, TN)
        else:
            view = jnp.concatenate(
                [ext[w, k * dilate : k * dilate + length, :] for w in range(windows)], axis=0
            )
            full[...] = dot(view, dpre[...], TN)
        keep, send, steps = (
            (keep_a, send_a, orders[0]) if k < 2 else (keep_b, send_b, orders[1])
        )
        cols = slice((k % 2) * middle, (k % 2 + 1) * middle)
        for chip in range(count):
            place = place_of(here ^ chip, steps)
            if k == 3:
                for h in range(2):
                    base = h * middle + chip * rows
                    out = slice(h * half, (h + 1) * half)
                    mine = full[pl.ds(pl.multiple_of(base + core * half, half), half), :]
                    theirs = full[pl.ds(pl.multiple_of(base + (1 - core) * half, half), half), :]
                    keep[place, out, cols] = mine
                    send[place, out, cols] = theirs.astype(BF)
            else:
                base = 2 * chip * rows
                mine = full[pl.ds(pl.multiple_of(base + core * rows, rows), rows), :]
                theirs = full[pl.ds(pl.multiple_of(base + (1 - core) * rows, rows), rows), :]
                keep[place, :, cols] = mine
                send[place, :, cols] = theirs.astype(BF)


def grads_block(ext, hid, e, dpre, orders, dilate, count):
    windows, length, width = e.shape
    flat, middle = hid.shape
    rows = width // (2 * count)
    shape = (count, rows, 2 * middle)
    return pl.pallas_call(
        functools.partial(grads_kernel, orders, dilate),
        out_shape=(
            jax.ShapeDtypeStruct(shape, F32),
            jax.ShapeDtypeStruct(shape, BF),
            jax.ShapeDtypeStruct(shape, F32),
            jax.ShapeDtypeStruct(shape, BF),
        ),
        in_specs=[VMEM] * 4,
        out_specs=(VMEM,) * 4,
        scratch_shapes=[pltpu.VMEM((width, middle), F32)],
        compiler_params=params(),
        cost_estimate=pl.CostEstimate(
            flops=8 * flat * width * middle, bytes_accessed=16 << 20, transcendentals=0
        ),
        name="grads_block",
    )(ext, hid, e, dpre)


def back_kernel(orders, dilate, chained, *refs):
    dpre, low, high, x_ref, e_ref, a0, a1, b0, b1 = refs[:9]
    if chained:
        (m0, m1, pre_ref, out_ref, dprev, dfirst, dlast) = refs[9:16]
        ext, dn, taps, rest, sem, taps_m, rest_m, sem_m = refs[16:]
    else:
        out_ref = refs[9]
        ext, dn, taps, rest, sem = refs[10:]
    copies = fetch_weights(orders, (a0, a1, b0, b1), taps, rest, sem)
    windows, length, width = x_ref.shape
    middle = dpre.shape[1]
    if chained:
        here, core = lax.axis_index("seq"), lax.axis_index("dp")
        for index in range(m0.shape[0]):
            where = here ^ offset_of(index, orders[1])
            for j, (piece, lane) in enumerate(((m0, core), (m1, 1 - core))):
                copy = pltpu.make_async_copy(
                    piece.at[index], rest_m.at[where, lane], sem_m.at[2 * index + j]
                )
                copy.start()
                copies.append(copy)
    for w in range(windows):
        ext[w, :dilate, :] = low[w]
        ext[w, dilate : dilate + length, :] = dpre[w * length : (w + 1) * length, :]
        ext[w, dilate + length :, :] = high[w]
    for copy in copies:
        copy.wait()
    conv = conv_weights(taps, rest, middle)
    for w in range(windows):
        dn[...] = sum(
            dot(ext[w, (2 - k) * dilate : (2 - k) * dilate + length, :], conv[k], NT)
            for k in range(3)
        )

        @pl.loop(0, length // 32)
        def _(i):
            rows = pl.ds(pl.multiple_of(i * 32, 32), 32)
            v = x_ref[w, rows, :].astype(F32)
            scale = norm_scale(v)
            u = v * scale
            g = dn[rows, :] * gelu_slope(u)
            dv = scale * (g - u * jnp.mean(g * u, axis=-1, keepdims=True))
            out_ref[w, rows, :] = (e_ref[w, rows, :].astype(F32) + dv).astype(BF)

        if chained:
            mix = mix_halves(rest_m, middle)
            edge = dfirst.shape[1]
            dhid = dot(out_ref[w, :, :middle], mix[0], NT) + dot(out_ref[w, :, middle:], mix[1], NT)
            rows = slice(w * length, (w + 1) * length)
            dprev[rows, :] = (gelu_slope(pre_ref[rows, :]) * dhid).astype(BF)
            dfirst[w] = dprev[w * length : w * length + edge, :]
            dlast[w] = dprev[(w + 1) * length - edge : (w + 1) * length, :]


def back_block(dpre, low, high, x, e, pieces, orders, dilate, previous=None):
    windows, length, width = x.shape
    count, rows, packed = pieces[0].shape
    flat, middle = dpre.shape
    chained = previous is not None
    operands = [dpre, low, high, x, e, *pieces]
    in_specs = [VMEM] * 5 + [ANY] * 4
    shapes = [jax.ShapeDtypeStruct(x.shape, BF)]
    scratch = [
        pltpu.VMEM((windows, length + 2 * dilate, middle), BF),
        pltpu.VMEM((length, width), F32),
    ] + weight_scratch(count, rows, packed)
    if chained:
        others, pre, edge = previous
        operands += [others[2], others[3], pre]
        in_specs += [ANY, ANY, VMEM]
        shapes += [
            jax.ShapeDtypeStruct((flat, middle), BF),
            jax.ShapeDtypeStruct((windows, edge, middle), BF),
            jax.ShapeDtypeStruct((windows, edge, middle), BF),
        ]
        scratch += [pltpu.VMEM((8, 128), BF)] + weight_scratch(count, rows, packed)[1:]
    return pl.pallas_call(
        functools.partial(back_kernel, orders, dilate, chained),
        out_shape=tuple(shapes),
        in_specs=in_specs,
        out_specs=(VMEM,) * len(shapes),
        scratch_shapes=scratch,
        compiler_params=params(),
        cost_estimate=pl.CostEstimate(
            flops=8 * flat * width * middle, bytes_accessed=16 << 20, transcendentals=0
        ),
        name="back_block",
    )(*operands)


def pack(conv, mix):
    middle = conv.shape[2]
    first = conv[:, :2].reshape(conv.shape[0], 2 * middle)
    tall = jnp.concatenate([mix[:, :middle], mix[:, middle:]], axis=0)
    second = jnp.concatenate([conv[:, 2], tall], axis=1)
    return first, second


def unpack(first, second, middle):
    rows = first.shape[0]
    conv = jnp.concatenate(
        [first.reshape(rows, 2, middle), second[:, None, :middle]], axis=1
    )
    half = rows // 2
    mix = jnp.concatenate([second[:half, middle:], second[half:, middle:]], axis=1)
    return conv, mix


def body(activations, cotangent, conv_one, mix_one, conv_two, mix_two):
    count = lax.axis_size("seq")
    orders = step_orders(count)
    middle = conv_one.shape[2]
    length = activations.shape[1]
    low, high = halo(
        activations[:, :DILATE_ONE], activations[:, length - DILATE_ONE :]
    )
    pieces_one = gather_pair(*pack(conv_one, mix_one), orders)
    pieces_two = gather_pair(*pack(conv_two, mix_two), orders)
    ext_one = norm_ext(activations, low, high)
    pre_one, hid_one, second_in, first, last = forward_block(
        ext_one, activations, pieces_one, orders, DILATE_ONE, DILATE_TWO
    )
    low, high = halo(first, last)
    ext_two, hid_two, dpre_two, dfirst, dlast = turn_block(
        first, last, low, high, cotangent, pieces_two, orders, DILATE_TWO
    )
    dlow, dhigh = halo(dfirst, dlast)
    ka, sa, kb, sb = grads_block(ext_two, hid_two, cotangent, dpre_two, orders, DILATE_TWO, count)
    grads_two = unpack(scatter_sum(ka, sa, orders[0]), scatter_sum(kb, sb, orders[1]), middle)
    upstream, dpre_one, dfirst, dlast = back_block(
        dpre_two, dlow, dhigh, second_in, cotangent, pieces_two, orders, DILATE_TWO,
        (pieces_one, pre_one, DILATE_ONE),
    )
    dlow, dhigh = halo(dfirst, dlast)
    ka, sa, kb, sb = grads_block(ext_one, hid_one, upstream, dpre_one, orders, DILATE_ONE, count)
    grads_one = unpack(scatter_sum(ka, sa, orders[0]), scatter_sum(kb, sb, orders[1]), middle)
    (input_grad,) = back_block(
        dpre_one, dlow, dhigh, activations, upstream, pieces_one, orders, DILATE_ONE
    )
    return (input_grad, *grads_one, *grads_two)


def solution(mesh):
    in_specs = (
        P(("parts", "dp"), "seq", None),
        P(("parts", "dp"), "seq", None),
        P(("seq", "dp"), None, None),
        P(("seq", "dp"), None),
        P(("seq", "dp"), None, None),
        P(("seq", "dp"), None),
    )
    out_specs = (
        P(("parts", "dp"), "seq", None),
        P(("parts", "seq", "dp"), None, None),
        P(("parts", "seq", "dp"), None),
        P(("parts", "seq", "dp"), None, None),
        P(("parts", "seq", "dp"), None),
    )
    return jax.shard_map(body, mesh=mesh, in_specs=in_specs, out_specs=out_specs, check_vma=False)
```

time: 513 us -> 273 us (0.53)
  waiting for transfers between devices: 408 us -> 125 us
  Pallas kernels: 0 us -> 62 us
  starting transfers between devices: 21.4 us -> 64.3 us
  matrix products: 37.7 us -> 0 us
  other arithmetic: 24.2 us -> 8.08 us
  between operations: 14.6 us -> 1.42 us
    reduce_scatter x4 -> x0, waiting for transfers between devices: 242 us -> none  [the longest x2 178 us: backward(): lax.psum_scatter(jnp.stack(terms, axis=1), ('seq', 'dp'), scatter_dimensi...]
    all_gather x4 -> x0, waiting for transfers between devices: 138 us -> none  [the longest x2 74.3 us: fetch(): lax.all_gather(conv_w, ('seq', 'dp'), axis=0, tiled=True)]
    ppermute x8 -> x40, waiting for transfers between devices: 25.1 us -> 125 us  [the longest x32 85.8 us: swap(): return lax.ppermute(value, axis, [(i, i ^ bit) for i in range(count)])]
    pallas_call x0 -> x7, Pallas kernels: none -> 62 us  [the longest x2 30 us: back_block(): pl.pallas_call(functools.partial(back_kernel, orders, dilate, chained), o...]
    ppermute x8 -> x40, starting transfers between devices: 21 us -> 64.3 us  [the longest x32 37.6 us: swap(): return lax.ppermute(value, axis, [(i, i ^ bit) for i in range(count)])]
    dot_general x23 -> x0, matrix products: 37.7 us -> none  [the longest x4 8 us: backward(): jnp.dot(back_views[2 - tap].reshape(-1, middle), full_conv[:, tap, :].T,...]
    convert_element_type x4 -> x0, other arithmetic: 11.1 us -> none  [the longest x2 6.87 us: backward(): result = (upstream.astype(jnp.float32) + dinput).astype(jnp.bfloat16)]
    another operation x2 -> x0, other arithmetic: 6.74 us -> none  [backward(): jnp.stack(terms, axis=1)]
  transfers between devices with their start and end apart: 16 -> 40, of which waited for: 11 -> 22; matrix products, arithmetic and copies ran while one was open for 11% -> 5% of each run, Pallas kernels for 0% -> 18%
where the time goes in v1:
time: 273 us; the launch traced here: 272 us
  waiting for transfers between devices  125 us (46%)
  starting transfers between devices  64.3 us (24%)
  Pallas kernels  62 us (23%)
  local copies, waits for them, and re-layouts  11.3 us (4%)
  other arithmetic  8.08 us (3%)
    ppermute x32, waiting for transfers between devices, swap(): return lax.ppermute(value, axis, [(i, i ^ bit) for i in range(count)])  85.8 us
    ppermute x32, starting transfers between devices, swap(): return lax.ppermute(value, axis, [(i, i ^ bit) for i in range(count)])  37.6 us
    pallas_call x2, Pallas kernels, back_block(): pl.pallas_call(functools.partial(back_kernel, orders, dilate, chained), o...  30 us
    ppermute x4, waiting for transfers between devices, halo(): low = lax.ppermute(last, 'seq', [(i, i + 1) for i in range(count - 1)])  27.3 us
    ppermute x4, starting transfers between devices, halo(): low = lax.ppermute(last, 'seq', [(i, i + 1) for i in range(count - 1)])  21.1 us
    ppermute x4, waiting for transfers between devices, halo(): high = lax.ppermute(first, 'seq', [(i + 1, i) for i in range(count - 1)])  12 us
    pallas_call x1, Pallas kernels, forward_block(): pl.pallas_call(functools.partial(forward_kernel, orders, dilate, edge), o...  11.2 us
    pallas_call x2, Pallas kernels, grads_block(): pl.pallas_call(functools.partial(grads_kernel, orders, dilate), out_shape...  8.72 us
  transfers between devices with their start and end apart: 40, of which 22 were waited for; matrix products, arithmetic and copies ran while one was open for 5% of the time, Pallas kernels for 18%

profile of v1, /device:TPU:0, one launch (start us, length us, event | category | flops | bytes accessed | tf_op | source)
XLA Modules:
  0.0 272.1 jit_solution(7255638658530918660)
XLA Ops:
  1.8 4.1 %collective-permute-start.12 = (bf16[1,64,1024]{2,1,0:T(8,128)(2,1)S(1)}, bf16[1,64,1024]{2,1,0:T(8,128)(2,1)S(1)}, u32[]{:S(2)}, u32[]{:S(2)}) collective-permute-start(bf16[1,64,1024]{2,1,0:T(8,128)(2,1)S(1)} %broadcast_in_dim_reshape.7), channel_id=1, source_target_pairs={{0,8},{2,10},{4,12},{6,14},{8,0},{10,2},{12,4},{14,6},{1,9},{3,11}... | collective-permute-start | bytes 393224 | tf_op jit(solution)/shard_map/ppermute | solution.py:46
  11.8 6.0 %collective-permute-done.2 = bf16[1,64,1024]{2,1,0:T(8,128)(2,1)S(1)} collective-permute-done((bf16[1,64,1024]{2,1,0:T(8,128)(2,1)S(1)}, bf16[1,64,1024]{2,1,0:T(8,128)(2,1)S(1)}, u32[]{:S(2)}, u32[]{:S(2)}) %collective-permute-start.2) | collective-permute-done | bytes 131104 | tf_op jit(solution)/shard_map/ppermute | solution.py:46
  18.7 3.4 %collective-permute-start.7 = (bf16[2,64,1024]{2,1,0:T(8,128)(2,1)S(1)}, bf16[2,64,1024]{2,1,0:T(8,128)(2,1)S(1)}, u32[]{:S(2)}, u32[]{:S(2)}) collective-permute-start(bf16[2,64,1024]{2,1,0:T(8,128)(2,1)S(1)} %pad_maximum_fusion.9), channel_id=1, source_target_pairs={{0,8},{2,10},{4,12},{6,14},{8,0},{10,2},{12,4},{14,6},{1,9},{3,11}... | collective-permute-start | bytes 786440 | tf_op jit(solution)/shard_map/ppermute | solution.py:46
  23.2 9.3 %collective-permute-done.3 = bf16[2,64,1024]{2,1,0:T(8,128)(2,1)S(1)} collective-permute-done((bf16[2,64,1024]{2,1,0:T(8,128)(2,1)S(1)}, bf16[2,64,1024]{2,1,0:T(8,128)(2,1)S(1)}, u32[]{:S(2)}, u32[]{:S(2)}) %collective-permute-start.3) | collective-permute-done | bytes 262176 | tf_op jit(solution)/shard_map/ppermute | solution.py:46
  35.2 8.5 %collective-permute-done.13 = bf16[2,64,1024]{2,1,0:T(8,128)(2,1)S(1)} collective-permute-done((bf16[2,64,1024]{2,1,0:T(8,128)(2,1)S(1)}, bf16[2,64,1024]{2,1,0:T(8,128)(2,1)S(1)}, u32[]{:S(2)}, u32[]{:S(2)}) %collective-permute-start.13) | collective-permute-done | bytes 262176 | tf_op jit(solution)/shard_map/ppermute | solution.py:46
  46.4 8.9 %collective-permute-done.8 = bf16[4,64,1024]{2,1,0:T(8,128)(2,1)S(1)} collective-permute-done((bf16[4,64,1024]{2,1,0:T(8,128)(2,1)S(1)}, bf16[4,64,1024]{2,1,0:T(8,128)(2,1)S(1)}, u32[]{:S(2)}, u32[]{:S(2)}) %collective-permute-start.8) | collective-permute-done | bytes 524320 | tf_op jit(solution)/shard_map/ppermute | solution.py:46
  57.5 9.0 %collective-permute-done.18 = bf16[4,64,1024]{2,1,0:T(8,128)(2,1)S(1)} collective-permute-done((bf16[4,64,1024]{2,1,0:T(8,128)(2,1)S(1)}, bf16[4,64,1024]{2,1,0:T(8,128)(2,1)S(1)}, u32[]{:S(2)}, u32[]{:S(2)}) %collective-permute-start.18) | collective-permute-done | bytes 524320 | tf_op jit(solution)/shard_map/ppermute | solution.py:46
  66.7 7.0 %collective-permute-start = (bf16[2,64,1024]{2,1,0:T(8,128)(2,1)S(1)}, bf16[2,64,1024]{2,1,0:T(8,128)(2,1)S(1)}, u32[]{:S(2)}, u32[]{:S(2)}) collective-permute-start(bf16[2,64,1024]{2,1,0:T(8,128)(2,1)S(1)} %get-tuple-element.50), channel_id=1, source_target_pairs={{0,2},{2,4},{4,6},{6,8},{8,10},{10,12},{12,14},{1,3},{3,5},{5,7},{... | collective-permute-start | bytes 786440 | tf_op jit(solution)/shard_map/ppermute | solution.py:88
  73.7 4.1 %collective-permute-done.low_ref = bf16[2,64,1024]{2,1,0:T(8,128)(2,1)S(1)} collective-permute-done((bf16[2,64,1024]{2,1,0:T(8,128)(2,1)S(1)}, bf16[2,64,1024]{2,1,0:T(8,128)(2,1)S(1)}, u32[]{:S(2)}, u32[]{:S(2)}) %collective-permute-start) | collective-permute-done | bytes 262176 | tf_op jit(solution)/shard_map/ppermute | solution.py:88
  77.8 3.6 %norm_ext.1.ext = bf16[2,384,1024]{2,1,0:T(8,128)(2,1)S(1)} custom-call(bf16[2,256,1024]{2,1,0:T(8,128)(2,1)S(1)} %copy-done, bf16[2,64,1024]{2,1,0:T(8,128)(2,1)S(1)} %collective-permute-done.low_ref, bf16[2,64,1024]{2,1,0:T(8,128)(2,1)S(1)} %collective-permute-done.1.high_ref), custom_call_target="tpu_custom_call" | custom-call | tf_op jit(solution)/shard_map/norm_ext/pallas_call | solution.py:153
  81.5 11.2 %forward_block.1 = (f32[512,512]{1,0:T(8,128)S(1)}, bf16[512,512]{1,0:T(8,128)(2,1)S(1)}, bf16[2,256,1024]{2,1,0:T(8,128)(2,1)S(1)}, bf16[2,128,1024]{2,1,0:T(8,128)(2,1)S(1)}, bf16[2,128,1024]{2,1,0:T(8,128)(2,1)S(1)}) custom-call(bf16[2,384,1024]{2,1,0:T(8,128)(2,1)S(1)} %norm_ext.1.ext, bf16[2,256,1024]{2,1,0:T(8,128)(2,1)S(1)} %copy-done, ...), custom_call_target="tpu_custom_call" | custom-call | flops 2147483648 | bytes 16777216 | tf_op jit(solution)/shard_map/forward_block/pallas_call | solution.py:196
  94.9 5.2 %collective-permute-start.10 = (bf16[2,128,1024]{2,1,0:T(8,128)(2,1)S(1)}, bf16[2,128,1024]{2,1,0:T(8,128)(2,1)S(1)}, u32[]{:S(2)}, u32[]{:S(2)}) collective-permute-start(bf16[2,128,1024]{2,1,0:T(8,128)(2,1)S(1)} %get-tuple-element.28.last), channel_id=1, source_target_pairs={{0,2},{2,4},{4,6},{6,8},{8,10},{10,12},{12,14},{1,3},{3,5},{5,7},{... | collective-permute-start | bytes 1572872 | tf_op jit(solution)/shard_map/ppermute | solution.py:88
  100.2 7.3 %collective-permute-done.11.high = bf16[2,128,1024]{2,1,0:T(8,128)(2,1)S(1)} collective-permute-done((bf16[2,128,1024]{2,1,0:T(8,128)(2,1)S(1)}, bf16[2,128,1024]{2,1,0:T(8,128)(2,1)S(1)}, u32[]{:S(2)}, u32[]{:S(2)}) %collective-permute-start.11) | collective-permute-done | bytes 524320 | tf_op jit(solution)/shard_map/ppermute | solution.py:89
  107.6 11.4 %collective-permute-done.10.low = bf16[2,128,1024]{2,1,0:T(8,128)(2,1)S(1)} collective-permute-done((bf16[2,128,1024]{2,1,0:T(8,128)(2,1)S(1)}, bf16[2,128,1024]{2,1,0:T(8,128)(2,1)S(1)}, u32[]{:S(2)}, u32[]{:S(2)}) %collective-permute-start.10) | collective-permute-done | bytes 524320 | tf_op jit(solution)/shard_map/ppermute | solution.py:88
  118.9 8.4 %turn_block.1 = (bf16[2,512,1024]{2,1,0:T(8,128)(2,1)S(1)}, bf16[512,512]{1,0:T(8,128)(2,1)S(1)}, bf16[512,512]{1,0:T(8,128)(2,1)S(1)}, bf16[2,128,512]{2,1,0:T(8,128)(2,1)S(1)}, bf16[2,128,512]{2,1,0:T(8,128)(2,1)S(1)}) custom-call(bf16[2,128,1024]{2,1,0:T(8,128)(2,1)S(1)} %get-tuple-element.27.first, bf16[2,128,1024]{2,1,0:T(8,128)(2,1)S(1)} %get-tuple-element.28.last, ...), custom_call_target="tpu_custom_call" | custom-call | flops 2147483648 | bytes 16777216 | tf_op jit(solution)/shard_map/turn_block/pallas_call | solution.py:248
  130.4 5.0 %grads_block.3 = (f32[8,64,1024]{2,1,0:T(8,128)S(1)}, bf16[8,64,1024]{2,1,0:T(8,128)(2,1)}, f32[8,64,1024]{2,1,0:T(8,128)S(1)}, bf16[8,64,1024]{2,1,0:T(8,128)(2,1)}) custom-call(bf16[2,512,1024]{2,1,0:T(8,128)(2,1)S(1)} %copy-done.13, bf16[512,512]{1,0:T(8,128)(2,1)S(1)} %get-tuple-element.44.hid, bf16[2,256,1024]{2,1,0:T(8,128)(2,1)S(1)} %copy-done.3, ...), custom_call_target="tpu_custom_call" | custom-call | flops 2147483648 | bytes 16777216 | tf_op jit(solution)/shard_map/grads_block/pallas_call | solution.py:313
  135.4 4.4 %collective-permute-start.20 = (bf16[2,128,512]{2,1,0:T(8,128)(2,1)S(1)}, bf16[2,128,512]{2,1,0:T(8,128)(2,1)S(1)}, u32[]{:S(2)}, u32[]{:S(2)}) collective-permute-start(bf16[2,128,512]{2,1,0:T(8,128)(2,1)S(1)} %get-tuple-element.30), channel_id=1, source_target_pairs={{0,2},{2,4},{4,6},{6,8},{8,10},{10,12},{12,14},{1,3},{3,5},{5,7},{... | collective-permute-start | bytes 786440 | tf_op jit(solution)/shard_map/ppermute | solution.py:88
  141.6 10.0 %collective-permute-done.20.refs_1_ = bf16[2,128,512]{2,1,0:T(8,128)(2,1)S(1)} collective-permute-done((bf16[2,128,512]{2,1,0:T(8,128)(2,1)S(1)}, bf16[2,128,512]{2,1,0:T(8,128)(2,1)S(1)}, u32[]{:S(2)}, u32[]{:S(2)}) %collective-permute-start.20) | collective-permute-done | bytes 262176 | tf_op jit(solution)/shard_map/ppermute | solution.py:88
  151.6 16.9 %back_block.2 = (bf16[2,256,1024]{2,1,0:T(8,128)(2,1)S(1)}, bf16[512,512]{1,0:T(8,128)(2,1)S(1)}, bf16[2,64,512]{2,1,0:T(8,128)(2,1)S(1)}, bf16[2,64,512]{2,1,0:T(8,128)(2,1)S(1)}) custom-call(bf16[512,512]{1,0:T(8,128)(2,1)S(1)} %get-tuple-element.29.refs_0_.dpre, bf16[2,128,512]{2,1,0:T(8,128)(2,1)S(1)} %collective-permute-done.20.refs_1_, ...), custom_call_target="tpu_custom_call" | custom-call | flops 2147483648 | bytes 16777216 | tf_op jit(solution)/shard_map/back_block/pallas_call | solution.py:408
  168.5 3.7 %grads_block.2 = (f32[8,64,1024]{2,1,0:T(8,128)S(1)}, bf16[8,64,1024]{2,1,0:T(8,128)(2,1)S(1)}, f32[8,64,1024]{2,1,0:T(8,128)S(1)}, bf16[8,64,1024]{2,1,0:T(8,128)(2,1)S(1)}) custom-call(bf16[2,384,1024]{2,1,0:T(8,128)(2,1)S(1)} %norm_ext.1.ext, bf16[512,512]{1,0:T(8,128)(2,1)S(1)} %copy-done.15, bf16[2,256,1024]{2,1,0:T(8,128)(2,1)S(1)} %get-tuple-element.37.refs_4_.e_ref, ...), custom_call_target="tpu_custom_call" | custom-call | flops 2147483648 | bytes 16777216 | tf_op jit(solution)/shard_map/grads_block/pallas_call | solution.py:313
  172.3 4.4 %collective-permute-start.22 = (bf16[2,64,512]{2,1,0:T(8,128)(2,1)S(1)}, bf16[2,64,512]{2,1,0:T(8,128)(2,1)S(1)}, u32[]{:S(2)}, u32[]{:S(2)}) collective-permute-start(bf16[2,64,512]{2,1,0:T(8,128)(2,1)S(1)} %get-tuple-element.35), channel_id=1, source_target_pairs={{0,2},{2,4},{4,6},{6,8},{8,10},{10,12},{12,14},{1,3},{3,5},{5,7},{... | collective-permute-start | bytes 393224 | tf_op jit(solution)/shard_map/ppermute | solution.py:88
  180.1 4.6 %collective-permute-done.23.refs_2_ = bf16[2,64,512]{2,1,0:T(8,128)(2,1)S(1)} collective-permute-done((bf16[2,64,512]{2,1,0:T(8,128)(2,1)S(1)}, bf16[2,64,512]{2,1,0:T(8,128)(2,1)S(1)}, u32[]{:S(2)}, u32[]{:S(2)}) %collective-permute-start.23) | collective-permute-done | bytes 131104 | tf_op jit(solution)/shard_map/ppermute | solution.py:89
  184.7 13.2 %back_block.3 = bf16[2,256,1024]{2,1,0:T(8,128)(2,1)} custom-call(bf16[512,512]{1,0:T(8,128)(2,1)S(1)} %get-tuple-element.34.refs_0_.dpre, bf16[2,64,512]{2,1,0:T(8,128)(2,1)S(1)} %collective-permute-done.22.refs_1_, bf16[2,64,512]{2,1,0:T(8,128)(2,1)S(1)} %collective-permute-done.23.refs_2_, bf16[2,256,1024]{2,1,0:T(8,128)(2,1)S(1)} %copy-done, ...), custom_call_target="tpu_custom_call" | custom-call | flops 2147483648 | bytes 16777216 | tf_op jit(solution)/shard_map/back_block/pallas_call | solution.py:408
  202.7 3.7 %collective-permute-start.37 = (bf16[4,64,1024]{2,1,0:T(8,128)(2,1)S(1)}, bf16[4,64,1024]{2,1,0:T(8,128)(2,1)S(1)}, u32[]{:S(2)}, u32[]{:S(2)}) collective-permute-start(bf16[4,64,1024]{2,1,0:T(8,128)(2,1)S(1)} %slice.234), channel_id=1, source_target_pairs={{0,4},{2,6},{4,0},{6,2},{8,12},{10,14},{12,8},{14,10},{1,5},{3,7},... | collective-permute-start | bytes 1572872 | tf_op jit(solution)/shard_map/ppermute | solution.py:46
  207.7 6.1 %collective-permute-done.33 = bf16[4,64,1024]{2,1,0:T(8,128)(2,1)S(1)} collective-permute-done((bf16[4,64,1024]{2,1,0:T(8,128)(2,1)S(1)}, bf16[4,64,1024]{2,1,0:T(8,128)(2,1)S(1)}, u32[]{:S(2)}, u32[]{:S(2)}) %collective-permute-start.33) | collective-permute-done | bytes 524320 | tf_op jit(solution)/shard_map/ppermute | solution.py:46
  214.0 3.7 %collective-permute-start.34 = (bf16[2,64,1024]{2,1,0:T(8,128)(2,1)S(1)}, bf16[2,64,1024]{2,1,0:T(8,128)(2,1)S(1)}, u32[]{:S(2)}, u32[]{:S(2)}) collective-permute-start(bf16[2,64,1024]{2,1,0:T(8,128)(2,1)S(1)} %slice.239), channel_id=1, source_target_pairs={{0,4},{2,6},{4,0},{6,2},{8,12},{10,14},{12,8},{14,10},{1,5},{3,7},... | collective-permute-start | bytes 786440 | tf_op jit(solution)/shard_map/ppermute | solution.py:46
  223.8 3.7 %collective-permute-start.26 = (bf16[2,64,1024]{2,1,0:T(8,128)(2,1)S(1)}, bf16[2,64,1024]{2,1,0:T(8,128)(2,1)S(1)}, u32[]{:S(2)}, u32[]{:S(2)}) collective-permute-start(bf16[2,64,1024]{2,1,0:T(8,128)(2,1)S(1)} %slice.241), channel_id=1, source_target_pairs={{0,4},{2,6},{4,0},{6,2},{8,12},{10,14},{12,8},{14,10},{1,5},{3,7},... | collective-permute-start | bytes 786440 | tf_op jit(solution)/shard_map/ppermute | solution.py:46
  227.5 8.6 %collective-permute-done.29 = bf16[4,64,1024]{2,1,0:T(8,128)(2,1)S(1)} collective-permute-done((bf16[4,64,1024]{2,1,0:T(8,128)(2,1)S(1)}, bf16[4,64,1024]{2,1,0:T(8,128)(2,1)S(1)}, u32[]{:S(2)}, u32[]{:S(2)}) %collective-permute-start.29) | collective-permute-done | bytes 524320 | tf_op jit(solution)/shard_map/ppermute | solution.py:46
  237.6 3.7 %collective-permute-done.38 = bf16[2,64,1024]{2,1,0:T(8,128)(2,1)S(1)} collective-permute-done((bf16[2,64,1024]{2,1,0:T(8,128)(2,1)S(1)}, bf16[2,64,1024]{2,1,0:T(8,128)(2,1)S(1)}, u32[]{:S(2)}, u32[]{:S(2)}) %collective-permute-start.38) | collective-permute-done | bytes 262176 | tf_op jit(solution)/shard_map/ppermute | solution.py:46
  246.5 12.2 %collective-permute-done.35 = bf16[1,64,1024]{2,1,0:T(8,128)(2,1)S(1)} collective-permute-done((bf16[1,64,1024]{2,1,0:T(8,128)(2,1)S(1)}, bf16[1,64,1024]{2,1,0:T(8,128)(2,1)S(1)}, u32[]{:S(2)}, u32[]{:S(2)}) %collective-permute-start.35) | collective-permute-done | bytes 131104 | tf_op jit(solution)/shard_map/ppermute | solution.py:46
  263.3 3.7 %collective-permute-done.31 = bf16[1,64,1024]{2,1,0:T(8,128)(2,1)S(1)} collective-permute-done((bf16[1,64,1024]{2,1,0:T(8,128)(2,1)S(1)}, bf16[1,64,1024]{2,1,0:T(8,128)(2,1)S(1)}, u32[]{:S(2)}, u32[]{:S(2)}) %collective-permute-start.31) | collective-permute-done | bytes 131104 | tf_op jit(solution)/shard_map/ppermute | solution.py:46
  267.1 3.2 %collective-permute-done.27 = bf16[1,64,1024]{2,1,0:T(8,128)(2,1)S(1)} collective-permute-done((bf16[1,64,1024]{2,1,0:T(8,128)(2,1)S(1)}, bf16[1,64,1024]{2,1,0:T(8,128)(2,1)S(1)}, u32[]{:S(2)}, u32[]{:S(2)}) %collective-permute-start.27) | collective-permute-done | bytes 131104 | tf_op jit(solution)/shard_map/ppermute | solution.py:46
  (160 shorter events, 52.3 us)
Async XLA Ops:
  1.8 20.3 %collective-permute-start.12 = (bf16[1,64,1024]{2,1,0:T(8,128)(2,1)S(1)}, bf16[1,64,1024]{2,1,0:T(8,128)(2,1)S(1)}, u32[]{:S(2)}, u32[]{:S(2)}) collective-permute-start(bf16[1,64,1024]{2,1,0:T(8,128)(2,1)S(1)} %broadcast_in_dim_reshape.7), channel_id=1, source_target_pairs={{0,8},{2,10},{4,12},{6,14},{8,0},{10,2},{12,4},{14,6},{1,9},{3,11}... | collective-permute-start | bytes 393224 | tf_op jit(solution)/shard_map/ppermute | solution.py:46
  8.8 13.5 %collective-permute-start.16 = (bf16[1,64,1024]{2,1,0:T(8,128)(2,1)S(1)}, bf16[1,64,1024]{2,1,0:T(8,128)(2,1)S(1)}, u32[]{:S(2)}, u32[]{:S(2)}) collective-permute-start(bf16[1,64,1024]{2,1,0:T(8,128)(2,1)S(1)} %maximum_bitcast_fusion.1), channel_id=1, source_target_pairs={{0,2},{2,0},{4,6},{6,4},{8,10},{10,8},{12,14},{14,12},{1,3},{3,1},... | collective-permute-start | bytes 393224 | tf_op jit(solution)/shard_map/ppermute | solution.py:46
  17.9 14.6 %collective-permute-start.3 = (bf16[2,64,1024]{2,1,0:T(8,128)(2,1)S(1)}, bf16[2,64,1024]{2,1,0:T(8,128)(2,1)S(1)}, u32[]{:S(2)}, u32[]{:S(2)}) collective-permute-start(bf16[2,64,1024]{2,1,0:T(8,128)(2,1)S(1)} %pad_maximum_fusion.8), channel_id=1, source_target_pairs={{0,4},{2,6},{4,0},{6,2},{8,12},{10,14},{12,8},{14,10},{1,5},{3,7},... | collective-permute-start | bytes 786440 | tf_op jit(solution)/shard_map/ppermute | solution.py:46
  18.7 16.4 %collective-permute-start.7 = (bf16[2,64,1024]{2,1,0:T(8,128)(2,1)S(1)}, bf16[2,64,1024]{2,1,0:T(8,128)(2,1)S(1)}, u32[]{:S(2)}, u32[]{:S(2)}) collective-permute-start(bf16[2,64,1024]{2,1,0:T(8,128)(2,1)S(1)} %pad_maximum_fusion.9), channel_id=1, source_target_pairs={{0,8},{2,10},{4,12},{6,14},{8,0},{10,2},{12,4},{14,6},{1,9},{3,11}... | collective-permute-start | bytes 786440 | tf_op jit(solution)/shard_map/ppermute | solution.py:46
  22.2 21.5 %collective-permute-start.13 = (bf16[2,64,1024]{2,1,0:T(8,128)(2,1)S(1)}, bf16[2,64,1024]{2,1,0:T(8,128)(2,1)S(1)}, u32[]{:S(2)}, u32[]{:S(2)}) collective-permute-start(bf16[2,64,1024]{2,1,0:T(8,128)(2,1)S(1)} %pad_maximum_fusion.10), channel_id=1, source_target_pairs={{0,4},{2,6},{4,0},{6,2},{8,12},{10,14},{12,8},{14,10},{1,5},{3,7},... | collective-permute-start | bytes 786440 | tf_op jit(solution)/shard_map/ppermute | solution.py:46
  22.3 23.1 %collective-permute-start.17 = (bf16[2,64,1024]{2,1,0:T(8,128)(2,1)S(1)}, bf16[2,64,1024]{2,1,0:T(8,128)(2,1)S(1)}, u32[]{:S(2)}, u32[]{:S(2)}) collective-permute-start(bf16[2,64,1024]{2,1,0:T(8,128)(2,1)S(1)} %pad_maximum_fusion.11), channel_id=1, source_target_pairs={{0,8},{2,10},{4,12},{6,14},{8,0},{10,2},{12,4},{14,6},{1,9},{3,11}... | collective-permute-start | bytes 786440 | tf_op jit(solution)/shard_map/ppermute | solution.py:46
  32.5 13.7 %collective-permute-start.4 = (bf16[4,64,1024]{2,1,0:T(8,128)(2,1)S(1)}, bf16[4,64,1024]{2,1,0:T(8,128)(2,1)S(1)}, u32[]{:S(2)}, u32[]{:S(2)}) collective-permute-start(bf16[4,64,1024]{2,1,0:T(8,128)(2,1)S(1)} %pad_maximum_fusion.2), channel_id=1, source_target_pairs={{0,2},{2,0},{4,6},{6,4},{8,10},{10,8},{12,14},{14,12},{1,3},{3,1},... | collective-permute-start | bytes 1572872 | tf_op jit(solution)/shard_map/ppermute | solution.py:46
  35.1 20.2 %collective-permute-start.8 = (bf16[4,64,1024]{2,1,0:T(8,128)(2,1)S(1)}, bf16[4,64,1024]{2,1,0:T(8,128)(2,1)S(1)}, u32[]{:S(2)}, u32[]{:S(2)}) collective-permute-start(bf16[4,64,1024]{2,1,0:T(8,128)(2,1)S(1)} %pad_maximum_fusion.3), channel_id=1, source_target_pairs={{0,4},{2,6},{4,0},{6,2},{8,12},{10,14},{12,8},{14,10},{1,5},{3,7},... | collective-permute-start | bytes 1572872 | tf_op jit(solution)/shard_map/ppermute | solution.py:46
  43.8 13.1 %collective-permute-start.14 = (bf16[4,64,1024]{2,1,0:T(8,128)(2,1)S(1)}, bf16[4,64,1024]{2,1,0:T(8,128)(2,1)S(1)}, u32[]{:S(2)}, u32[]{:S(2)}) collective-permute-start(bf16[4,64,1024]{2,1,0:T(8,128)(2,1)S(1)} %pad_maximum_fusion.4), channel_id=1, source_target_pairs={{0,2},{2,0},{4,6},{6,4},{8,10},{10,8},{12,14},{14,12},{1,3},{3,1},... | collective-permute-start | bytes 1572872 | tf_op jit(solution)/shard_map/ppermute | solution.py:46
  45.5 21.0 %collective-permute-start.18 = (bf16[4,64,1024]{2,1,0:T(8,128)(2,1)S(1)}, bf16[4,64,1024]{2,1,0:T(8,128)(2,1)S(1)}, u32[]{:S(2)}, u32[]{:S(2)}) collective-permute-start(bf16[4,64,1024]{2,1,0:T(8,128)(2,1)S(1)} %pad_maximum_fusion.5), channel_id=1, source_target_pairs={{0,4},{2,6},{4,0},{6,2},{8,12},{10,14},{12,8},{14,10},{1,5},{3,7},... | collective-permute-start | bytes 1572872 | tf_op jit(solution)/shard_map/ppermute | solution.py:46
  46.3 35.2 %collective-permute-start.5 = (bf16[8,64,1024]{2,1,0:T(8,128)(2,1)S(1)}, bf16[8,64,1024]{2,1,0:T(8,128)(2,1)S(1)}, u32[]{:S(2)}, u32[]{:S(2)}) collective-permute-start(bf16[8,64,1024]{2,1,0:T(8,128)(2,1)S(1)} %constant_dynamic-update-slice_fusion.a0.refs_5_), channel_id=1, source_target_pairs={{0,1},{1,0},{2,3},{3,2},{4,5},{5,4},{6,7},{7,6},{8,9},{9,8},{10,11... | collective-permute-start | bytes 3145736 | tf_op jit(solution)/shard_map/ppermute | solution.py:46
  55.4 26.1 %collective-permute-start.9 = (bf16[8,64,1024]{2,1,0:T(8,128)(2,1)S(1)}, bf16[8,64,1024]{2,1,0:T(8,128)(2,1)S(1)}, u32[]{:S(2)}, u32[]{:S(2)}) collective-permute-start(bf16[8,64,1024]{2,1,0:T(8,128)(2,1)S(1)} %pad_maximum_fusion.b0.refs_9_.refs_7_), channel_id=1, source_target_pairs={{0,1},{1,0},{2,3},{3,2},{4,5},{5,4},{6,7},{7,6},{8,9},{9,8},{10,11... | collective-permute-start | bytes 3145736 | tf_op jit(solution)/shard_map/ppermute | solution.py:46
  55.5 11.2 %collective-permute-start.1 = (bf16[2,64,1024]{2,1,0:T(8,128)(2,1)S(1)}, bf16[2,64,1024]{2,1,0:T(8,128)(2,1)S(1)}, u32[]{:S(2)}, u32[]{:S(2)}) collective-permute-start(bf16[2,64,1024]{2,1,0:T(8,128)(2,1)S(1)} %get-tuple-element.49), channel_id=1, source_target_pairs={{2,0},{4,2},{6,4},{8,6},{10,8},{12,10},{14,12},{3,1},{5,3},{7,5},{... | collective-permute-start | bytes 786440 | tf_op jit(solution)/shard_map/ppermute | solution.py:89
  56.9 43.3 %collective-permute-start.15 = (bf16[8,64,1024]{2,1,0:T(8,128)(2,1)S(1)}, bf16[8,64,1024]{2,1,0:T(8,128)(2,1)S(1)}, u32[]{:S(2)}, u32[]{:S(2)}) collective-permute-start(bf16[8,64,1024]{2,1,0:T(8,128)(2,1)S(1)} %constant_dynamic-update-slice_fusion.4.a0.refs_5_), channel_id=1, source_target_pairs={{0,1},{1,0},{2,3},{3,2},{4,5},{5,4},{6,7},{7,6},{8,9},{9,8},{10,11... | collective-permute-start | bytes 3145736 | tf_op jit(solution)/shard_map/ppermute | solution.py:46
  66.6 33.6 %collective-permute-start.19 = (bf16[8,64,1024]{2,1,0:T(8,128)(2,1)S(1)}, bf16[8,64,1024]{2,1,0:T(8,128)(2,1)S(1)}, u32[]{:S(2)}, u32[]{:S(2)}) collective-permute-start(bf16[8,64,1024]{2,1,0:T(8,128)(2,1)S(1)} %pad_maximum_fusion.1.b0.refs_7_), channel_id=1, source_target_pairs={{0,1},{1,0},{2,3},{3,2},{4,5},{5,4},{6,7},{7,6},{8,9},{9,8},{10,11... | collective-permute-start | bytes 3145736 | tf_op jit(solution)/shard_map/ppermute | solution.py:46
  93.7 13.9 %collective-permute-start.11 = (bf16[2,128,1024]{2,1,0:T(8,128)(2,1)S(1)}, bf16[2,128,1024]{2,1,0:T(8,128)(2,1)S(1)}, u32[]{:S(2)}, u32[]{:S(2)}) collective-permute-start(bf16[2,128,1024]{2,1,0:T(8,128)(2,1)S(1)} %get-tuple-element.27.first), channel_id=1, source_target_pairs={{2,0},{4,2},{6,4},{8,6},{10,8},{12,10},{14,12},{3,1},{5,3},{7,5},{... | collective-permute-start | bytes 1572872 | tf_op jit(solution)/shard_map/ppermute | solution.py:89
  94.9 24.0 %collective-permute-start.10 = (bf16[2,128,1024]{2,1,0:T(8,128)(2,1)S(1)}, bf16[2,128,1024]{2,1,0:T(8,128)(2,1)S(1)}, u32[]{:S(2)}, u32[]{:S(2)}) collective-permute-start(bf16[2,128,1024]{2,1,0:T(8,128)(2,1)S(1)} %get-tuple-element.28.last), channel_id=1, source_target_pairs={{0,2},{2,4},{4,6},{6,8},{8,10},{10,12},{12,14},{1,3},{3,5},{5,7},{... | collective-permute-start | bytes 1572872 | tf_op jit(solution)/shard_map/ppermute | solution.py:88
  135.4 62.5 %collective-permute-start.32 = (bf16[8,64,1024]{2,1,0:T(8,128)(2,1)}, bf16[8,64,1024]{2,1,0:T(8,128)(2,1)S(1)}, u32[]{:S(2)}, u32[]{:S(2)}) collective-permute-start(bf16[8,64,1024]{2,1,0:T(8,128)(2,1)} %get-tuple-element.46), channel_id=1, source_target_pairs={{0,1},{1,0},{2,3},{3,2},{4,5},{5,4},{6,7},{7,6},{8,9},{9,8},{10,11... | collective-permute-start | bytes 3145736 | tf_op jit(solution)/shard_map/ppermute | solution.py:46
  135.4 16.2 %collective-permute-start.20 = (bf16[2,128,512]{2,1,0:T(8,128)(2,1)S(1)}, bf16[2,128,512]{2,1,0:T(8,128)(2,1)S(1)}, u32[]{:S(2)}, u32[]{:S(2)}) collective-permute-start(bf16[2,128,512]{2,1,0:T(8,128)(2,1)S(1)} %get-tuple-element.30), channel_id=1, source_target_pairs={{0,2},{2,4},{4,6},{6,8},{8,10},{10,12},{12,14},{1,3},{3,5},{5,7},{... | collective-permute-start | bytes 786440 | tf_op jit(solution)/shard_map/ppermute | solution.py:88
  139.8 11.8 %collective-permute-start.21 = (bf16[2,128,512]{2,1,0:T(8,128)(2,1)S(1)}, bf16[2,128,512]{2,1,0:T(8,128)(2,1)S(1)}, u32[]{:S(2)}, u32[]{:S(2)}) collective-permute-start(bf16[2,128,512]{2,1,0:T(8,128)(2,1)S(1)} %get-tuple-element.31), channel_id=1, source_target_pairs={{2,0},{4,2},{6,4},{8,6},{10,8},{12,10},{14,12},{3,1},{5,3},{7,5},{... | collective-permute-start | bytes 786440 | tf_op jit(solution)/shard_map/ppermute | solution.py:89
  141.4 59.6 %collective-permute-start.36 = (bf16[8,64,1024]{2,1,0:T(8,128)(2,1)}, bf16[8,64,1024]{2,1,0:T(8,128)(2,1)}, u32[]{:S(2)}, u32[]{:S(2)}) collective-permute-start(bf16[8,64,1024]{2,1,0:T(8,128)(2,1)} %get-tuple-element.48), channel_id=1, source_target_pairs={{0,1},{1,0},{2,3},{3,2},{4,5},{5,4},{6,7},{7,6},{8,9},{9,8},{10,11... | collective-permute-start | bytes 3145736 | tf_op jit(solution)/shard_map/ppermute | solution.py:46
  172.2 34.2 %collective-permute-start.24 = (bf16[8,64,1024]{2,1,0:T(8,128)(2,1)S(1)}, bf16[8,64,1024]{2,1,0:T(8,128)(2,1)S(1)}, u32[]{:S(2)}, u32[]{:S(2)}) collective-permute-start(bf16[8,64,1024]{2,1,0:T(8,128)(2,1)S(1)} %get-tuple-element.40), channel_id=1, source_target_pairs={{0,1},{1,0},{2,3},{3,2},{4,5},{5,4},{6,7},{7,6},{8,9},{9,8},{10,11... | collective-permute-start | bytes 3145736 | tf_op jit(solution)/shard_map/ppermute | solution.py:46
  180.1 27.0 %collective-permute-start.28 = (bf16[8,64,1024]{2,1,0:T(8,128)(2,1)S(1)}, bf16[8,64,1024]{2,1,0:T(8,128)(2,1)S(1)}, u32[]{:S(2)}, u32[]{:S(2)}) collective-permute-start(bf16[8,64,1024]{2,1,0:T(8,128)(2,1)S(1)} %get-tuple-element.42), channel_id=1, source_target_pairs={{0,1},{1,0},{2,3},{3,2},{4,5},{5,4},{6,7},{7,6},{8,9},{9,8},{10,11... | collective-permute-start | bytes 3145736 | tf_op jit(solution)/shard_map/ppermute | solution.py:46
  198.3 15.5 %collective-permute-start.33 = (bf16[4,64,1024]{2,1,0:T(8,128)(2,1)S(1)}, bf16[4,64,1024]{2,1,0:T(8,128)(2,1)S(1)}, u32[]{:S(2)}, u32[]{:S(2)}) collective-permute-start(bf16[4,64,1024]{2,1,0:T(8,128)(2,1)S(1)} %slice.235), channel_id=1, source_target_pairs={{0,2},{2,0},{4,6},{6,4},{8,10},{10,8},{12,14},{14,12},{1,3},{3,1},... | collective-permute-start | bytes 1572872 | tf_op jit(solution)/shard_map/ppermute | solution.py:46
  202.7 16.5 %collective-permute-start.37 = (bf16[4,64,1024]{2,1,0:T(8,128)(2,1)S(1)}, bf16[4,64,1024]{2,1,0:T(8,128)(2,1)S(1)}, u32[]{:S(2)}, u32[]{:S(2)}) collective-permute-start(bf16[4,64,1024]{2,1,0:T(8,128)(2,1)S(1)} %slice.234), channel_id=1, source_target_pairs={{0,4},{2,6},{4,0},{6,2},{8,12},{10,14},{12,8},{14,10},{1,5},{3,7},... | collective-permute-start | bytes 1572872 | tf_op jit(solution)/shard_map/ppermute | solution.py:46
  207.0 16.7 %collective-permute-start.25 = (bf16[4,64,1024]{2,1,0:T(8,128)(2,1)S(1)}, bf16[4,64,1024]{2,1,0:T(8,128)(2,1)S(1)}, u32[]{:S(2)}, u32[]{:S(2)}) collective-permute-start(bf16[4,64,1024]{2,1,0:T(8,128)(2,1)S(1)} %slice.237), channel_id=1, source_target_pairs={{0,2},{2,0},{4,6},{6,4},{8,10},{10,8},{12,14},{14,12},{1,3},{3,1},... | collective-permute-start | bytes 1572872 | tf_op jit(solution)/shard_map/ppermute | solution.py:46
  207.6 28.6 %collective-permute-start.29 = (bf16[4,64,1024]{2,1,0:T(8,128)(2,1)S(1)}, bf16[4,64,1024]{2,1,0:T(8,128)(2,1)S(1)}, u32[]{:S(2)}, u32[]{:S(2)}) collective-permute-start(bf16[4,64,1024]{2,1,0:T(8,128)(2,1)S(1)} %slice.236), channel_id=1, source_target_pairs={{0,4},{2,6},{4,0},{6,2},{8,12},{10,14},{12,8},{14,10},{1,5},{3,7},... | collective-permute-start | bytes 1572872 | tf_op jit(solution)/shard_map/ppermute | solution.py:46
  214.0 30.4 %collective-permute-start.34 = (bf16[2,64,1024]{2,1,0:T(8,128)(2,1)S(1)}, bf16[2,64,1024]{2,1,0:T(8,128)(2,1)S(1)}, u32[]{:S(2)}, u32[]{:S(2)}) collective-permute-start(bf16[2,64,1024]{2,1,0:T(8,128)(2,1)S(1)} %slice.239), channel_id=1, source_target_pairs={{0,4},{2,6},{4,0},{6,2},{8,12},{10,14},{12,8},{14,10},{1,5},{3,7},... | collective-permute-start | bytes 786440 | tf_op jit(solution)/shard_map/ppermute | solution.py:46
  219.5 21.8 %collective-permute-start.38 = (bf16[2,64,1024]{2,1,0:T(8,128)(2,1)S(1)}, bf16[2,64,1024]{2,1,0:T(8,128)(2,1)S(1)}, u32[]{:S(2)}, u32[]{:S(2)}) collective-permute-start(bf16[2,64,1024]{2,1,0:T(8,128)(2,1)S(1)} %slice.238), channel_id=1, source_target_pairs={{0,8},{2,10},{4,12},{6,14},{8,0},{10,2},{12,4},{14,6},{1,9},{3,11}... | collective-permute-start | bytes 786440 | tf_op jit(solution)/shard_map/ppermute | solution.py:46
  223.8 39.3 %collective-permute-start.26 = (bf16[2,64,1024]{2,1,0:T(8,128)(2,1)S(1)}, bf16[2,64,1024]{2,1,0:T(8,128)(2,1)S(1)}, u32[]{:S(2)}, u32[]{:S(2)}) collective-permute-start(bf16[2,64,1024]{2,1,0:T(8,128)(2,1)S(1)} %slice.241), channel_id=1, source_target_pairs={{0,4},{2,6},{4,0},{6,2},{8,12},{10,14},{12,8},{14,10},{1,5},{3,7},... | collective-permute-start | bytes 786440 | tf_op jit(solution)/shard_map/ppermute | solution.py:46
  237.0 24.9 %collective-permute-start.30 = (bf16[2,64,1024]{2,1,0:T(8,128)(2,1)}, bf16[2,64,1024]{2,1,0:T(8,128)(2,1)S(1)}, u32[]{:S(2)}, u32[]{:S(2)}) collective-permute-start(bf16[2,64,1024]{2,1,0:T(8,128)(2,1)} %slice.240), channel_id=1, source_target_pairs={{0,8},{2,10},{4,12},{6,14},{8,0},{10,2},{12,4},{14,6},{1,9},{3,11}... | collective-permute-start | bytes 786440 | tf_op jit(solution)/shard_map/ppermute | solution.py:46
  244.5 14.1 %collective-permute-start.35 = (bf16[1,64,1024]{2,1,0:T(8,128)(2,1)S(1)}, bf16[1,64,1024]{2,1,0:T(8,128)(2,1)S(1)}, u32[]{:S(2)}, u32[]{:S(2)}) collective-permute-start(bf16[1,64,1024]{2,1,0:T(8,128)(2,1)S(1)} %slice.243), channel_id=1, source_target_pairs={{0,8},{2,10},{4,12},{6,14},{8,0},{10,2},{12,4},{14,6},{1,9},{3,11}... | collective-permute-start | bytes 393224 | tf_op jit(solution)/shard_map/ppermute | solution.py:46
  (25 other events, 378.4 us)

commit v2 on v1

v2 whole, which is shorter than its diff:
```python
import functools
import math

import jax
import jax.numpy as jnp
from jax import lax
from jax.experimental import pallas as pl
from jax.experimental.pallas import tpu as pltpu
from jax.sharding import PartitionSpec as P

DILATE_ONE = 64
DILATE_TWO = 128
BF = jnp.bfloat16
F32 = jnp.float32
ROOT = math.sqrt(2.0 / math.pi)
CUBE = 0.044715
VMEM = pl.BlockSpec(memory_space=pltpu.VMEM)
NT = (((1,), (1,)), ((), ()))
TN = (((0,), (0,)), ((), ()))


def gelu(v):
    return v * (0.5 * (1.0 + jnp.tanh(ROOT * (v + CUBE * (v * v * v)))))


def gelu_slope(v):
    t = jnp.tanh(ROOT * (v + CUBE * (v * v * v)))
    return 0.5 * (1.0 + t) + (0.5 * v) * (1.0 - t * t) * (ROOT * (1.0 + 3.0 * CUBE * (v * v)))


def norm_scale(v):
    return lax.rsqrt(jnp.mean(v * v, axis=-1, keepdims=True) + 1e-06)


def dot(a, b, dims=(((1,), (0,)), ((), ()))):
    return lax.dot_general(a, b, dims, preferred_element_type=F32)


def cost(flat, width, middle):
    return pl.CostEstimate(
        flops=8 * flat * width * middle, bytes_accessed=8 << 20, transcendentals=0
    )


def params():
    return pltpu.CompilerParams(vmem_limit_bytes=40 << 20)


def tie(*values):
    return lax.optimization_barrier(values)


def step_orders(count):
    bits = [1 << i for i in reversed(range(count.bit_length() - 1))]
    assert math.prod([2] * len(bits)) == count
    return bits, bits[-1:] + bits[:-1]


def place_of(offset, steps):
    place = 0
    for j, step in enumerate(steps):
        shift = step.bit_length() - 1
        place = place + (((offset >> shift) & 1) << j)
    return place


def cross(value):
    return lax.ppermute(value, "dp", [(0, 1), (1, 0)])


def hop(value, orders, j):
    count = lax.axis_size("seq")
    pairs = [
        (2 * i + core, 2 * (i ^ orders[core][j]) + core)
        for i in range(count)
        for core in range(2)
    ]
    return lax.ppermute(value, ("seq", "dp"), pairs)


def widen(value, orders, j):
    return jnp.concatenate([value, hop(value, orders, j)], axis=0)


def fold(total, orders, j):
    half = total.shape[0] // 2
    return total[:half] + hop(total[half:].astype(BF), orders, j).astype(F32)


def halo(first, last):
    count = lax.axis_size("seq")
    low = lax.ppermute(last, "seq", [(i, i + 1) for i in range(count - 1)])
    high = lax.ppermute(first, "seq", [(i + 1, i) for i in range(count - 1)])
    return low, high


def by_core(own, other, run):
    core = lax.axis_index("dp")

    @pl.when(core == 0)
    def _():
        run(own, other)

    @pl.when(core == 1)
    def _():
        run(other, own)


def conv_weights(orders, taps, rest, middle):
    here = lax.axis_index("seq")
    count = taps.shape[0]

    def whole(ref, steps, half):
        cols = slice(half * middle, (half + 1) * middle)
        return jnp.concatenate(
            [ref[place_of(here ^ chip, steps), :, cols] for chip in range(count)], axis=0
        )

    return [
        lambda: whole(taps, orders[0], 0),
        lambda: whole(taps, orders[0], 1),
        lambda: whole(rest, orders[1], 0),
    ]


def mix_halves(orders, rest, middle):
    here = lax.axis_index("seq")
    count, rows = rest.shape[:2]
    part = rows // 4

    def half(h):
        pieces = []
        for chip in range(count):
            place = place_of(here ^ chip, orders[1])
            for lane in range(2):
                start = (2 * lane + h) * part
                pieces.append(rest[place, start : start + part, middle:])
        return jnp.concatenate(pieces, axis=0)

    return [lambda: half(0), lambda: half(1)]


def norm_kernel(x_ref, low_ref, high_ref, ext_ref):
    dilate = low_ref.shape[1]
    length = x_ref.shape[1]
    for w in range(x_ref.shape[0]):
        for source, start, size in (
            (low_ref, 0, dilate),
            (x_ref, dilate, length),
            (high_ref, dilate + length, dilate),
        ):

            @pl.loop(0, size // 32)
            def _(i):
                rows = pl.multiple_of(i * 32, 32)
                v = source[w, pl.ds(rows, 32), :].astype(F32)
                ext_ref[w, pl.ds(start + rows, 32), :] = gelu(v * norm_scale(v)).astype(BF)


def norm_ext(x, low, high):
    windows, length, width = x.shape
    return pl.pallas_call(
        norm_kernel,
        out_shape=jax.ShapeDtypeStruct((windows, length + 2 * low.shape[1], width), BF),
        in_specs=[VMEM] * 3,
        out_specs=VMEM,
        compiler_params=params(),
        name="norm_ext",
    )(x, low, high)


def forward_kernel(
    orders, dilate, edge, ext, x_ref, own, other, pre_ref, hid_ref, x2_ref, first_ref, last_ref
):
    windows, length, width = x_ref.shape
    middle = hid_ref.shape[1]

    def run(taps, rest):
        conv = conv_weights(orders, taps, rest, middle)
        mix = mix_halves(orders, rest, middle)
        for w in range(windows):
            rows = slice(w * length, (w + 1) * length)
            pre = sum(dot(ext[w, k * dilate : k * dilate + length, :], conv[k]()) for k in range(3))
            pre_ref[rows, :] = pre
            hid = gelu(pre).astype(BF)
            hid_ref[rows, :] = hid
            for h in range(2):
                cols = slice(h * middle, (h + 1) * middle)
                x2_ref[w, :, cols] = (x_ref[w, :, cols].astype(F32) + dot(hid, mix[h]())).astype(BF)

    by_core(own, other, run)
    for w in range(windows):
        for target, start in ((first_ref, 0), (last_ref, length - edge)):

            @pl.loop(0, edge // 32)
            def _(i):
                rows = pl.multiple_of(i * 32, 32)
                v = x2_ref[w, pl.ds(start + rows, 32), :].astype(F32)
                target[w, pl.ds(rows, 32), :] = gelu(v * norm_scale(v)).astype(BF)


def forward_block(ext, x, pieces, orders, dilate, edge):
    windows, length, width = x.shape
    middle = pieces[0].shape[2] // 2
    flat = windows * length
    return pl.pallas_call(
        functools.partial(forward_kernel, orders, dilate, edge),
        out_shape=(
            jax.ShapeDtypeStruct((flat, middle), F32),
            jax.ShapeDtypeStruct((flat, middle), BF),
            jax.ShapeDtypeStruct(x.shape, BF),
            jax.ShapeDtypeStruct((windows, edge, width), BF),
            jax.ShapeDtypeStruct((windows, edge, width), BF),
        ),
        in_specs=[VMEM] * 4,
        out_specs=(VMEM,) * 5,
        compiler_params=params(),
        cost_estimate=cost(flat, width, middle),
        name="forward_block",
    )(ext, x, *pieces)


def turn_kernel(
    orders, dilate, first, last, low, high, e_ref, own, other,
    ext, hid_ref, dpre_ref, dfirst, dlast,
):
    windows, length, width = e_ref.shape
    edge = first.shape[1]
    middle = hid_ref.shape[1]
    for w in range(windows):
        for source, start in (
            (low, 0), (first, dilate), (last, dilate + length - edge), (high, dilate + length),
        ):
            ext[w, start : start + edge, :] = source[w]

    def run(taps, rest):
        conv = conv_weights(orders, taps, rest, middle)
        mix = mix_halves(orders, rest, middle)
        for w in range(windows):
            rows = slice(w * length, (w + 1) * length)
            pre = sum(dot(ext[w, k * dilate : k * dilate + length, :], conv[k]()) for k in range(3))
            dhid = dot(e_ref[w, :, :middle], mix[0](), NT) + dot(e_ref[w, :, middle:], mix[1](), NT)
            hid_ref[rows, :] = gelu(pre).astype(BF)
            dpre_ref[rows, :] = (gelu_slope(pre) * dhid).astype(BF)

    by_core(own, other, run)
    for w in range(windows):
        dfirst[w] = dpre_ref[w * length : w * length + dilate, :]
        dlast[w] = dpre_ref[(w + 1) * length - dilate : (w + 1) * length, :]


def turn_block(first, last, low, high, e, pieces, orders, dilate):
    windows, length, width = e.shape
    middle = pieces[0].shape[2] // 2
    flat = windows * length
    return pl.pallas_call(
        functools.partial(turn_kernel, orders, dilate),
        out_shape=(
            jax.ShapeDtypeStruct((windows, length + 2 * dilate, width), BF),
            jax.ShapeDtypeStruct((flat, middle), BF),
            jax.ShapeDtypeStruct((flat, middle), BF),
            jax.ShapeDtypeStruct((windows, dilate, middle), BF),
            jax.ShapeDtypeStruct((windows, dilate, middle), BF),
        ),
        in_specs=[VMEM] * 7,
        out_specs=(VMEM,) * 5,
        compiler_params=params(),
        cost_estimate=cost(flat, width, middle),
        name="turn_block",
    )(first, last, low, high, e, *pieces)


def grads_kernel(orders, dilate, ext, hid, e_ref, dpre, keep, send, full):
    here, core = lax.axis_index("seq"), lax.axis_index("dp")
    windows, length, width = e_ref.shape
    middle = hid.shape[1]
    count, rows = keep.shape[:2]
    part = rows // 4

    def put(target, k):
        steps = orders[k // 2]
        cols = slice((k % 2) * middle, (k % 2 + 1) * middle)
        for chip in range(count):
            place = place_of(here ^ chip, steps)
            if k < 3:
                value = full[chip * rows : (chip + 1) * rows, :]
                target[place, :, cols] = value.astype(target.dtype)
                continue
            for lane in range(2):
                for h in range(2):
                    base = h * middle + (2 * chip + lane) * part
                    start = (2 * lane + h) * part
                    value = full[base : base + part, :]
                    target[place, start : start + part, cols] = value.astype(target.dtype)

    for k in range(4):
        if k == 3:
            for h in range(2):
                e = jnp.concatenate(
                    [e_ref[w, :, h * middle : (h + 1) * middle] for w in range(windows)], axis=0
                )
                full[h * middle : (h + 1) * middle, :] = dot(hid[...], e, TN)
        else:
            view = jnp.concatenate(
                [ext[w, k * dilate : k * dilate + length, :] for w in range(windows)], axis=0
            )
            full[...] = dot(view, dpre[...], TN)

        @pl.when(core == k // 2)
        def _():
            put(keep, k)

        @pl.when(core != k // 2)
        def _():
            put(send, k)


def grads_block(ext, hid, e, dpre, orders, dilate, count):
    windows, length, width = e.shape
    flat, middle = hid.shape
    shape = (count, width // count, 2 * middle)
    return pl.pallas_call(
        functools.partial(grads_kernel, orders, dilate),
        out_shape=(jax.ShapeDtypeStruct(shape, F32), jax.ShapeDtypeStruct(shape, BF)),
        in_specs=[VMEM] * 4,
        out_specs=(VMEM,) * 2,
        scratch_shapes=[pltpu.VMEM((width, middle), F32)],
        compiler_params=params(),
        cost_estimate=cost(flat, width, middle),
        name="grads_block",
    )(ext, hid, e, dpre)


def back_kernel(orders, dilate, chained, *refs):
    dpre, low, high, x_ref, e_ref, own, other = refs[:7]
    if chained:
        own_m, other_m, pre_ref, out_ref, dprev, dfirst, dlast, ext, dn = refs[7:]
    else:
        out_ref, ext, dn = refs[7:]
    windows, length, width = x_ref.shape
    middle = dpre.shape[1]
    for w in range(windows):
        ext[w, :dilate, :] = low[w]
        ext[w, dilate : dilate + length, :] = dpre[w * length : (w + 1) * length, :]
        ext[w, dilate + length :, :] = high[w]

    def run(taps, rest):
        conv = conv_weights(orders, taps, rest, middle)
        for w in range(windows):
            dn[w] = sum(
                dot(ext[w, (2 - k) * dilate : (2 - k) * dilate + length, :], conv[k](), NT)
                for k in range(3)
            )

    by_core(own, other, run)
    for w in range(windows):

        @pl.loop(0, length // 32)
        def _(i):
            rows = pl.ds(pl.multiple_of(i * 32, 32), 32)
            v = x_ref[w, rows, :].astype(F32)
            scale = norm_scale(v)
            u = v * scale
            g = dn[w, rows, :] * gelu_slope(u)
            dv = scale * (g - u * jnp.mean(g * u, axis=-1, keepdims=True))
            out_ref[w, rows, :] = (e_ref[w, rows, :].astype(F32) + dv).astype(BF)

    if chained:

        def turn(taps, rest):
            mix = mix_halves(orders, rest, middle)
            for w in range(windows):
                dhid = dot(out_ref[w, :, :middle], mix[0](), NT) + dot(
                    out_ref[w, :, middle:], mix[1](), NT
                )
                rows = slice(w * length, (w + 1) * length)
                dprev[rows, :] = (gelu_slope(pre_ref[rows, :]) * dhid).astype(BF)

        by_core(own_m, other_m, turn)
        edge = dfirst.shape[1]
        for w in range(windows):
            dfirst[w] = dprev[w * length : w * length + edge, :]
            dlast[w] = dprev[(w + 1) * length - edge : (w + 1) * length, :]


def back_block(dpre, low, high, x, e, pieces, orders, dilate, previous=None):
    windows, length, width = x.shape
    flat, middle = dpre.shape
    chained = previous is not None
    operands = [dpre, low, high, x, e, *pieces]
    shapes = [jax.ShapeDtypeStruct(x.shape, BF)]
    if chained:
        others, pre, edge = previous
        operands += [*others, pre]
        shapes += [
            jax.ShapeDtypeStruct((flat, middle), BF),
            jax.ShapeDtypeStruct((windows, edge, middle), BF),
            jax.ShapeDtypeStruct((windows, edge, middle), BF),
        ]
    return pl.pallas_call(
        functools.partial(back_kernel, orders, dilate, chained),
        out_shape=tuple(shapes),
        in_specs=[VMEM] * len(operands),
        out_specs=(VMEM,) * len(shapes),
        scratch_shapes=[
            pltpu.VMEM((windows, length + 2 * dilate, middle), BF),
            pltpu.VMEM((windows, length, width), F32),
        ],
        compiler_params=params(),
        cost_estimate=cost(flat, width, middle),
        name="back_block",
    )(*operands)


def pack(conv, mix):
    middle = conv.shape[2]
    first = conv[:, :2].reshape(conv.shape[0], 2 * middle)
    tall = jnp.concatenate([mix[:, :middle], mix[:, middle:]], axis=0)
    second = jnp.concatenate([conv[:, 2], tall], axis=1)
    return first, second


def unpack(total, middle):
    rows = total.shape[0] // 2
    leading = lax.axis_index("dp") == 0
    got = cross(jnp.where(leading, total[rows:], total[:rows]))
    first = jnp.where(leading, total[:rows], got)
    second = jnp.where(leading, got, total[rows:])
    conv = jnp.concatenate(
        [first.reshape(rows, 2, middle), second[:, None, :middle]], axis=1
    )
    half = rows // 2
    mix = jnp.concatenate([second[:half, middle:], second[half:, middle:]], axis=1)
    return conv, mix


def body(activations, cotangent, conv_one, mix_one, conv_two, mix_two):
    count = lax.axis_size("seq")
    orders = step_orders(count)
    depth = len(orders[0])
    middle = conv_one.shape[2]
    length = activations.shape[1]
    leading = lax.axis_index("dp") == 0

    packed = [pack(conv_one, mix_one), pack(conv_two, mix_two)]
    mine = [jnp.where(leading, first, second) for first, second in packed]
    got = cross(jnp.stack([jnp.where(leading, second, first) for first, second in packed]))
    own_one, own_two = (
        jnp.where(
            leading,
            jnp.concatenate([mine[b], got[b]], axis=0),
            jnp.concatenate([got[b], mine[b]], axis=0),
        )[None]
        for b in range(2)
    )
    low, high = halo(
        activations[:, :DILATE_ONE], activations[:, length - DILATE_ONE :]
    )
    own_one = widen(own_one, orders, 0)
    ext_one = norm_ext(activations, low, high)
    own_one, own_two, ext_one = tie(own_one, own_two, ext_one)
    for j in range(1, depth):
        own_one, own_two = tie(widen(own_one, orders, j), widen(own_two, orders, j - 1))
    pieces_one = (own_one, cross(own_one))
    own_two = widen(own_two, orders, depth - 1)
    pre_one, hid_one, second_in, first, last = forward_block(
        ext_one, activations, pieces_one, orders, DILATE_ONE, DILATE_TWO
    )
    own_two, first, last = tie(own_two, first, last)
    low, high = halo(first, last)
    pieces_two = (own_two, cross(own_two))
    ext_two, hid_two, dpre_two, dfirst, dlast = turn_block(
        first, last, low, high, cotangent, pieces_two, orders, DILATE_TWO
    )
    dlow, dhigh = halo(dfirst, dlast)
    keep, send = grads_block(ext_two, hid_two, cotangent, dpre_two, orders, DILATE_TWO, count)
    dlow, dhigh, keep, send = tie(dlow, dhigh, keep, send)
    total_two = keep + cross(send).astype(F32)
    total_two, dlow, dhigh = tie(total_two, dlow, dhigh)
    upstream, dpre_one, dfirst, dlast = back_block(
        dpre_two, dlow, dhigh, second_in, cotangent, pieces_two, orders, DILATE_TWO,
        (pieces_one, pre_one, DILATE_ONE),
    )
    dlow, dhigh = halo(dfirst, dlast)
    keep, send = grads_block(ext_one, hid_one, upstream, dpre_one, orders, DILATE_ONE, count)
    total_two = fold(total_two, orders, depth - 1)
    total_two, keep, send, dlow, dhigh = tie(total_two, keep, send, dlow, dhigh)
    total_one = keep + cross(send).astype(F32)
    (input_grad,) = back_block(
        dpre_one, dlow, dhigh, activations, upstream, pieces_one, orders, DILATE_ONE
    )
    for j in reversed(range(depth - 1)):
        total_two = fold(total_two, orders, j)
    for j in reversed(range(depth)):
        total_one = fold(total_one, orders, j)
    return (input_grad, *unpack(total_one[0], middle), *unpack(total_two[0], middle))


def solution(mesh):
    in_specs = (
        P(("parts", "dp"), "seq", None),
        P(("parts", "dp"), "seq", None),
        P(("seq", "dp"), None, None),
        P(("seq", "dp"), None),
        P(("seq", "dp"), None, None),
        P(("seq", "dp"), None),
    )
    out_specs = (
        P(("parts", "dp"), "seq", None),
        P(("parts", "seq", "dp"), None, None),
        P(("parts", "seq", "dp"), None),
        P(("parts", "seq", "dp"), None, None),
        P(("parts", "seq", "dp"), None),
    )
    return jax.shard_map(body, mesh=mesh, in_specs=in_specs, out_specs=out_specs, check_vma=False)
```

time: 273 us -> 232 us (0.85)
  Pallas kernels: 62 us -> 33.2 us
  starting transfers between devices: 64.3 us -> 54.6 us
  local copies, waits for them, and re-layouts: 11.3 us -> 8.39 us
    pallas_call x2, Pallas kernels: 30 us -> 14.7 us  [back_block(): pl.pallas_call(functools.partial(back_kernel, orders, dilate, chained), o...]
    ppermute x32 -> x19, starting transfers between devices: 37.6 us -> 31.5 us  [the longest x12 21 us: hop(): return lax.ppermute(value, ('seq', 'dp'), pairs)]
    pallas_call x1, Pallas kernels: 11.2 us -> 5.11 us  [forward_block(): pl.pallas_call(functools.partial(forward_kernel, orders, dilate, edge), o...]
    pallas_call x1, Pallas kernels: 8.45 us -> 2.96 us  [turn_block(): pl.pallas_call(functools.partial(turn_kernel, orders, dilate), out_shape=...]
    ppermute x4, waiting for transfers between devices: 27.3 us -> 23.7 us  [halo(): low = lax.ppermute(last, 'seq', [(i, i + 1) for i in range(count - 1)])]
    ppermute x4, starting transfers between devices: 21.1 us -> 17.8 us  [halo(): low = lax.ppermute(last, 'seq', [(i, i + 1) for i in range(count - 1)])]
    ppermute x32 -> x19, waiting for transfers between devices: 85.8 us -> 88.5 us  [the longest x12 80.1 us: hop(): return lax.ppermute(value, ('seq', 'dp'), pairs)]
  transfers between devices with their start and end apart: 40 -> 27, of which waited for: 22 -> 15; matrix products, arithmetic and copies ran while one was open for 5% -> 2% of each run, Pallas kernels for 18% -> 11%
where the time goes in v2:
time: 232 us; the launch traced here: 231 us
  waiting for transfers between devices  125 us (54%)
  starting transfers between devices  54.6 us (24%)
  Pallas kernels  33.2 us (14%)
  other arithmetic  8.43 us (4%)
  local copies, waits for them, and re-layouts  8.39 us (4%)
    ppermute x12, waiting for transfers between devices, hop(): return lax.ppermute(value, ('seq', 'dp'), pairs)  80.1 us
    ppermute x4, waiting for transfers between devices, halo(): low = lax.ppermute(last, 'seq', [(i, i + 1) for i in range(count - 1)])  23.7 us
    ppermute x12, starting transfers between devices, hop(): return lax.ppermute(value, ('seq', 'dp'), pairs)  21 us
    ppermute x4, starting transfers between devices, halo(): low = lax.ppermute(last, 'seq', [(i, i + 1) for i in range(count - 1)])  17.8 us
    pallas_call x2, Pallas kernels, back_block(): pl.pallas_call(functools.partial(back_kernel, orders, dilate, chained), o...  14.7 us
    ppermute x4, waiting for transfers between devices, halo(): high = lax.ppermute(first, 'seq', [(i + 1, i) for i in range(count - 1)])  13.1 us
    ppermute x7, starting transfers between devices, cross(): return lax.ppermute(value, 'dp', [(0, 1), (1, 0)])  10.5 us
    ppermute x7, waiting for transfers between devices, cross(): return lax.ppermute(value, 'dp', [(0, 1), (1, 0)])  8.35 us
  transfers between devices with their start and end apart: 27, of which 15 were waited for; matrix products, arithmetic and copies ran while one was open for 2% of the time, Pallas kernels for 11%

profile of v2, /device:TPU:0, one launch (start us, length us, event | category | flops | bytes accessed | tf_op | source)
XLA Modules:
  0.0 231.2 jit_solution(11456406950793659747)
XLA Ops:
  8.3 5.1 %collective-permute-start.2 = (bf16[2,64,1024]{2,1,0:T(8,128)(2,1)S(1)}, bf16[2,64,1024]{2,1,0:T(8,128)(2,1)S(1)}, u32[]{:S(2)}, u32[]{:S(2)}) collective-permute-start(bf16[2,64,1024]{2,1,0:T(8,128)(2,1)S(1)} %get-tuple-element.86), channel_id=1, source_target_pairs={{0,2},{2,4},{4,6},{6,8},{8,10},{10,12},{12,14},{1,3},{3,5},{5,7},{... | collective-permute-start | bytes 786440 | tf_op jit(solution)/shard_map/ppermute | solution.py:92
  13.6 3.1 %collective-permute-start.1 = (bf16[1,128,1024]{2,1,0:T(8,128)(2,1)S(1)}, bf16[1,128,1024]{2,1,0:T(8,128)(2,1)S(1)}, u32[]{:S(2)}, u32[]{:S(2)}) collective-permute-start(bf16[1,128,1024]{2,1,0:T(8,128)(2,1)S(1)} %maximum_select_fusion), channel_id=1, source_target_pairs={{0,8},{1,3},{2,10},{3,1},{4,12},{5,7},{6,14},{7,5},{8,0},{9,11},{1... | collective-permute-start | bytes 786440 | tf_op jit(solution)/shard_map/ppermute | solution.py:78
  18.6 5.6 %collective-permute-done.2.low_ref = bf16[2,64,1024]{2,1,0:T(8,128)(2,1)S(1)} collective-permute-done((bf16[2,64,1024]{2,1,0:T(8,128)(2,1)S(1)}, bf16[2,64,1024]{2,1,0:T(8,128)(2,1)S(1)}, u32[]{:S(2)}, u32[]{:S(2)}) %collective-permute-start.2) | collective-permute-done | bytes 262176 | tf_op jit(solution)/shard_map/ppermute | solution.py:92
  24.2 3.6 %norm_ext.1.ext = bf16[2,384,1024]{2,1,0:T(8,128)(2,1)S(1)} custom-call(bf16[2,256,1024]{2,1,0:T(8,128)(2,1)S(1)} %copy-done, bf16[2,64,1024]{2,1,0:T(8,128)(2,1)S(1)} %collective-permute-done.2.low_ref, bf16[2,64,1024]{2,1,0:T(8,128)(2,1)S(1)} %collective-permute-done.3.high_ref), custom_call_target="tpu_custom_call" | custom-call | tf_op jit(solution)/shard_map/norm_ext/pallas_call | solution.py:162
  30.1 2.6 %collective-permute-start.5 = (bf16[1,128,1024]{2,1,0:T(8,128)(2,1)S(1)}, bf16[1,128,1024]{2,1,0:T(8,128)(2,1)S(1)}, u32[]{:S(2)}, u32[]{:S(2)}) collective-permute-start(bf16[1,128,1024]{2,1,0:T(8,128)(2,1)S(1)} %maximum_select_fusion.1), channel_id=1, source_target_pairs={{0,8},{1,3},{2,10},{3,1},{4,12},{5,7},{6,14},{7,5},{8,0},{9,11},{1... | collective-permute-start | bytes 786440 | tf_op jit(solution)/shard_map/ppermute | solution.py:78
  32.7 14.1 %collective-permute-done.5 = bf16[1,128,1024]{2,1,0:T(8,128)(2,1)S(1)} collective-permute-done((bf16[1,128,1024]{2,1,0:T(8,128)(2,1)S(1)}, bf16[1,128,1024]{2,1,0:T(8,128)(2,1)S(1)}, u32[]{:S(2)}, u32[]{:S(2)}) %collective-permute-start.5) | collective-permute-done | bytes 262176 | tf_op jit(solution)/shard_map/ppermute | solution.py:78
  46.9 2.7 %collective-permute-start.6 = (bf16[4,128,1024]{2,1,0:T(8,128)(2,1)S(1)}, bf16[4,128,1024]{2,1,0:T(8,128)(2,1)S(1)}, u32[]{:S(2)}, u32[]{:S(2)}) collective-permute-start(bf16[4,128,1024]{2,1,0:T(8,128)(2,1)S(1)} %pad_maximum_fusion.2), channel_id=1, source_target_pairs={{0,2},{1,5},{2,0},{3,7},{4,6},{5,1},{6,4},{7,3},{8,10},{9,13},{10,... | collective-permute-start | bytes 3145736 | tf_op jit(solution)/shard_map/ppermute | solution.py:78
  50.0 19.8 %collective-permute-done.7 = bf16[2,128,1024]{2,1,0:T(8,128)(2,1)S(1)} collective-permute-done((bf16[2,128,1024]{2,1,0:T(8,128)(2,1)S(1)}, bf16[2,128,1024]{2,1,0:T(8,128)(2,1)S(1)}, u32[]{:S(2)}, u32[]{:S(2)}) %collective-permute-start.7) | collective-permute-done | bytes 524320 | tf_op jit(solution)/shard_map/ppermute | solution.py:78
  70.2 3.4 %collective-permute-start.9 = (bf16[8,128,1024]{2,1,0:T(8,128)(2,1)S(1)}, bf16[8,128,1024]{2,1,0:T(8,128)(2,1)S(1)}, u32[]{:S(2)}, u32[]{:S(2)}) collective-permute-start(bf16[8,128,1024]{2,1,0:T(8,128)(2,1)S(1)} %pad_maximum_fusion.own.refs_7_.refs_5_), channel_id=1, source_target_pairs={{0,1},{1,0},{2,3},{3,2},{4,5},{5,4},{6,7},{7,6},{8,9},{9,8},{10,11... | collective-permute-start | bytes 6291464 | tf_op jit(solution)/shard_map/ppermute | solution.py:68
  73.6 2.3 collective-permute-start.8
  75.8 12.8 %collective-permute-done.8 = bf16[4,128,1024]{2,1,0:T(8,128)(2,1)S(1)} collective-permute-done((bf16[4,128,1024]{2,1,0:T(8,128)(2,1)S(1)}, bf16[4,128,1024]{2,1,0:T(8,128)(2,1)S(1)}, u32[]{:S(2)}, u32[]{:S(2)}) %collective-permute-start.8) | collective-permute-done | bytes 1048608 | tf_op jit(solution)/shard_map/ppermute | solution.py:78
  88.8 5.1 %forward_block.1 = (f32[512,512]{1,0:T(8,128)S(1)}, bf16[512,512]{1,0:T(8,128)(2,1)S(1)}, bf16[2,256,1024]{2,1,0:T(8,128)(2,1)S(1)}, bf16[2,128,1024]{2,1,0:T(8,128)(2,1)S(1)}, bf16[2,128,1024]{2,1,0:T(8,128)(2,1)S(1)}) custom-call(bf16[2,384,1024]{2,1,0:T(8,128)(2,1)S(1)} %norm_ext.1.ext, bf16[2,256,1024]{2,1,0:T(8,128)(2,1)S(1)} %copy-done, ...), custom_call_target="tpu_custom_call" | custom-call | flops 2147483648 | bytes 8388608 | tf_op jit(solution)/shard_map/forward_block/pallas_call | solution.py:206
  96.2 4.6 %collective-permute-start.10 = (bf16[2,128,1024]{2,1,0:T(8,128)(2,1)S(1)}, bf16[2,128,1024]{2,1,0:T(8,128)(2,1)S(1)}, u32[]{:S(2)}, u32[]{:S(2)}) collective-permute-start(bf16[2,128,1024]{2,1,0:T(8,128)(2,1)S(1)} %get-tuple-element.55.last), channel_id=1, source_target_pairs={{0,2},{2,4},{4,6},{6,8},{8,10},{10,12},{12,14},{1,3},{3,5},{5,7},{... | collective-permute-start | bytes 1572872 | tf_op jit(solution)/shard_map/ppermute | solution.py:92
  100.8 10.6 %collective-permute-done.11.high = bf16[2,128,1024]{2,1,0:T(8,128)(2,1)S(1)} collective-permute-done((bf16[2,128,1024]{2,1,0:T(8,128)(2,1)S(1)}, bf16[2,128,1024]{2,1,0:T(8,128)(2,1)S(1)}, u32[]{:S(2)}, u32[]{:S(2)}) %collective-permute-start.11) | collective-permute-done | bytes 524320 | tf_op jit(solution)/shard_map/ppermute | solution.py:93
  111.4 11.4 %collective-permute-done.10.low = bf16[2,128,1024]{2,1,0:T(8,128)(2,1)S(1)} collective-permute-done((bf16[2,128,1024]{2,1,0:T(8,128)(2,1)S(1)}, bf16[2,128,1024]{2,1,0:T(8,128)(2,1)S(1)}, u32[]{:S(2)}, u32[]{:S(2)}) %collective-permute-start.10) | collective-permute-done | bytes 524320 | tf_op jit(solution)/shard_map/ppermute | solution.py:92
  122.9 3.0 %turn_block.1 = (bf16[2,512,1024]{2,1,0:T(8,128)(2,1)S(1)}, bf16[512,512]{1,0:T(8,128)(2,1)S(1)}, bf16[512,512]{1,0:T(8,128)(2,1)S(1)}, bf16[2,128,512]{2,1,0:T(8,128)(2,1)S(1)}, bf16[2,128,512]{2,1,0:T(8,128)(2,1)S(1)}) custom-call(bf16[2,128,1024]{2,1,0:T(8,128)(2,1)S(1)} %get-tuple-element.54.first, bf16[2,128,1024]{2,1,0:T(8,128)(2,1)S(1)} %get-tuple-element.55.last, ...), custom_call_target="tpu_custom_call" | custom-call | flops 2147483648 | bytes 8388608 | tf_op jit(solution)/shard_map/turn_block/pallas_call | solution.py:256
  125.8 4.4 %collective-permute-start.13 = (bf16[2,128,512]{2,1,0:T(8,128)(2,1)S(1)}, bf16[2,128,512]{2,1,0:T(8,128)(2,1)S(1)}, u32[]{:S(2)}, u32[]{:S(2)}) collective-permute-start(bf16[2,128,512]{2,1,0:T(8,128)(2,1)S(1)} %get-tuple-element.58), channel_id=1, source_target_pairs={{0,2},{2,4},{4,6},{6,8},{8,10},{10,12},{12,14},{1,3},{3,5},{5,7},{... | collective-permute-start | bytes 786440 | tf_op jit(solution)/shard_map/ppermute | solution.py:92
  131.5 3.4 %grads_block.2 = (f32[8,128,1024]{2,1,0:T(8,128)S(1)}, bf16[8,128,1024]{2,1,0:T(8,128)(2,1)S(1)}) custom-call(bf16[2,512,1024]{2,1,0:T(8,128)(2,1)S(1)} %get-tuple-element.60.ext, bf16[512,512]{1,0:T(8,128)(2,1)S(1)} %get-tuple-element.61.hid, bf16[2,256,1024]{2,1,0:T(8,128)(2,1)S(1)} %copy-done.3, bf16[512,512]{1,0:T(8,128)(2,1)S(1)} %get-tuple-element.57.dpre.refs_0_), custom_call_target="tpu_custom_call" | custom-call | flops 2147483648 | bytes 8388608 | tf_op jit(solution)/shard_map/grads_block/pallas_call | solution.py:322
  135.0 6.7 %collective-permute-done.13.refs_1_ = bf16[2,128,512]{2,1,0:T(8,128)(2,1)S(1)} collective-permute-done((bf16[2,128,512]{2,1,0:T(8,128)(2,1)S(1)}, bf16[2,128,512]{2,1,0:T(8,128)(2,1)S(1)}, u32[]{:S(2)}, u32[]{:S(2)}) %collective-permute-start.13) | collective-permute-done | bytes 262176 | tf_op jit(solution)/shard_map/ppermute | solution.py:92
  141.6 4.2 %collective-permute-done.15 = bf16[8,128,1024]{2,1,0:T(8,128)(2,1)S(1)} collective-permute-done((bf16[8,128,1024]{2,1,0:T(8,128)(2,1)S(1)}, bf16[8,128,1024]{2,1,0:T(8,128)(2,1)S(1)}, u32[]{:S(2)}, u32[]{:S(2)}) %collective-permute-start.15) | collective-permute-done | bytes 2097184 | tf_op jit(solution)/shard_map/ppermute | solution.py:68
  148.1 2.5 %collective-permute-start.16 = (bf16[4,128,1024]{2,1,0:T(8,128)(2,1)}, bf16[4,128,1024]{2,1,0:T(8,128)(2,1)}, u32[]{:S(2)}, u32[]{:S(2)}) collective-permute-start(bf16[4,128,1024]{2,1,0:T(8,128)(2,1)} %slice.227), channel_id=1, source_target_pairs={{0,2},{1,5},{2,0},{3,7},{4,6},{5,1},{6,4},{7,3},{8,10},{9,13},{10,... | collective-permute-start | bytes 3145736 | tf_op jit(solution)/shard_map/ppermute | solution.py:78
  150.6 7.4 %back_block.2 = (bf16[2,256,1024]{2,1,0:T(8,128)(2,1)S(1)}, bf16[512,512]{1,0:T(8,128)(2,1)S(1)}, bf16[2,64,512]{2,1,0:T(8,128)(2,1)S(1)}, bf16[2,64,512]{2,1,0:T(8,128)(2,1)S(1)}) custom-call(bf16[512,512]{1,0:T(8,128)(2,1)S(1)} %get-tuple-element.57.dpre.refs_0_, bf16[2,128,512]{2,1,0:T(8,128)(2,1)S(1)} %collective-permute-done.13.refs_1_, ...), custom_call_target="tpu_custom_call" | custom-call | flops 2147483648 | bytes 8388608 | tf_op jit(solution)/shard_map/back_block/pallas_call | solution.py:400
  158.1 3.7 %collective-permute-start.17 = (bf16[2,64,512]{2,1,0:T(8,128)(2,1)S(1)}, bf16[2,64,512]{2,1,0:T(8,128)(2,1)S(1)}, u32[]{:S(2)}, u32[]{:S(2)}) collective-permute-start(bf16[2,64,512]{2,1,0:T(8,128)(2,1)S(1)} %get-tuple-element.78), channel_id=1, source_target_pairs={{0,2},{2,4},{4,6},{6,8},{8,10},{10,12},{12,14},{1,3},{3,5},{5,7},{... | collective-permute-start | bytes 393224 | tf_op jit(solution)/shard_map/ppermute | solution.py:92
  163.3 3.4 %grads_block.3 = (f32[8,128,1024]{2,1,0:T(8,128)S(1)}, bf16[8,128,1024]{2,1,0:T(8,128)(2,1)S(1)}) custom-call(bf16[2,384,1024]{2,1,0:T(8,128)(2,1)S(1)} %copy-done.2, bf16[512,512]{1,0:T(8,128)(2,1)S(1)} %copy-done.10, bf16[2,256,1024]{2,1,0:T(8,128)(2,1)S(1)} %get-tuple-element.75.e_ref.refs_4_, bf16[512,512]{1,0:T(8,128)(2,1)S(1)} %get-tuple-element.72.dpre.refs_0_), custom_call_target="tpu_custom_call" | custom-call | flops 2147483648 | bytes 8388608 | tf_op jit(solution)/shard_map/grads_block/pallas_call | solution.py:322
  168.9 4.2 %collective-permute-done.19 = bf16[8,128,1024]{2,1,0:T(8,128)(2,1)S(1)} collective-permute-done((bf16[8,128,1024]{2,1,0:T(8,128)(2,1)S(1)}, bf16[8,128,1024]{2,1,0:T(8,128)(2,1)S(1)}, u32[]{:S(2)}, u32[]{:S(2)}) %collective-permute-start.19) | collective-permute-done | bytes 2097184 | tf_op jit(solution)/shard_map/ppermute | solution.py:68
  174.3 2.3 %collective-permute-start.20 = (bf16[4,128,1024]{2,1,0:T(8,128)(2,1)S(1)}, bf16[4,128,1024]{2,1,0:T(8,128)(2,1)S(1)}, u32[]{:S(2)}, u32[]{:S(2)}) collective-permute-start(bf16[4,128,1024]{2,1,0:T(8,128)(2,1)S(1)} %slice.226), channel_id=1, source_target_pairs={{0,2},{1,5},{2,0},{3,7},{4,6},{5,1},{6,4},{7,3},{8,10},{9,13},{10,... | collective-permute-start | bytes 3145736 | tf_op jit(solution)/shard_map/ppermute | solution.py:78
  177.3 20.0 %collective-permute-done.24 = bf16[2,128,1024]{2,1,0:T(8,128)(2,1)S(1)} collective-permute-done((bf16[2,128,1024]{2,1,0:T(8,128)(2,1)S(1)}, bf16[2,128,1024]{2,1,0:T(8,128)(2,1)S(1)}, u32[]{:S(2)}, u32[]{:S(2)}) %collective-permute-start.24) | collective-permute-done | bytes 524320 | tf_op jit(solution)/shard_map/ppermute | solution.py:78
  200.1 7.2 %back_block.3 = bf16[2,256,1024]{2,1,0:T(8,128)(2,1)} custom-call(bf16[512,512]{1,0:T(8,128)(2,1)S(1)} %get-tuple-element.72.dpre.refs_0_, bf16[2,64,512]{2,1,0:T(8,128)(2,1)S(1)} %collective-permute-done.17.refs_1_, bf16[2,64,512]{2,1,0:T(8,128)(2,1)S(1)} %collective-permute-done.18.refs_2_, bf16[2,256,1024]{2,1,0:T(8,128)(2,1)S(1)} %copy-done, ...), custom_call_target="tpu_custom_call" | custom-call | flops 2147483648 | bytes 8388608 | tf_op jit(solution)/shard_map/back_block/pallas_call | solution.py:400
  207.3 2.2 collective-permute-done.25
  209.6 2.9 %collective-permute-start.26 = (f32[64,1024]{1,0:T(8,128)S(1)}, f32[64,1024]{1,0:T(8,128)S(1)}, u32[]{:S(2)}, u32[]{:S(2)}) collective-permute-start(f32[64,1024]{1,0:T(8,128)S(1)} %fusion.4), channel_id=1, source_target_pairs={{0,1},{1,0},{2,3},{3,2},{4,5},{5,4},{6,7},{7,6},{8,9},{9,8},{10,11... | collective-permute-start | bytes 786440 | tf_op jit(solution)/shard_map/ppermute | solution.py:68
  213.7 10.6 %collective-permute-done.22 = bf16[1,128,1024]{2,1,0:T(8,128)(2,1)S(1)} collective-permute-done((bf16[1,128,1024]{2,1,0:T(8,128)(2,1)S(1)}, bf16[1,128,1024]{2,1,0:T(8,128)(2,1)S(1)}, u32[]{:S(2)}, u32[]{:S(2)}) %collective-permute-start.22) | collective-permute-done | bytes 262176 | tf_op jit(solution)/shard_map/ppermute | solution.py:78
  224.4 3.7 %collective-permute-start.23 = (f32[64,1024]{1,0:T(8,128)S(1)}, f32[64,1024]{1,0:T(8,128)S(1)}, u32[]{:S(2)}, u32[]{:S(2)}) collective-permute-start(f32[64,1024]{1,0:T(8,128)S(1)} %fusion.1), channel_id=1, source_target_pairs={{0,1},{1,0},{2,3},{3,2},{4,5},{5,4},{6,7},{7,6},{8,9},{9,8},{10,11... | collective-permute-start | bytes 786440 | tf_op jit(solution)/shard_map/ppermute | solution.py:68
  (111 shorter events, 31.2 us)
Async XLA Ops:
  6.4 7.0 %collective-permute-start = (bf16[2,64,1024]{2,1,0:T(8,128)(2,1)S(1)}, bf16[2,64,1024]{2,1,0:T(8,128)(2,1)S(1)}, u32[]{:S(2)}, u32[]{:S(2)}) collective-permute-start(bf16[2,64,1024]{2,1,0:T(8,128)(2,1)S(1)} %pad_maximum_fusion.8), channel_id=1, source_target_pairs={{0,1},{1,0},{2,3},{3,2},{4,5},{5,4},{6,7},{7,6},{8,9},{9,8},{10,11... | collective-permute-start | bytes 786440 | tf_op jit(solution)/shard_map/ppermute | solution.py:68
  7.0 11.6 %collective-permute-start.3 = (bf16[2,64,1024]{2,1,0:T(8,128)(2,1)S(1)}, bf16[2,64,1024]{2,1,0:T(8,128)(2,1)S(1)}, u32[]{:S(2)}, u32[]{:S(2)}) collective-permute-start(bf16[2,64,1024]{2,1,0:T(8,128)(2,1)S(1)} %get-tuple-element.85), channel_id=1, source_target_pairs={{2,0},{4,2},{6,4},{8,6},{10,8},{12,10},{14,12},{3,1},{5,3},{7,5},{... | collective-permute-start | bytes 786440 | tf_op jit(solution)/shard_map/ppermute | solution.py:93
  8.3 15.9 %collective-permute-start.2 = (bf16[2,64,1024]{2,1,0:T(8,128)(2,1)S(1)}, bf16[2,64,1024]{2,1,0:T(8,128)(2,1)S(1)}, u32[]{:S(2)}, u32[]{:S(2)}) collective-permute-start(bf16[2,64,1024]{2,1,0:T(8,128)(2,1)S(1)} %get-tuple-element.86), channel_id=1, source_target_pairs={{0,2},{2,4},{4,6},{6,8},{8,10},{10,12},{12,14},{1,3},{3,5},{5,7},{... | collective-permute-start | bytes 786440 | tf_op jit(solution)/shard_map/ppermute | solution.py:92
  13.6 14.4 %collective-permute-start.1 = (bf16[1,128,1024]{2,1,0:T(8,128)(2,1)S(1)}, bf16[1,128,1024]{2,1,0:T(8,128)(2,1)S(1)}, u32[]{:S(2)}, u32[]{:S(2)}) collective-permute-start(bf16[1,128,1024]{2,1,0:T(8,128)(2,1)S(1)} %maximum_select_fusion), channel_id=1, source_target_pairs={{0,8},{1,3},{2,10},{3,1},{4,12},{5,7},{6,14},{7,5},{8,0},{9,11},{1... | collective-permute-start | bytes 786440 | tf_op jit(solution)/shard_map/ppermute | solution.py:78
  27.9 61.0 %copy-start.1 = (bf16[2,384,1024]{2,1,0:T(8,128)(2,1)}, bf16[2,384,1024]{2,1,0:T(8,128)(2,1)S(1)}, u32[]{:S(2)}) copy-start(bf16[2,384,1024]{2,1,0:T(8,128)(2,1)S(1)} %norm_ext.1.ext) | copy-start | bytes 4718596
  28.0 18.8 %collective-permute-start.4 = (bf16[2,128,1024]{2,1,0:T(8,128)(2,1)S(1)}, bf16[2,128,1024]{2,1,0:T(8,128)(2,1)S(1)}, u32[]{:S(2)}, u32[]{:S(2)}) collective-permute-start(bf16[2,128,1024]{2,1,0:T(8,128)(2,1)S(1)} %pad_maximum_fusion.4), channel_id=1, source_target_pairs={{0,4},{1,9},{2,6},{3,11},{4,0},{5,13},{6,2},{7,15},{8,12},{9,1},{1... | collective-permute-start | bytes 1572872 | tf_op jit(solution)/shard_map/ppermute | solution.py:78
  30.1 16.7 %collective-permute-start.5 = (bf16[1,128,1024]{2,1,0:T(8,128)(2,1)S(1)}, bf16[1,128,1024]{2,1,0:T(8,128)(2,1)S(1)}, u32[]{:S(2)}, u32[]{:S(2)}) collective-permute-start(bf16[1,128,1024]{2,1,0:T(8,128)(2,1)S(1)} %maximum_select_fusion.1), channel_id=1, source_target_pairs={{0,8},{1,3},{2,10},{3,1},{4,12},{5,7},{6,14},{7,5},{8,0},{9,11},{1... | collective-permute-start | bytes 786440 | tf_op jit(solution)/shard_map/ppermute | solution.py:78
  46.9 23.0 %collective-permute-start.6 = (bf16[4,128,1024]{2,1,0:T(8,128)(2,1)S(1)}, bf16[4,128,1024]{2,1,0:T(8,128)(2,1)S(1)}, u32[]{:S(2)}, u32[]{:S(2)}) collective-permute-start(bf16[4,128,1024]{2,1,0:T(8,128)(2,1)S(1)} %pad_maximum_fusion.2), channel_id=1, source_target_pairs={{0,2},{1,5},{2,0},{3,7},{4,6},{5,1},{6,4},{7,3},{8,10},{9,13},{10,... | collective-permute-start | bytes 3145736 | tf_op jit(solution)/shard_map/ppermute | solution.py:78
  49.7 20.2 %collective-permute-start.7 = (bf16[2,128,1024]{2,1,0:T(8,128)(2,1)S(1)}, bf16[2,128,1024]{2,1,0:T(8,128)(2,1)S(1)}, u32[]{:S(2)}, u32[]{:S(2)}) collective-permute-start(bf16[2,128,1024]{2,1,0:T(8,128)(2,1)S(1)} %pad_maximum_fusion.5), channel_id=1, source_target_pairs={{0,4},{1,9},{2,6},{3,11},{4,0},{5,13},{6,2},{7,15},{8,12},{9,1},{1... | collective-permute-start | bytes 1572872 | tf_op jit(solution)/shard_map/ppermute | solution.py:78
  70.2 18.6 %collective-permute-start.9 = (bf16[8,128,1024]{2,1,0:T(8,128)(2,1)S(1)}, bf16[8,128,1024]{2,1,0:T(8,128)(2,1)S(1)}, u32[]{:S(2)}, u32[]{:S(2)}) collective-permute-start(bf16[8,128,1024]{2,1,0:T(8,128)(2,1)S(1)} %pad_maximum_fusion.own.refs_7_.refs_5_), channel_id=1, source_target_pairs={{0,1},{1,0},{2,3},{3,2},{4,5},{5,4},{6,7},{7,6},{8,9},{9,8},{10,11... | collective-permute-start | bytes 6291464 | tf_op jit(solution)/shard_map/ppermute | solution.py:68
  73.6 15.1 %collective-permute-start.8 = (bf16[4,128,1024]{2,1,0:T(8,128)(2,1)S(1)}, bf16[4,128,1024]{2,1,0:T(8,128)(2,1)S(1)}, u32[]{:S(2)}, u32[]{:S(2)}) collective-permute-start(bf16[4,128,1024]{2,1,0:T(8,128)(2,1)S(1)} %pad_maximum_fusion.3), channel_id=1, source_target_pairs={{0,2},{1,5},{2,0},{3,7},{4,6},{5,1},{6,4},{7,3},{8,10},{9,13},{10,... | collective-permute-start | bytes 3145736 | tf_op jit(solution)/shard_map/ppermute | solution.py:78
  88.8 34.0 %copy-start.3 = (bf16[2,256,1024]{2,1,0:T(8,128)(2,1)S(1)}, bf16[2,256,1024]{2,1,0:T(8,128)(2,1)}, u32[]{:S(2)}) copy-start(bf16[2,256,1024]{2,1,0:T(8,128)(2,1)} %refs_4_.1) | copy-start | bytes 3145732
  94.9 30.9 %copy-start.5 = (f32[512,512]{1,0:T(8,128)}, f32[512,512]{1,0:T(8,128)S(1)}, u32[]{:S(2)}) copy-start(f32[512,512]{1,0:T(8,128)S(1)} %get-tuple-element.71.refs_9_) | copy-start | bytes 3145732
  94.9 30.9 %copy-start.9 = (bf16[512,512]{1,0:T(8,128)(2,1)}, bf16[512,512]{1,0:T(8,128)(2,1)S(1)}, u32[]{:S(2)}) copy-start(bf16[512,512]{1,0:T(8,128)(2,1)S(1)} %get-tuple-element.74.hid) | copy-start | bytes 1572868
  94.9 27.9 %collective-permute-start.12 = (bf16[8,128,1024]{2,1,0:T(8,128)(2,1)S(1)}, bf16[8,128,1024]{2,1,0:T(8,128)(2,1)S(1)}, u32[]{:S(2)}, u32[]{:S(2)}) collective-permute-start(bf16[8,128,1024]{2,1,0:T(8,128)(2,1)S(1)} %pad_maximum_fusion.1.own.refs_5_), channel_id=1, source_target_pairs={{0,1},{1,0},{2,3},{3,2},{4,5},{5,4},{6,7},{7,6},{8,9},{9,8},{10,11... | collective-permute-start | bytes 6291464 | tf_op jit(solution)/shard_map/ppermute | solution.py:68
  94.9 16.5 %collective-permute-start.11 = (bf16[2,128,1024]{2,1,0:T(8,128)(2,1)S(1)}, bf16[2,128,1024]{2,1,0:T(8,128)(2,1)S(1)}, u32[]{:S(2)}, u32[]{:S(2)}) collective-permute-start(bf16[2,128,1024]{2,1,0:T(8,128)(2,1)S(1)} %get-tuple-element.54.first), channel_id=1, source_target_pairs={{2,0},{4,2},{6,4},{8,6},{10,8},{12,10},{14,12},{3,1},{5,3},{7,5},{... | collective-permute-start | bytes 1572872 | tf_op jit(solution)/shard_map/ppermute | solution.py:93
  96.2 26.6 %collective-permute-start.10 = (bf16[2,128,1024]{2,1,0:T(8,128)(2,1)S(1)}, bf16[2,128,1024]{2,1,0:T(8,128)(2,1)S(1)}, u32[]{:S(2)}, u32[]{:S(2)}) collective-permute-start(bf16[2,128,1024]{2,1,0:T(8,128)(2,1)S(1)} %get-tuple-element.55.last), channel_id=1, source_target_pairs={{0,2},{2,4},{4,6},{6,8},{8,10},{10,12},{12,14},{1,3},{3,5},{5,7},{... | collective-permute-start | bytes 1572872 | tf_op jit(solution)/shard_map/ppermute | solution.py:92
  125.8 15.8 %collective-permute-start.13 = (bf16[2,128,512]{2,1,0:T(8,128)(2,1)S(1)}, bf16[2,128,512]{2,1,0:T(8,128)(2,1)S(1)}, u32[]{:S(2)}, u32[]{:S(2)}) collective-permute-start(bf16[2,128,512]{2,1,0:T(8,128)(2,1)S(1)} %get-tuple-element.58), channel_id=1, source_target_pairs={{0,2},{2,4},{4,6},{6,8},{8,10},{10,12},{12,14},{1,3},{3,5},{5,7},{... | collective-permute-start | bytes 786440 | tf_op jit(solution)/shard_map/ppermute | solution.py:92
  130.2 11.4 %collective-permute-start.14 = (bf16[2,128,512]{2,1,0:T(8,128)(2,1)S(1)}, bf16[2,128,512]{2,1,0:T(8,128)(2,1)S(1)}, u32[]{:S(2)}, u32[]{:S(2)}) collective-permute-start(bf16[2,128,512]{2,1,0:T(8,128)(2,1)S(1)} %get-tuple-element.59), channel_id=1, source_target_pairs={{2,0},{4,2},{6,4},{8,6},{10,8},{12,10},{14,12},{3,1},{5,3},{7,5},{... | collective-permute-start | bytes 786440 | tf_op jit(solution)/shard_map/ppermute | solution.py:93
  141.6 4.2 %collective-permute-start.15 = (bf16[8,128,1024]{2,1,0:T(8,128)(2,1)S(1)}, bf16[8,128,1024]{2,1,0:T(8,128)(2,1)S(1)}, u32[]{:S(2)}, u32[]{:S(2)}) collective-permute-start(bf16[8,128,1024]{2,1,0:T(8,128)(2,1)S(1)} %get-tuple-element.65), channel_id=1, source_target_pairs={{0,1},{1,0},{2,3},{3,2},{4,5},{5,4},{6,7},{7,6},{8,9},{9,8},{10,11... | collective-permute-start | bytes 6291464 | tf_op jit(solution)/shard_map/ppermute | solution.py:68
  148.1 18.7 %collective-permute-start.16 = (bf16[4,128,1024]{2,1,0:T(8,128)(2,1)}, bf16[4,128,1024]{2,1,0:T(8,128)(2,1)}, u32[]{:S(2)}, u32[]{:S(2)}) collective-permute-start(bf16[4,128,1024]{2,1,0:T(8,128)(2,1)} %slice.227), channel_id=1, source_target_pairs={{0,2},{1,5},{2,0},{3,7},{4,6},{5,1},{6,4},{7,3},{8,10},{9,13},{10,... | collective-permute-start | bytes 3145736 | tf_op jit(solution)/shard_map/ppermute | solution.py:78
  150.6 12.7 %copy-start.2 = (bf16[2,384,1024]{2,1,0:T(8,128)(2,1)S(1)}, bf16[2,384,1024]{2,1,0:T(8,128)(2,1)}, u32[]{:S(2)}) copy-start(bf16[2,384,1024]{2,1,0:T(8,128)(2,1)} %copy-done.1) | copy-start | bytes 4718596
  158.1 10.3 %collective-permute-start.17 = (bf16[2,64,512]{2,1,0:T(8,128)(2,1)S(1)}, bf16[2,64,512]{2,1,0:T(8,128)(2,1)S(1)}, u32[]{:S(2)}, u32[]{:S(2)}) collective-permute-start(bf16[2,64,512]{2,1,0:T(8,128)(2,1)S(1)} %get-tuple-element.78), channel_id=1, source_target_pairs={{0,2},{2,4},{4,6},{6,8},{8,10},{10,12},{12,14},{1,3},{3,5},{5,7},{... | collective-permute-start | bytes 393224 | tf_op jit(solution)/shard_map/ppermute | solution.py:92
  161.8 7.2 %collective-permute-start.18 = (bf16[2,64,512]{2,1,0:T(8,128)(2,1)S(1)}, bf16[2,64,512]{2,1,0:T(8,128)(2,1)S(1)}, u32[]{:S(2)}, u32[]{:S(2)}) collective-permute-start(bf16[2,64,512]{2,1,0:T(8,128)(2,1)S(1)} %get-tuple-element.79), channel_id=1, source_target_pairs={{2,0},{4,2},{6,4},{8,6},{10,8},{12,10},{14,12},{3,1},{5,3},{7,5},{... | collective-permute-start | bytes 393224 | tf_op jit(solution)/shard_map/ppermute | solution.py:93
  168.9 4.2 %collective-permute-start.19 = (bf16[8,128,1024]{2,1,0:T(8,128)(2,1)S(1)}, bf16[8,128,1024]{2,1,0:T(8,128)(2,1)S(1)}, u32[]{:S(2)}, u32[]{:S(2)}) collective-permute-start(bf16[8,128,1024]{2,1,0:T(8,128)(2,1)S(1)} %get-tuple-element.83), channel_id=1, source_target_pairs={{0,1},{1,0},{2,3},{3,2},{4,5},{5,4},{6,7},{7,6},{8,9},{9,8},{10,11... | collective-permute-start | bytes 6291464 | tf_op jit(solution)/shard_map/ppermute | solution.py:68
  174.3 23.3 %collective-permute-start.20 = (bf16[4,128,1024]{2,1,0:T(8,128)(2,1)S(1)}, bf16[4,128,1024]{2,1,0:T(8,128)(2,1)S(1)}, u32[]{:S(2)}, u32[]{:S(2)}) collective-permute-start(bf16[4,128,1024]{2,1,0:T(8,128)(2,1)S(1)} %slice.226), channel_id=1, source_target_pairs={{0,2},{1,5},{2,0},{3,7},{4,6},{5,1},{6,4},{7,3},{8,10},{9,13},{10,... | collective-permute-start | bytes 3145736 | tf_op jit(solution)/shard_map/ppermute | solution.py:78
  176.7 20.5 %collective-permute-start.24 = (bf16[2,128,1024]{2,1,0:T(8,128)(2,1)S(1)}, bf16[2,128,1024]{2,1,0:T(8,128)(2,1)S(1)}, u32[]{:S(2)}, u32[]{:S(2)}) collective-permute-start(bf16[2,128,1024]{2,1,0:T(8,128)(2,1)S(1)} %slice.228), channel_id=1, source_target_pairs={{0,4},{1,9},{2,6},{3,11},{4,0},{5,13},{6,2},{7,15},{8,12},{9,1},{1... | collective-permute-start | bytes 1572872 | tf_op jit(solution)/shard_map/ppermute | solution.py:78
  197.5 12.1 %collective-permute-start.25 = (bf16[1,128,1024]{2,1,0:T(8,128)(2,1)S(1)}, bf16[1,128,1024]{2,1,0:T(8,128)(2,1)S(1)}, u32[]{:S(2)}, u32[]{:S(2)}) collective-permute-start(bf16[1,128,1024]{2,1,0:T(8,128)(2,1)S(1)} %slice.230), channel_id=1, source_target_pairs={{0,8},{1,3},{2,10},{3,1},{4,12},{5,7},{6,14},{7,5},{8,0},{9,11},{1... | collective-permute-start | bytes 786440 | tf_op jit(solution)/shard_map/ppermute | solution.py:78
  198.1 15.0 %collective-permute-start.21 = (bf16[2,128,1024]{2,1,0:T(8,128)(2,1)S(1)}, bf16[2,128,1024]{2,1,0:T(8,128)(2,1)S(1)}, u32[]{:S(2)}, u32[]{:S(2)}) collective-permute-start(bf16[2,128,1024]{2,1,0:T(8,128)(2,1)S(1)} %slice.229), channel_id=1, source_target_pairs={{0,4},{1,9},{2,6},{3,11},{4,0},{5,13},{6,2},{7,15},{8,12},{9,1},{1... | collective-permute-start | bytes 1572872 | tf_op jit(solution)/shard_map/ppermute | solution.py:78
  209.6 4.0 %collective-permute-start.26 = (f32[64,1024]{1,0:T(8,128)S(1)}, f32[64,1024]{1,0:T(8,128)S(1)}, u32[]{:S(2)}, u32[]{:S(2)}) collective-permute-start(f32[64,1024]{1,0:T(8,128)S(1)} %fusion.4), channel_id=1, source_target_pairs={{0,1},{1,0},{2,3},{3,2},{4,5},{5,4},{6,7},{7,6},{8,9},{9,8},{10,11... | collective-permute-start | bytes 786440 | tf_op jit(solution)/shard_map/ppermute | solution.py:68
  213.2 11.1 %collective-permute-start.22 = (bf16[1,128,1024]{2,1,0:T(8,128)(2,1)S(1)}, bf16[1,128,1024]{2,1,0:T(8,128)(2,1)S(1)}, u32[]{:S(2)}, u32[]{:S(2)}) collective-permute-start(bf16[1,128,1024]{2,1,0:T(8,128)(2,1)S(1)} %slice.231), channel_id=1, source_target_pairs={{0,8},{1,3},{2,10},{3,1},{4,12},{5,7},{6,14},{7,5},{8,0},{9,11},{1... | collective-permute-start | bytes 786440 | tf_op jit(solution)/shard_map/ppermute | solution.py:78
  224.4 5.2 %collective-permute-start.23 = (f32[64,1024]{1,0:T(8,128)S(1)}, f32[64,1024]{1,0:T(8,128)S(1)}, u32[]{:S(2)}, u32[]{:S(2)}) collective-permute-start(f32[64,1024]{1,0:T(8,128)S(1)} %fusion.1), channel_id=1, source_target_pairs={{0,1},{1,0},{2,3},{3,2},{4,5},{5,4},{6,7},{7,6},{8,9},{9,8},{10,11... | collective-permute-start | bytes 786440 | tf_op jit(solution)/shard_map/ppermute | solution.py:68
  (8 other events, 39.5 us)

commit v3 on v2

--- a/solution.py
+++ b/solution.py
@@ -43,7 +43,7 @@
 
 
 def params():
-    return pltpu.CompilerParams(vmem_limit_bytes=40 << 20)
+    return pltpu.CompilerParams(vmem_limit_bytes=16 << 20)
 
 
 def tie(*values):
@@ -78,83 +78,110 @@
     return lax.ppermute(value, ("seq", "dp"), pairs)
 
 
-def widen(value, orders, j):
-    return jnp.concatenate([value, hop(value, orders, j)], axis=0)
-
-
-def fold(total, orders, j):
-    half = total.shape[0] // 2
-    return total[:half] + hop(total[half:].astype(BF), orders, j).astype(F32)
+def widen(value, got):
+    return jnp.concatenate([value, got], axis=0)
+
+
+def give(total, orders, j):
+    return hop(total[total.shape[0] // 2 :].astype(BF), orders, j)
+
+
+def fold_all(keep, got):
+    return keep + got.astype(F32)
+
+
+def fold(total, got):
+    return total[: total.shape[0] // 2] + got.astype(F32)
 
 
 def halo(first, last):
     count = lax.axis_size("seq")
-    low = lax.ppermute(last, "seq", [(i, i + 1) for i in range(count - 1)])
-    high = lax.ppermute(first, "seq", [(i + 1, i) for i in range(count - 1)])
+    low = lax.ppermute(last, "seq", [(i, i + 2) for i in range(count - 2)])
+    high = lax.ppermute(first, "seq", [(i + 2, i) for i in range(count - 2)])
     return low, high
 
 
-def by_core(own, other, run):
-    core = lax.axis_index("dp")
+def swap_pair(value):
+    count = lax.axis_size("seq")
+    return lax.ppermute(value, "seq", [(i, i ^ 1) for i in range(count)])
+
+
+def ordered(leading, mine, theirs):
+    return jnp.concatenate(
+        [jnp.where(leading, mine, theirs), jnp.where(leading, theirs, mine)], axis=0
+    )
+
+
+def split_pair(field, axis):
+    even = lax.axis_index("seq") % 2 == 0
+    half = field.shape[axis] // 2
+    low = lax.slice_in_dim(field, 0, half, axis=axis)
+    high = lax.slice_in_dim(field, half, 2 * half, axis=axis)
+    return jnp.where(even, low, high), jnp.where(even, high, low)
+
+
+def join_pair(mine, theirs, axis):
+    even = lax.axis_index("seq") % 2 == 0
+    return jnp.concatenate(
+        [jnp.where(even, mine, theirs), jnp.where(even, theirs, mine)], axis=axis
+    )
+
+
+def with_weights(pieces, orders, middle, run):
+    here, core = lax.axis_index("seq"), lax.axis_index("dp")
+    own, other = pieces
+    count, rows = own.shape[:2]
+    part = rows // 4
+
+    def case(taps, rest):
+        def whole(ref, steps, half):
+            cols = slice(half * middle, (half + 1) * middle)
+            return jnp.concatenate(
+                [ref[place_of(here ^ chip, steps), :, cols] for chip in range(count)], axis=0
+            )
+
+        def mix(h):
+            pieces = []
+            for chip in range(count):
+                place = place_of(here ^ chip, orders[1])
+                for lane in range(2):
+                    start = (2 * lane + h) * part
+                    pieces.append(rest[place, start : start + part, middle:])
+            return jnp.concatenate(pieces, axis=0)
+
+        run(
+            [
+                lambda: whole(taps, orders[0], 0),
+                lambda: whole(taps, orders[0], 1),
+                lambda: whole(rest, orders[1], 0),
+            ],
+            [lambda: mix(0), lambda: mix(1)],
+        )
 
     @pl.when(core == 0)
     def _():
-        run(own, other)
+        case(own, other)
 
     @pl.when(core == 1)
     def _():
-        run(other, own)
-
-
-def conv_weights(orders, taps, rest, middle):
-    here = lax.axis_index("seq")
-    count = taps.shape[0]
-
-    def whole(ref, steps, half):
-        cols = slice(half * middle, (half + 1) * middle)
-        return jnp.concatenate(
-            [ref[place_of(here ^ chip, steps), :, cols] for chip in range(count)], axis=0
-        )
-
-    return [
-        lambda: whole(taps, orders[0], 0),
-        lambda: whole(taps, orders[0], 1),
-        lambda: whole(rest, orders[1], 0),
-    ]
-
-
-def mix_halves(orders, rest, middle):
-    here = lax.axis_index("seq")
-    count, rows = rest.shape[:2]
-    part = rows // 4
-
-    def half(h):
-        pieces = []
-        for chip in range(count):
-            place = place_of(here ^ chip, orders[1])
-            for lane in range(2):
-                start = (2 * lane + h) * part
-                pieces.append(rest[place, start : start + part, middle:])
-        return jnp.concatenate(pieces, axis=0)
-
-    return [lambda: half(0), lambda: half(1)]
+        case(other, own)
+
+
+def norm_rows(source, w, start, size, target, put):
+    @pl.loop(0, size // 32)
+    def _(i):
+        rows = pl.multiple_of(i * 32, 32)
+        v = source[w, pl.ds(start + rows, 32), :].astype(F32)
+        target[w, pl.ds(put + rows, 32), :] = gelu(v * norm_scale(v)).astype(BF)
 
 
 def norm_kernel(x_ref, low_ref, high_ref, ext_ref):
     dilate = low_ref.shape[1]
     length = x_ref.shape[1]
     for w in range(x_ref.shape[0]):
-        for source, start, size in (
-            (low_ref, 0, dilate),
-            (x_ref, dilate, length),
-            (high_ref, dilate + length, dilate),
-        ):
-
-            @pl.loop(0, size // 32)
-            def _(i):
-                rows = pl.multiple_of(i * 32, 32)
-                v = source[w, pl.ds(rows, 32), :].astype(F32)
-                ext_ref[w, pl.ds(start + rows, 32), :] = gelu(v * norm_scale(v)).astype(BF)
+        norm_rows(low_ref, w, 0, dilate, ext_ref, 0)
+        norm_rows(x_ref, w, 0, length, ext_ref, dilate)
+        norm_rows(high_ref, w, 0, dilate, ext_ref, dilate + length)
 
 
 def norm_ext(x, low, high):
@@ -172,12 +199,11 @@
 def forward_kernel(
     orders, dilate, edge, ext, x_ref, own, other, pre_ref, hid_ref, x2_ref, first_ref, last_ref
 ):
+    pieces = (own, other)
     windows, length, width = x_ref.shape
     middle = hid_ref.shape[1]
 
-    def run(taps, rest):
-        conv = conv_weights(orders, taps, rest, middle)
-        mix = mix_halves(orders, rest, middle)
+    def run(conv, mix):
         for w in range(windows):
             rows = slice(w * length, (w + 1) * length)
             pre = sum(dot(ext[w, k * dilate : k * dilate + length, :], conv[k]()) for k in range(3))
@@ -188,15 +214,10 @@
                 cols = slice(h * middle, (h + 1) * middle)
                 x2_ref[w, :, cols] = (x_ref[w, :, cols].astype(F32) + dot(hid, mix[h]())).astype(BF)
 
-    by_core(own, other, run)
+    with_weights(pieces, orders, middle, run)
     for w in range(windows):
-        for target, start in ((first_ref, 0), (last_ref, length - edge)):
-
-            @pl.loop(0, edge // 32)
-            def _(i):
-                rows = pl.multiple_of(i * 32, 32)
-                v = x2_ref[w, pl.ds(start + rows, 32), :].astype(F32)
-                target[w, pl.ds(rows, 32), :] = gelu(v * norm_scale(v)).astype(BF)
+        norm_rows(x2_ref, w, 0, edge, first_ref, 0)
+        norm_rows(x2_ref, w, length - edge, edge, last_ref, 0)
 
 
 def forward_block(ext, x, pieces, orders, dilate, edge):
@@ -221,9 +242,10 @@
 
 
 def turn_kernel(
-    orders, dilate, first, last, low, high, e_ref, own, other,
+    orders, dilate, first, last, low, high, x_ref, e_ref, own, other,
     ext, hid_ref, dpre_ref, dfirst, dlast,
 ):
+    pieces = (own, other)
     windows, length, width = e_ref.shape
     edge = first.shape[1]
     middle = hid_ref.shape[1]
@@ -232,10 +254,9 @@
             (low, 0), (first, dilate), (last, dilate + length - edge), (high, dilate + length),
         ):
             ext[w, start : start + edge, :] = source[w]
-
-    def run(taps, rest):
-        conv = conv_weights(orders, taps, rest, middle)
-        mix = mix_halves(orders, rest, middle)
+        norm_rows(x_ref, w, edge, length - 2 * edge, ext, dilate + edge)
+
+    def run(conv, mix):
         for w in range(windows):
             rows = slice(w * length, (w + 1) * length)
             pre = sum(dot(ext[w, k * dilate : k * dilate + length, :], conv[k]()) for k in range(3))
@@ -243,13 +264,13 @@
             hid_ref[rows, :] = gelu(pre).astype(BF)
             dpre_ref[rows, :] = (gelu_slope(pre) * dhid).astype(BF)
 
-    by_core(own, other, run)
+    with_weights(pieces, orders, middle, run)
     for w in range(windows):
         dfirst[w] = dpre_ref[w * length : w * length + dilate, :]
         dlast[w] = dpre_ref[(w + 1) * length - dilate : (w + 1) * length, :]
 
 
-def turn_block(first, last, low, high, e, pieces, orders, dilate):
+def turn_block(first, last, low, high, x, e, pieces, orders, dilate):
     windows, length, width = e.shape
     middle = pieces[0].shape[2] // 2
     flat = windows * length
@@ -262,12 +283,12 @@
             jax.ShapeDtypeStruct((windows, dilate, middle), BF),
             jax.ShapeDtypeStruct((windows, dilate, middle), BF),
         ),
-        in_specs=[VMEM] * 7,
+        in_specs=[VMEM] * 8,
         out_specs=(VMEM,) * 5,
         compiler_params=params(),
         cost_estimate=cost(flat, width, middle),
         name="turn_block",
-    )(first, last, low, high, e, *pieces)
+    )(first, last, low, high, x, e, *pieces)
 
 
 def grads_kernel(orders, dilate, ext, hid, e_ref, dpre, keep, send, full):
@@ -332,9 +353,11 @@
 
 
 def back_kernel(orders, dilate, chained, *refs):
-    dpre, low, high, x_ref, e_ref, own, other = refs[:7]
+    dpre, low, high, x_ref, e_ref = refs[:5]
+    pieces = refs[5:7]
     if chained:
-        own_m, other_m, pre_ref, out_ref, dprev, dfirst, dlast, ext, dn = refs[7:]
+        pieces_m = refs[7:9]
+        pre_ref, out_ref, dprev, dfirst, dlast, ext, dn = refs[9:]
     else:
         out_ref, ext, dn = refs[7:]
     windows, length, width = x_ref.shape
@@ -344,15 +367,14 @@
         ext[w, dilate : dilate + length, :] = dpre[w * length : (w + 1) * length, :]
         ext[w, dilate + length :, :] = high[w]
 
-    def run(taps, rest):
-        conv = conv_weights(orders, taps, rest, middle)
+    def run(conv, mix):
         for w in range(windows):
             dn[w] = sum(
                 dot(ext[w, (2 - k) * dilate : (2 - k) * dilate + length, :], conv[k](), NT)
                 for k in range(3)
             )
 
-    by_core(own, other, run)
+    with_weights(pieces, orders, middle, run)
     for w in range(windows):
 
         @pl.loop(0, length // 32)
@@ -367,8 +389,7 @@
 
     if chained:
 
-        def turn(taps, rest):
-            mix = mix_halves(orders, rest, middle)
+        def turn(conv, mix):
             for w in range(windows):
                 dhid = dot(out_ref[w, :, :middle], mix[0](), NT) + dot(
                     out_ref[w, :, middle:], mix[1](), NT
@@ -376,7 +397,7 @@
                 rows = slice(w * length, (w + 1) * length)
                 dprev[rows, :] = (gelu_slope(pre_ref[rows, :]) * dhid).astype(BF)
 
-        by_core(own_m, other_m, turn)
+        with_weights(pieces_m, orders, middle, turn)
         edge = dfirst.shape[1]
         for w in range(windows):
             dfirst[w] = dprev[w * length : w * length + edge, :]
@@ -437,63 +458,93 @@
 def body(activations, cotangent, conv_one, mix_one, conv_two, mix_two):
     count = lax.axis_size("seq")
     orders = step_orders(count)
-    depth = len(orders[0])
+    last_step = len(orders[0]) - 1
     middle = conv_one.shape[2]
-    length = activations.shape[1]
     leading = lax.axis_index("dp") == 0
 
-    packed = [pack(conv_one, mix_one), pack(conv_two, mix_two)]
-    mine = [jnp.where(leading, first, second) for first, second in packed]
-    got = cross(jnp.stack([jnp.where(leading, second, first) for first, second in packed]))
-    own_one, own_two = (
-        jnp.where(
-            leading,
-            jnp.concatenate([mine[b], got[b]], axis=0),
-            jnp.concatenate([got[b], mine[b]], axis=0),
-        )[None]
-        for b in range(2)
-    )
-    low, high = halo(
-        activations[:, :DILATE_ONE], activations[:, length - DILATE_ONE :]
-    )
-    own_one = widen(own_one, orders, 0)
-    ext_one = norm_ext(activations, low, high)
-    own_one, own_two, ext_one = tie(own_one, own_two, ext_one)
-    for j in range(1, depth):
-        own_one, own_two = tie(widen(own_one, orders, j), widen(own_two, orders, j - 1))
-    pieces_one = (own_one, cross(own_one))
-    own_two = widen(own_two, orders, depth - 1)
+    def chip_part(conv, mix):
+        first, second = pack(conv, mix)
+        got = cross(jnp.where(leading, second, first))
+        return ordered(leading, jnp.where(leading, first, second), got)[None]
+
+    own_one = chip_part(conv_one, mix_one)
+    got_one = hop(own_one, orders, 0)
+    activations, conv_two, mix_two, own_one = tie(activations, conv_two, mix_two, own_one)
+    mine_x, gives_x = split_pair(activations, 0)
+    got_x = swap_pair(gives_x)
+    own_two = chip_part(conv_two, mix_two)
+    own_one = widen(own_one, got_one)
+    got_one = hop(own_one, orders, 1)
+    got_two = hop(own_two, orders, 0)
+    own_one, cotangent, got_x = tie(own_one, cotangent, got_x)
+    x = join_pair(mine_x, got_x, 1)
+    length = x.shape[1]
+    low, high = halo(x[:, :DILATE_ONE], x[:, length - DILATE_ONE :])
+    mine_e, gives_e = split_pair(cotangent, 0)
+    got_e = swap_pair(gives_e)
+    ext_one = norm_ext(x, low, high)
+    got_one, got_two, ext_one = tie(got_one, got_two, ext_one)
+    for j in range(2, last_step + 1):
+        own_one, own_two = widen(own_one, got_one), widen(own_two, got_two)
+        got_one, got_two = tie(hop(own_one, orders, j), hop(own_two, orders, j - 1))
+    own_one = widen(own_one, got_one)
+    got_one = cross(own_one)
+    own_one, got_two = tie(own_one, got_two)
+    own_two = widen(own_two, got_two)
+    got_two = hop(own_two, orders, last_step)
+    e = join_pair(mine_e, got_e, 1)
+    pieces_one = (own_one, got_one)
     pre_one, hid_one, second_in, first, last = forward_block(
-        ext_one, activations, pieces_one, orders, DILATE_ONE, DILATE_TWO
-    )
-    own_two, first, last = tie(own_two, first, last)
+        ext_one, x, pieces_one, orders, DILATE_ONE, DILATE_TWO
+    )
     low, high = halo(first, last)
+    got_two, first, last = tie(got_two, first, last)
+    own_two = widen(own_two, got_two)
     pieces_two = (own_two, cross(own_two))
     ext_two, hid_two, dpre_two, dfirst, dlast = turn_block(
-        first, last, low, high, cotangent, pieces_two, orders, DILATE_TWO
-    )
+        first, last, low, high, second_in, e, pieces_two, orders, DILATE_TWO
+    )
+
     dlow, dhigh = halo(dfirst, dlast)
-    keep, send = grads_block(ext_two, hid_two, cotangent, dpre_two, orders, DILATE_TWO, count)
-    dlow, dhigh, keep, send = tie(dlow, dhigh, keep, send)
-    total_two = keep + cross(send).astype(F32)
-    total_two, dlow, dhigh = tie(total_two, dlow, dhigh)
+    keep_two, send = grads_block(ext_two, hid_two, e, dpre_two, orders, DILATE_TWO, count)
+    dlow, dhigh, send = tie(dlow, dhigh, send)
+    got_two = cross(send)
     upstream, dpre_one, dfirst, dlast = back_block(
-        dpre_two, dlow, dhigh, second_in, cotangent, pieces_two, orders, DILATE_TWO,
+        dpre_two, dlow, dhigh, second_in, e, pieces_two, orders, DILATE_TWO,
         (pieces_one, pre_one, DILATE_ONE),
     )
+    got_two, dpre_one, upstream = tie(got_two, dpre_one, upstream)
+    total_two = fold_all(keep_two, got_two)
+    got_two = give(total_two, orders, last_step)
+    total_two, dpre_one = tie(total_two, dpre_one)
+    keep_one, send = grads_block(ext_one, hid_one, upstream, dpre_one, orders, DILATE_ONE, count)
+    got_one = cross(send)
+    dfirst, dlast, send, got_two = tie(dfirst, dlast, send, got_two)
     dlow, dhigh = halo(dfirst, dlast)
-    keep, send = grads_block(ext_one, hid_one, upstream, dpre_one, orders, DILATE_ONE, count)
-    total_two = fold(total_two, orders, depth - 1)
-    total_two, keep, send, dlow, dhigh = tie(total_two, keep, send, dlow, dhigh)
-    total_one = keep + cross(send).astype(F32)
+    total_one = fold_all(keep_one, got_one)
+    got_one = give(total_one, orders, last_step)
+    total_one, dlow, dhigh, got_two = tie(total_one, dlow, dhigh, got_two)
     (input_grad,) = back_block(
-        dpre_one, dlow, dhigh, activations, upstream, pieces_one, orders, DILATE_ONE
-    )
-    for j in reversed(range(depth - 1)):
-        total_two = fold(total_two, orders, j)
-    for j in reversed(range(depth)):
-        total_one = fold(total_one, orders, j)
-    return (input_grad, *unpack(total_one[0], middle), *unpack(total_two[0], middle))
+        dpre_one, dlow, dhigh, x, upstream, pieces_one, orders, DILATE_ONE
+    )
+    input_grad, got_one, got_two = tie(input_grad, got_one, got_two)
+    mine_g, gives_g = split_pair(input_grad, 1)
+    for j in reversed(range(last_step)):
+        total_two = fold(total_two, got_two)
+        got_two = give(total_two, orders, j)
+        total_one = fold(total_one, got_one)
+        got_one = give(total_one, orders, j)
+        if j == last_step - 1:
+            total_one, gives_g = tie(total_one, gives_g)
+            got_g = swap_pair(gives_g)
+        if j > 0:
+            got_one, got_two = tie(got_one, got_two)
+    total_two = fold(total_two, got_two)
+    grads_two = unpack(total_two[0], middle)
+    grads_two, got_one, got_g = tie(grads_two, got_one, got_g)
+    total_one = fold(total_one, got_one)
+    input_grad = join_pair(mine_g, got_g, 0)
+    return (input_grad, *unpack(total_one[0], middle), *grads_two)
 
 
 def solution(mesh):

time: 232 us -> 203 us (0.88)
  waiting for transfers between devices: 125 us -> 101 us
  local copies, waits for them, and re-layouts: 8.39 us -> 4.43 us
    ppermute x8 -> x11, waiting for transfers between devices: 36.8 us -> 21.4 us  [the longest x4 9.47 us: halo(): high = lax.ppermute(first, 'seq', [(i + 2, i) for i in range(count - 2)])]
    ppermute x12, waiting for transfers between devices: 80.1 us -> 75.6 us  [hop(): return lax.ppermute(value, ('seq', 'dp'), pairs)]
    ppermute x7 -> x8, waiting for transfers between devices: 8.35 us -> 4.37 us  [cross(): return lax.ppermute(value, 'dp', [(0, 1), (1, 0)])]
    ppermute x7 -> x8, starting transfers between devices: 10.5 us -> 7.3 us  [cross(): return lax.ppermute(value, 'dp', [(0, 1), (1, 0)])]
    ppermute x12, starting transfers between devices: 21 us -> 23.5 us  [hop(): return lax.ppermute(value, ('seq', 'dp'), pairs)]
    ppermute x8 -> x11, starting transfers between devices: 23.2 us -> 24.9 us  [the longest x4 15.2 us: halo(): low = lax.ppermute(last, 'seq', [(i, i + 2) for i in range(count - 2)])]
  transfers between devices with their start and end apart: 27 -> 31, of which waited for: 15 -> 19; matrix products, arithmetic and copies ran while one was open for 2% -> 3% of each run, Pallas kernels for 11% -> 12%
where the time goes in v3:
time: 203 us
  waiting for transfers between devices  101 us (50%)
  starting transfers between devices  55.7 us (27%)
  Pallas kernels  31.6 us (16%)
  other arithmetic  8.71 us (4%)
  local copies, waits for them, and re-layouts  4.43 us (2%)
    ppermute x12, waiting for transfers between devices, hop(): return lax.ppermute(value, ('seq', 'dp'), pairs)  75.6 us
    ppermute x12, starting transfers between devices, hop(): return lax.ppermute(value, ('seq', 'dp'), pairs)  23.5 us
    ppermute x4, starting transfers between devices, halo(): low = lax.ppermute(last, 'seq', [(i, i + 2) for i in range(count - 2)])  15.2 us
    pallas_call x2, Pallas kernels, back_block(): pl.pallas_call(functools.partial(back_kernel, orders, dilate, chained), o...  13.9 us
    ppermute x4, waiting for transfers between devices, halo(): high = lax.ppermute(first, 'seq', [(i + 2, i) for i in range(count - 2)])  9.47 us
    ppermute x8, starting transfers between devices, cross(): return lax.ppermute(value, 'dp', [(0, 1), (1, 0)])  7.3 us
    pallas_call x2, Pallas kernels, grads_block(): pl.pallas_call(functools.partial(grads_kernel, orders, dilate), out_shape...  7.09 us
    ppermute x4, waiting for transfers between devices, halo(): low = lax.ppermute(last, 'seq', [(i, i + 2) for i in range(count - 2)])  6.53 us
  transfers between devices with their start and end apart: 31, of which 19 were waited for; matrix products, arithmetic and copies ran while one was open for 3% of the time, Pallas kernels for 12%

profile of v3, /device:TPU:0, one launch (start us, length us, event | category | flops | bytes accessed | tf_op | source)
XLA Modules:
  0.0 203.0 jit_solution(7879494667254430972)
XLA Ops:
  5.0 4.0 %collective-permute-start.2 = (bf16[1,128,1024]{2,1,0:T(8,128)(2,1)S(1)}, bf16[1,128,1024]{2,1,0:T(8,128)(2,1)S(1)}, u32[]{:S(2)}, u32[]{:S(2)}) collective-permute-start(bf16[1,128,1024]{2,1,0:T(8,128)(2,1)S(1)} %maximum_bitcast_fusion), channel_id=1, source_target_pairs={{0,8},{1,3},{2,10},{3,1},{4,12},{5,7},{6,14},{7,5},{8,0},{9,11},{1... | collective-permute-start | bytes 786440 | tf_op jit(solution)/shard_map/ppermute | solution.py:78
  10.9 5.4 %collective-permute-done.2 = bf16[1,128,1024]{2,1,0:T(8,128)(2,1)S(1)} collective-permute-done((bf16[1,128,1024]{2,1,0:T(8,128)(2,1)S(1)}, bf16[1,128,1024]{2,1,0:T(8,128)(2,1)S(1)}, u32[]{:S(2)}, u32[]{:S(2)}) %collective-permute-start.2) | collective-permute-done | bytes 262176 | tf_op jit(solution)/shard_map/ppermute | solution.py:78
  16.4 6.7 %collective-permute-start.3 = (bf16[2,128,1024]{2,1,0:T(8,128)(2,1)S(1)}, bf16[2,128,1024]{2,1,0:T(8,128)(2,1)S(1)}, u32[]{:S(2)}, u32[]{:S(2)}) collective-permute-start(bf16[2,128,1024]{2,1,0:T(8,128)(2,1)S(1)} %constant_dynamic-update-slice_fusion), channel_id=1, source_target_pairs={{0,4},{1,9},{2,6},{3,11},{4,0},{5,13},{6,2},{7,15},{8,12},{9,1},{1... | collective-permute-start | bytes 1572872 | tf_op jit(solution)/shard_map/ppermute | solution.py:78
  23.1 3.6 %collective-permute-start.4 = (bf16[1,128,1024]{2,1,0:T(8,128)(2,1)S(1)}, bf16[1,128,1024]{2,1,0:T(8,128)(2,1)S(1)}, u32[]{:S(2)}, u32[]{:S(2)}) collective-permute-start(bf16[1,128,1024]{2,1,0:T(8,128)(2,1)S(1)} %maximum_bitcast_fusion.1), channel_id=1, source_target_pairs={{0,8},{1,3},{2,10},{3,1},{4,12},{5,7},{6,14},{7,5},{8,0},{9,11},{1... | collective-permute-start | bytes 786440 | tf_op jit(solution)/shard_map/ppermute | solution.py:78
  26.8 1.9 collective-permute-start.6
  30.2 5.3 %collective-permute-done.6.low_ref = bf16[1,64,1024]{2,1,0:T(8,128)(2,1)S(1)} collective-permute-done((bf16[1,64,1024]{2,1,0:T(8,128)(2,1)S(1)}, bf16[1,64,1024]{2,1,0:T(8,128)(2,1)S(1)}, u32[]{:S(2)}, u32[]{:S(2)}) %collective-permute-start.6) | collective-permute-done | bytes 131104 | tf_op jit(solution)/shard_map/ppermute | solution.py:99
  35.5 3.2 %collective-permute-done.7.high_ref = bf16[1,64,1024]{2,1,0:T(8,128)(2,1)S(1)} collective-permute-done((bf16[1,64,1024]{2,1,0:T(8,128)(2,1)S(1)}, bf16[1,64,1024]{2,1,0:T(8,128)(2,1)S(1)}, u32[]{:S(2)}, u32[]{:S(2)}) %collective-permute-start.7) | collective-permute-done | bytes 131104 | tf_op jit(solution)/shard_map/ppermute | solution.py:100
  38.7 3.0 %norm_ext.1.ext = bf16[1,640,1024]{2,1,0:T(8,128)(2,1)S(1)} custom-call(bf16[1,512,1024]{2,1,0:T(8,128)(2,1)S(1)} %pad_maximum_fusion.1.x_ref.refs_3_, bf16[1,64,1024]{2,1,0:T(8,128)(2,1)S(1)} %collective-permute-done.6.low_ref, bf16[1,64,1024]{2,1,0:T(8,128)(2,1)S(1)} %collective-permute-done.7.high_ref), custom_call_target="tpu_custom_call" | custom-call | tf_op jit(solution)/shard_map/norm_ext/pallas_call | solution.py:189
  42.1 16.4 %collective-permute-done.9 = bf16[2,128,1024]{2,1,0:T(8,128)(2,1)S(1)} collective-permute-done((bf16[2,128,1024]{2,1,0:T(8,128)(2,1)S(1)}, bf16[2,128,1024]{2,1,0:T(8,128)(2,1)S(1)}, u32[]{:S(2)}, u32[]{:S(2)}) %collective-permute-start.9) | collective-permute-done | bytes 524320 | tf_op jit(solution)/shard_map/ppermute | solution.py:78
  58.6 3.8 %collective-permute-start.11 = (bf16[8,128,1024]{2,1,0:T(8,128)(2,1)S(1)}, bf16[8,128,1024]{2,1,0:T(8,128)(2,1)S(1)}, u32[]{:S(2)}, u32[]{:S(2)}) collective-permute-start(bf16[8,128,1024]{2,1,0:T(8,128)(2,1)S(1)} %constant_dynamic-update-slice_fusion.2.own.refs_7_.refs_5_), channel_id=1, source_target_pairs={{0,1},{1,0},{2,3},{3,2},{4,5},{5,4},{6,7},{7,6},{8,9},{9,8},{10,11... | collective-permute-start | bytes 6291464 | tf_op jit(solution)/shard_map/ppermute | solution.py:68
  62.5 3.1 %collective-permute-start.10 = (bf16[4,128,1024]{2,1,0:T(8,128)(2,1)S(1)}, bf16[4,128,1024]{2,1,0:T(8,128)(2,1)S(1)}, u32[]{:S(2)}, u32[]{:S(2)}) collective-permute-start(bf16[4,128,1024]{2,1,0:T(8,128)(2,1)S(1)} %pad_maximum_fusion.3), channel_id=1, source_target_pairs={{0,2},{1,5},{2,0},{3,7},{4,6},{5,1},{6,4},{7,3},{8,10},{9,13},{10,... | collective-permute-start | bytes 3145736 | tf_op jit(solution)/shard_map/ppermute | solution.py:78
  66.2 3.7 %forward_block.1 = (f32[512,512]{1,0:T(8,128)S(1)}, bf16[512,512]{1,0:T(8,128)(2,1)S(1)}, bf16[1,512,1024]{2,1,0:T(8,128)(2,1)S(1)}, bf16[1,128,1024]{2,1,0:T(8,128)(2,1)S(1)}, bf16[1,128,1024]{2,1,0:T(8,128)(2,1)S(1)}) custom-call(bf16[1,640,1024]{2,1,0:T(8,128)(2,1)S(1)} %norm_ext.1.ext, bf16[1,512,1024]{2,1,0:T(8,128)(2,1)S(1)} %pad_maximum_fusion.1.x_ref.refs_3_, ...), custom_call_target="tpu_custom_call" | custom-call | flops 2147483648 | bytes 8388608 | tf_op jit(solution)/shard_map/forward_block/pallas_call | solution.py:227
  69.9 8.5 %collective-permute-done.10 = bf16[4,128,1024]{2,1,0:T(8,128)(2,1)S(1)} collective-permute-done((bf16[4,128,1024]{2,1,0:T(8,128)(2,1)S(1)}, bf16[4,128,1024]{2,1,0:T(8,128)(2,1)S(1)}, u32[]{:S(2)}, u32[]{:S(2)}) %collective-permute-start.10) | collective-permute-done | bytes 1048608 | tf_op jit(solution)/shard_map/ppermute | solution.py:78
  79.7 2.1 %collective-permute-start.14 = (bf16[1,256,1024]{2,1,0:T(8,128)(2,1)S(1)}, bf16[1,256,1024]{2,1,0:T(8,128)(2,1)S(1)}, u32[]{:S(2)}, u32[]{:S(2)}) collective-permute-start(bf16[1,256,1024]{2,1,0:T(8,128)(2,1)S(1)} %broadcast_select_fusion.6), channel_id=1, source_target_pairs={{0,2},{2,0},{4,6},{6,4},{8,10},{10,8},{12,14},{14,12},{1,3},{3,1},... | collective-permute-start | bytes 1572872 | tf_op jit(solution)/shard_map/ppermute | solution.py:106
  83.1 5.9 %collective-permute-start.12 = (bf16[1,128,1024]{2,1,0:T(8,128)(2,1)S(1)}, bf16[1,128,1024]{2,1,0:T(8,128)(2,1)S(1)}, u32[]{:S(2)}, u32[]{:S(2)}) collective-permute-start(bf16[1,128,1024]{2,1,0:T(8,128)(2,1)S(1)} %get-tuple-element.82.last), channel_id=1, source_target_pairs={{0,4},{2,6},{4,8},{6,10},{8,12},{10,14},{1,5},{3,7},{5,9},{7,11},{... | collective-permute-start | bytes 786440 | tf_op jit(solution)/shard_map/ppermute | solution.py:99
  89.0 5.4 %collective-permute-done.14 = bf16[1,256,1024]{2,1,0:T(8,128)(2,1)S(1)} collective-permute-done((bf16[1,256,1024]{2,1,0:T(8,128)(2,1)S(1)}, bf16[1,256,1024]{2,1,0:T(8,128)(2,1)S(1)}, u32[]{:S(2)}, u32[]{:S(2)}) %collective-permute-start.14) | collective-permute-done | bytes 524320 | tf_op jit(solution)/shard_map/ppermute | solution.py:106
  94.6 3.8 %turn_block.1 = (bf16[1,768,1024]{2,1,0:T(8,128)(2,1)S(1)}, bf16[512,512]{1,0:T(8,128)(2,1)S(1)}, bf16[512,512]{1,0:T(8,128)(2,1)S(1)}, bf16[1,128,512]{2,1,0:T(8,128)(2,1)S(1)}, bf16[1,128,512]{2,1,0:T(8,128)(2,1)S(1)}) custom-call(bf16[1,128,1024]{2,1,0:T(8,128)(2,1)S(1)} %get-tuple-element.81.first, bf16[1,128,1024]{2,1,0:T(8,128)(2,1)S(1)} %get-tuple-element.82.last, ...), custom_call_target="tpu_custom_call" | custom-call | flops 2147483648 | bytes 8388608 | tf_op jit(solution)/shard_map/turn_block/pallas_call | solution.py:277
  98.5 4.3 %collective-permute-start.16 = (bf16[1,128,512]{2,1,0:T(8,128)(2,1)S(1)}, bf16[1,128,512]{2,1,0:T(8,128)(2,1)S(1)}, u32[]{:S(2)}, u32[]{:S(2)}) collective-permute-start(bf16[1,128,512]{2,1,0:T(8,128)(2,1)S(1)} %get-tuple-element.90), channel_id=1, source_target_pairs={{0,4},{2,6},{4,8},{6,10},{8,12},{10,14},{1,5},{3,7},{5,9},{7,11},{... | collective-permute-start | bytes 393224 | tf_op jit(solution)/shard_map/ppermute | solution.py:99
  104.1 3.7 %grads_block.2 = (f32[8,128,1024]{2,1,0:T(8,128)S(1)}, bf16[8,128,1024]{2,1,0:T(8,128)(2,1)S(1)}) custom-call(bf16[1,768,1024]{2,1,0:T(8,128)(2,1)S(1)} %get-tuple-element.86.ext, bf16[512,512]{1,0:T(8,128)(2,1)S(1)} %get-tuple-element.87.hid, bf16[1,512,1024]{2,1,0:T(8,128)(2,1)S(1)} %pad_maximum_fusion.4.e_ref.refs_4_, ...), custom_call_target="tpu_custom_call" | custom-call | flops 2147483648 | bytes 8388608 | tf_op jit(solution)/shard_map/grads_block/pallas_call | solution.py:343
  107.8 1.9 collective-permute-done.17.refs_2_
  109.7 7.4 %back_block.2 = (bf16[1,512,1024]{2,1,0:T(8,128)(2,1)S(1)}, bf16[512,512]{1,0:T(8,128)(2,1)S(1)}, bf16[1,64,512]{2,1,0:T(8,128)(2,1)S(1)}, bf16[1,64,512]{2,1,0:T(8,128)(2,1)S(1)}) custom-call(bf16[512,512]{1,0:T(8,128)(2,1)S(1)} %get-tuple-element.88.dpre.refs_0_, bf16[1,128,512]{2,1,0:T(8,128)(2,1)S(1)} %collective-permute-done.16.refs_1_, ...), custom_call_target="tpu_custom_call" | custom-call | flops 2147483648 | bytes 8388608 | tf_op jit(solution)/shard_map/back_block/pallas_call | solution.py:421
  118.2 3.4 %grads_block.3 = (f32[8,128,1024]{2,1,0:T(8,128)S(1)}, bf16[8,128,1024]{2,1,0:T(8,128)(2,1)S(1)}) custom-call(bf16[1,640,1024]{2,1,0:T(8,128)(2,1)S(1)} %norm_ext.1.ext, bf16[512,512]{1,0:T(8,128)(2,1)S(1)} %get-tuple-element.102.hid, bf16[1,512,1024]{2,1,0:T(8,128)(2,1)S(1)} %get-tuple-element.103.e_ref.refs_4_, ...), custom_call_target="tpu_custom_call" | custom-call | flops 2147483648 | bytes 8388608 | tf_op jit(solution)/shard_map/grads_block/pallas_call | solution.py:343
  129.0 8.2 %collective-permute-done.20 = bf16[4,128,1024]{2,1,0:T(8,128)(2,1)S(1)} collective-permute-done((bf16[4,128,1024]{2,1,0:T(8,128)(2,1)S(1)}, bf16[4,128,1024]{2,1,0:T(8,128)(2,1)S(1)}, u32[]{:S(2)}, u32[]{:S(2)}) %collective-permute-start.20) | collective-permute-done | bytes 1048608 | tf_op jit(solution)/shard_map/ppermute | solution.py:78
  137.2 3.0 %collective-permute-start.21 = (bf16[1,64,512]{2,1,0:T(8,128)(2,1)S(1)}, bf16[1,64,512]{2,1,0:T(8,128)(2,1)S(1)}, u32[]{:S(2)}, u32[]{:S(2)}) collective-permute-start(bf16[1,64,512]{2,1,0:T(8,128)(2,1)S(1)} %get-tuple-element.108), channel_id=1, source_target_pairs={{0,4},{2,6},{4,8},{6,10},{8,12},{10,14},{1,5},{3,7},{5,9},{7,11},{... | collective-permute-start | bytes 196616 | tf_op jit(solution)/shard_map/ppermute | solution.py:99
  142.8 4.4 %collective-permute-done.22.refs_2_ = bf16[1,64,512]{2,1,0:T(8,128)(2,1)S(1)} collective-permute-done((bf16[1,64,512]{2,1,0:T(8,128)(2,1)S(1)}, bf16[1,64,512]{2,1,0:T(8,128)(2,1)S(1)}, u32[]{:S(2)}, u32[]{:S(2)}) %collective-permute-start.22) | collective-permute-done | bytes 65568 | tf_op jit(solution)/shard_map/ppermute | solution.py:100
  147.2 6.5 %back_block.3 = bf16[1,512,1024]{2,1,0:T(8,128)(2,1)S(1)} custom-call(bf16[512,512]{1,0:T(8,128)(2,1)S(1)} %get-tuple-element.101.dpre.refs_0_, bf16[1,64,512]{2,1,0:T(8,128)(2,1)S(1)} %collective-permute-done.21.refs_1_, bf16[1,64,512]{2,1,0:T(8,128)(2,1)S(1)} %collective-permute-done.22.refs_2_, bf16[1,512,1024]{2,1,0:T(8,128)(2,1)S(1)} %pad_maximum_fusion.1.x_ref.refs_3_, ...), custom_call_target="tpu_custom_call" | custom-call | flops 2147483648 | bytes 8388608 | tf_op jit(solution)/shard_map/back_block/pallas_call | solution.py:421
  154.7 2.0 collective-permute-start.25
  156.7 11.9 %collective-permute-done.24 = bf16[2,128,1024]{2,1,0:T(8,128)(2,1)S(1)} collective-permute-done((bf16[2,128,1024]{2,1,0:T(8,128)(2,1)S(1)}, bf16[2,128,1024]{2,1,0:T(8,128)(2,1)S(1)}, u32[]{:S(2)}, u32[]{:S(2)}) %collective-permute-start.24) | collective-permute-done | bytes 524320 | tf_op jit(solution)/shard_map/ppermute | solution.py:78
  168.6 10.7 %collective-permute-done.25 = bf16[2,128,1024]{2,1,0:T(8,128)(2,1)S(1)} collective-permute-done((bf16[2,128,1024]{2,1,0:T(8,128)(2,1)S(1)}, bf16[2,128,1024]{2,1,0:T(8,128)(2,1)S(1)}, u32[]{:S(2)}, u32[]{:S(2)}) %collective-permute-start.25) | collective-permute-done | bytes 524320 | tf_op jit(solution)/shard_map/ppermute | solution.py:78
  180.6 8.1 %collective-permute-done.26 = bf16[1,128,1024]{2,1,0:T(8,128)(2,1)S(1)} collective-permute-done((bf16[1,128,1024]{2,1,0:T(8,128)(2,1)S(1)}, bf16[1,128,1024]{2,1,0:T(8,128)(2,1)S(1)}, u32[]{:S(2)}, u32[]{:S(2)}) %collective-permute-start.26) | collective-permute-done | bytes 262176 | tf_op jit(solution)/shard_map/ppermute | solution.py:78
  188.8 2.0 collective-permute-start.27
  193.5 6.2 %collective-permute-done.28 = bf16[1,128,1024]{2,1,0:T(8,128)(2,1)S(1)} collective-permute-done((bf16[1,128,1024]{2,1,0:T(8,128)(2,1)S(1)}, bf16[1,128,1024]{2,1,0:T(8,128)(2,1)S(1)}, u32[]{:S(2)}, u32[]{:S(2)}) %collective-permute-start.28) | collective-permute-done | bytes 262176 | tf_op jit(solution)/shard_map/ppermute | solution.py:78
  (107 shorter events, 31.9 us)
Async XLA Ops:
  0.7 8.5 %copy-start = (bf16[2,256,1024]{2,1,0:T(8,128)(2,1)S(1)}, bf16[2,256,1024]{2,1,0:T(8,128)(2,1)}, u32[]{:S(2)}) copy-start(bf16[2,256,1024]{2,1,0:T(8,128)(2,1)} %param.6) | copy-start | bytes 3145732
  3.4 1.5 collective-permute-start
  5.0 11.3 %collective-permute-start.2 = (bf16[1,128,1024]{2,1,0:T(8,128)(2,1)S(1)}, bf16[1,128,1024]{2,1,0:T(8,128)(2,1)S(1)}, u32[]{:S(2)}, u32[]{:S(2)}) collective-permute-start(bf16[1,128,1024]{2,1,0:T(8,128)(2,1)S(1)} %maximum_bitcast_fusion), channel_id=1, source_target_pairs={{0,8},{1,3},{2,10},{3,1},{4,12},{5,7},{6,14},{7,5},{8,0},{9,11},{1... | collective-permute-start | bytes 786440 | tf_op jit(solution)/shard_map/ppermute | solution.py:78
  9.1 1.8 collective-permute-start.1
  9.3 17.5 %collective-permute-start.5 = (bf16[1,256,1024]{2,1,0:T(8,128)(2,1)S(1)}, bf16[1,256,1024]{2,1,0:T(8,128)(2,1)S(1)}, u32[]{:S(2)}, u32[]{:S(2)}) collective-permute-start(bf16[1,256,1024]{2,1,0:T(8,128)(2,1)S(1)} %broadcast_select_fusion.10), channel_id=1, source_target_pairs={{0,2},{2,0},{4,6},{6,4},{8,10},{10,8},{12,14},{14,12},{1,3},{3,1},... | collective-permute-start | bytes 1572872 | tf_op jit(solution)/shard_map/ppermute | solution.py:106
  16.4 25.3 %collective-permute-start.3 = (bf16[2,128,1024]{2,1,0:T(8,128)(2,1)S(1)}, bf16[2,128,1024]{2,1,0:T(8,128)(2,1)S(1)}, u32[]{:S(2)}, u32[]{:S(2)}) collective-permute-start(bf16[2,128,1024]{2,1,0:T(8,128)(2,1)S(1)} %constant_dynamic-update-slice_fusion), channel_id=1, source_target_pairs={{0,4},{1,9},{2,6},{3,11},{4,0},{5,13},{6,2},{7,15},{8,12},{9,1},{1... | collective-permute-start | bytes 1572872 | tf_op jit(solution)/shard_map/ppermute | solution.py:78
  23.1 18.6 %collective-permute-start.4 = (bf16[1,128,1024]{2,1,0:T(8,128)(2,1)S(1)}, bf16[1,128,1024]{2,1,0:T(8,128)(2,1)S(1)}, u32[]{:S(2)}, u32[]{:S(2)}) collective-permute-start(bf16[1,128,1024]{2,1,0:T(8,128)(2,1)S(1)} %maximum_bitcast_fusion.1), channel_id=1, source_target_pairs={{0,8},{1,3},{2,10},{3,1},{4,12},{5,7},{6,14},{7,5},{8,0},{9,11},{1... | collective-permute-start | bytes 786440 | tf_op jit(solution)/shard_map/ppermute | solution.py:78
  26.8 8.6 %collective-permute-start.6 = (bf16[1,64,1024]{2,1,0:T(8,128)(2,1)S(1)}, bf16[1,64,1024]{2,1,0:T(8,128)(2,1)S(1)}, u32[]{:S(2)}, u32[]{:S(2)}) collective-permute-start(bf16[1,64,1024]{2,1,0:T(8,128)(2,1)S(1)} %slice.178), channel_id=1, source_target_pairs={{0,4},{2,6},{4,8},{6,10},{8,12},{10,14},{1,5},{3,7},{5,9},{7,11},{... | collective-permute-start | bytes 393224 | tf_op jit(solution)/shard_map/ppermute | solution.py:99
  28.8 9.9 %collective-permute-start.7 = (bf16[1,64,1024]{2,1,0:T(8,128)(2,1)S(1)}, bf16[1,64,1024]{2,1,0:T(8,128)(2,1)S(1)}, u32[]{:S(2)}, u32[]{:S(2)}) collective-permute-start(bf16[1,64,1024]{2,1,0:T(8,128)(2,1)S(1)} %slice.179), channel_id=1, source_target_pairs={{4,0},{6,2},{8,4},{10,6},{12,8},{14,10},{5,1},{7,3},{9,5},{11,7},{... | collective-permute-start | bytes 393224 | tf_op jit(solution)/shard_map/ppermute | solution.py:100
  41.8 16.7 %collective-permute-start.8 = (bf16[4,128,1024]{2,1,0:T(8,128)(2,1)S(1)}, bf16[4,128,1024]{2,1,0:T(8,128)(2,1)S(1)}, u32[]{:S(2)}, u32[]{:S(2)}) collective-permute-start(bf16[4,128,1024]{2,1,0:T(8,128)(2,1)S(1)} %pad_maximum_fusion.2), channel_id=1, source_target_pairs={{0,2},{1,5},{2,0},{3,7},{4,6},{5,1},{6,4},{7,3},{8,10},{9,13},{10,... | collective-permute-start | bytes 3145736 | tf_op jit(solution)/shard_map/ppermute | solution.py:78
  42.0 16.6 %collective-permute-start.9 = (bf16[2,128,1024]{2,1,0:T(8,128)(2,1)S(1)}, bf16[2,128,1024]{2,1,0:T(8,128)(2,1)S(1)}, u32[]{:S(2)}, u32[]{:S(2)}) collective-permute-start(bf16[2,128,1024]{2,1,0:T(8,128)(2,1)S(1)} %pad_maximum_fusion.6), channel_id=1, source_target_pairs={{0,4},{1,9},{2,6},{3,11},{4,0},{5,13},{6,2},{7,15},{8,12},{9,1},{1... | collective-permute-start | bytes 1572872 | tf_op jit(solution)/shard_map/ppermute | solution.py:78
  58.6 7.6 %collective-permute-start.11 = (bf16[8,128,1024]{2,1,0:T(8,128)(2,1)S(1)}, bf16[8,128,1024]{2,1,0:T(8,128)(2,1)S(1)}, u32[]{:S(2)}, u32[]{:S(2)}) collective-permute-start(bf16[8,128,1024]{2,1,0:T(8,128)(2,1)S(1)} %constant_dynamic-update-slice_fusion.2.own.refs_7_.refs_5_), channel_id=1, source_target_pairs={{0,1},{1,0},{2,3},{3,2},{4,5},{5,4},{6,7},{7,6},{8,9},{9,8},{10,11... | collective-permute-start | bytes 6291464 | tf_op jit(solution)/shard_map/ppermute | solution.py:68
  62.5 15.9 %collective-permute-start.10 = (bf16[4,128,1024]{2,1,0:T(8,128)(2,1)S(1)}, bf16[4,128,1024]{2,1,0:T(8,128)(2,1)S(1)}, u32[]{:S(2)}, u32[]{:S(2)}) collective-permute-start(bf16[4,128,1024]{2,1,0:T(8,128)(2,1)S(1)} %pad_maximum_fusion.3), channel_id=1, source_target_pairs={{0,2},{1,5},{2,0},{3,7},{4,6},{5,1},{6,4},{7,3},{8,10},{9,13},{10,... | collective-permute-start | bytes 3145736 | tf_op jit(solution)/shard_map/ppermute | solution.py:78
  78.7 16.0 %collective-permute-start.15 = (bf16[8,128,1024]{2,1,0:T(8,128)(2,1)S(1)}, bf16[8,128,1024]{2,1,0:T(8,128)(2,1)S(1)}, u32[]{:S(2)}, u32[]{:S(2)}) collective-permute-start(bf16[8,128,1024]{2,1,0:T(8,128)(2,1)S(1)} %pad_maximum_fusion.own.refs_5_), channel_id=1, source_target_pairs={{0,1},{1,0},{2,3},{3,2},{4,5},{5,4},{6,7},{7,6},{8,9},{9,8},{10,11... | collective-permute-start | bytes 6291464 | tf_op jit(solution)/shard_map/ppermute | solution.py:68
  79.7 14.7 %collective-permute-start.14 = (bf16[1,256,1024]{2,1,0:T(8,128)(2,1)S(1)}, bf16[1,256,1024]{2,1,0:T(8,128)(2,1)S(1)}, u32[]{:S(2)}, u32[]{:S(2)}) collective-permute-start(bf16[1,256,1024]{2,1,0:T(8,128)(2,1)S(1)} %broadcast_select_fusion.6), channel_id=1, source_target_pairs={{0,2},{2,0},{4,6},{6,4},{8,10},{10,8},{12,14},{14,12},{1,3},{3,1},... | collective-permute-start | bytes 1572872 | tf_op jit(solution)/shard_map/ppermute | solution.py:106
  81.8 12.8 %collective-permute-start.13 = (bf16[1,128,1024]{2,1,0:T(8,128)(2,1)S(1)}, bf16[1,128,1024]{2,1,0:T(8,128)(2,1)S(1)}, u32[]{:S(2)}, u32[]{:S(2)}) collective-permute-start(bf16[1,128,1024]{2,1,0:T(8,128)(2,1)S(1)} %get-tuple-element.81.first), channel_id=1, source_target_pairs={{4,0},{6,2},{8,4},{10,6},{12,8},{14,10},{5,1},{7,3},{9,5},{11,7},{... | collective-permute-start | bytes 786440 | tf_op jit(solution)/shard_map/ppermute | solution.py:100
  83.1 11.5 %collective-permute-start.12 = (bf16[1,128,1024]{2,1,0:T(8,128)(2,1)S(1)}, bf16[1,128,1024]{2,1,0:T(8,128)(2,1)S(1)}, u32[]{:S(2)}, u32[]{:S(2)}) collective-permute-start(bf16[1,128,1024]{2,1,0:T(8,128)(2,1)S(1)} %get-tuple-element.82.last), channel_id=1, source_target_pairs={{0,4},{2,6},{4,8},{6,10},{8,12},{10,14},{1,5},{3,7},{5,9},{7,11},{... | collective-permute-start | bytes 786440 | tf_op jit(solution)/shard_map/ppermute | solution.py:99
  98.5 9.3 %collective-permute-start.16 = (bf16[1,128,512]{2,1,0:T(8,128)(2,1)S(1)}, bf16[1,128,512]{2,1,0:T(8,128)(2,1)S(1)}, u32[]{:S(2)}, u32[]{:S(2)}) collective-permute-start(bf16[1,128,512]{2,1,0:T(8,128)(2,1)S(1)} %get-tuple-element.90), channel_id=1, source_target_pairs={{0,4},{2,6},{4,8},{6,10},{8,12},{10,14},{1,5},{3,7},{5,9},{7,11},{... | collective-permute-start | bytes 393224 | tf_op jit(solution)/shard_map/ppermute | solution.py:99
  102.8 6.9 %collective-permute-start.17 = (bf16[1,128,512]{2,1,0:T(8,128)(2,1)S(1)}, bf16[1,128,512]{2,1,0:T(8,128)(2,1)S(1)}, u32[]{:S(2)}, u32[]{:S(2)}) collective-permute-start(bf16[1,128,512]{2,1,0:T(8,128)(2,1)S(1)} %get-tuple-element.91), channel_id=1, source_target_pairs={{4,0},{6,2},{8,4},{10,6},{12,8},{14,10},{5,1},{7,3},{9,5},{11,7},{... | collective-permute-start | bytes 393224 | tf_op jit(solution)/shard_map/ppermute | solution.py:100
  109.7 7.5 %collective-permute-start.18 = (bf16[8,128,1024]{2,1,0:T(8,128)(2,1)S(1)}, bf16[8,128,1024]{2,1,0:T(8,128)(2,1)S(1)}, u32[]{:S(2)}, u32[]{:S(2)}) collective-permute-start(bf16[8,128,1024]{2,1,0:T(8,128)(2,1)S(1)} %get-tuple-element.93), channel_id=1, source_target_pairs={{0,1},{1,0},{2,3},{3,2},{4,5},{5,4},{6,7},{7,6},{8,9},{9,8},{10,11... | collective-permute-start | bytes 6291464 | tf_op jit(solution)/shard_map/ppermute | solution.py:68
  121.6 4.4 %collective-permute-start.19 = (bf16[8,128,1024]{2,1,0:T(8,128)(2,1)S(1)}, bf16[8,128,1024]{2,1,0:T(8,128)(2,1)S(1)}, u32[]{:S(2)}, u32[]{:S(2)}) collective-permute-start(bf16[8,128,1024]{2,1,0:T(8,128)(2,1)S(1)} %get-tuple-element.105), channel_id=1, source_target_pairs={{0,1},{1,0},{2,3},{3,2},{4,5},{5,4},{6,7},{7,6},{8,9},{9,8},{10,11... | collective-permute-start | bytes 6291464 | tf_op jit(solution)/shard_map/ppermute | solution.py:68
  122.4 14.9 %collective-permute-start.20 = (bf16[4,128,1024]{2,1,0:T(8,128)(2,1)S(1)}, bf16[4,128,1024]{2,1,0:T(8,128)(2,1)S(1)}, u32[]{:S(2)}, u32[]{:S(2)}) collective-permute-start(bf16[4,128,1024]{2,1,0:T(8,128)(2,1)S(1)} %slice.274), channel_id=1, source_target_pairs={{0,2},{1,5},{2,0},{3,7},{4,6},{5,1},{6,4},{7,3},{8,10},{9,13},{10,... | collective-permute-start | bytes 3145736 | tf_op jit(solution)/shard_map/ppermute | solution.py:78
  127.2 26.5 %collective-permute-start.23 = (bf16[4,128,1024]{2,1,0:T(8,128)(2,1)S(1)}, bf16[4,128,1024]{2,1,0:T(8,128)(2,1)S(1)}, u32[]{:S(2)}, u32[]{:S(2)}) collective-permute-start(bf16[4,128,1024]{2,1,0:T(8,128)(2,1)S(1)} %slice.273), channel_id=1, source_target_pairs={{0,2},{1,5},{2,0},{3,7},{4,6},{5,1},{6,4},{7,3},{8,10},{9,13},{10,... | collective-permute-start | bytes 3145736 | tf_op jit(solution)/shard_map/ppermute | solution.py:78
  137.2 5.6 %collective-permute-start.21 = (bf16[1,64,512]{2,1,0:T(8,128)(2,1)S(1)}, bf16[1,64,512]{2,1,0:T(8,128)(2,1)S(1)}, u32[]{:S(2)}, u32[]{:S(2)}) collective-permute-start(bf16[1,64,512]{2,1,0:T(8,128)(2,1)S(1)} %get-tuple-element.108), channel_id=1, source_target_pairs={{0,4},{2,6},{4,8},{6,10},{8,12},{10,14},{1,5},{3,7},{5,9},{7,11},{... | collective-permute-start | bytes 196616 | tf_op jit(solution)/shard_map/ppermute | solution.py:99
  140.3 6.9 %collective-permute-start.22 = (bf16[1,64,512]{2,1,0:T(8,128)(2,1)S(1)}, bf16[1,64,512]{2,1,0:T(8,128)(2,1)S(1)}, u32[]{:S(2)}, u32[]{:S(2)}) collective-permute-start(bf16[1,64,512]{2,1,0:T(8,128)(2,1)S(1)} %get-tuple-element.109), channel_id=1, source_target_pairs={{4,0},{6,2},{8,4},{10,6},{12,8},{14,10},{5,1},{7,3},{9,5},{11,7},{... | collective-permute-start | bytes 196616 | tf_op jit(solution)/shard_map/ppermute | solution.py:100
  154.6 14.0 %collective-permute-start.24 = (bf16[2,128,1024]{2,1,0:T(8,128)(2,1)S(1)}, bf16[2,128,1024]{2,1,0:T(8,128)(2,1)S(1)}, u32[]{:S(2)}, u32[]{:S(2)}) collective-permute-start(bf16[2,128,1024]{2,1,0:T(8,128)(2,1)S(1)} %slice.276), channel_id=1, source_target_pairs={{0,4},{1,9},{2,6},{3,11},{4,0},{5,13},{6,2},{7,15},{8,12},{9,1},{1... | collective-permute-start | bytes 1572872 | tf_op jit(solution)/shard_map/ppermute | solution.py:78
  154.7 24.6 %collective-permute-start.25 = (bf16[2,128,1024]{2,1,0:T(8,128)(2,1)S(1)}, bf16[2,128,1024]{2,1,0:T(8,128)(2,1)S(1)}, u32[]{:S(2)}, u32[]{:S(2)}) collective-permute-start(bf16[2,128,1024]{2,1,0:T(8,128)(2,1)S(1)} %slice.275), channel_id=1, source_target_pairs={{0,4},{1,9},{2,6},{3,11},{4,0},{5,13},{6,2},{7,15},{8,12},{9,1},{1... | collective-permute-start | bytes 1572872 | tf_op jit(solution)/shard_map/ppermute | solution.py:78
  179.5 9.2 %collective-permute-start.26 = (bf16[1,128,1024]{2,1,0:T(8,128)(2,1)S(1)}, bf16[1,128,1024]{2,1,0:T(8,128)(2,1)S(1)}, u32[]{:S(2)}, u32[]{:S(2)}) collective-permute-start(bf16[1,128,1024]{2,1,0:T(8,128)(2,1)S(1)} %slice.278), channel_id=1, source_target_pairs={{0,8},{1,3},{2,10},{3,1},{4,12},{5,7},{6,14},{7,5},{8,0},{9,11},{1... | collective-permute-start | bytes 786440 | tf_op jit(solution)/shard_map/ppermute | solution.py:78
  179.7 13.8 %collective-permute-start.29 = (bf16[1,256,1024]{2,1,0:T(8,128)(2,1)S(1)}, bf16[1,256,1024]{2,1,0:T(8,128)(2,1)S(1)}, u32[]{:S(2)}, u32[]{:S(2)}) collective-permute-start(bf16[1,256,1024]{2,1,0:T(8,128)(2,1)S(1)} %broadcast_select_fusion.2), channel_id=1, source_target_pairs={{0,2},{2,0},{4,6},{6,4},{8,10},{10,8},{12,14},{14,12},{1,3},{3,1},... | collective-permute-start | bytes 1572872 | tf_op jit(solution)/shard_map/ppermute | solution.py:106
  188.8 3.1 %collective-permute-start.27 = (f32[64,1024]{1,0:T(8,128)S(1)}, f32[64,1024]{1,0:T(8,128)S(1)}, u32[]{:S(2)}, u32[]{:S(2)}) collective-permute-start(f32[64,1024]{1,0:T(8,128)S(1)} %fusion.1), channel_id=1, source_target_pairs={{0,1},{1,0},{2,3},{3,2},{4,5},{5,4},{6,7},{7,6},{8,9},{9,8},{10,11... | collective-permute-start | bytes 786440 | tf_op jit(solution)/shard_map/ppermute | solution.py:68
  191.0 8.7 %collective-permute-start.28 = (bf16[1,128,1024]{2,1,0:T(8,128)(2,1)S(1)}, bf16[1,128,1024]{2,1,0:T(8,128)(2,1)S(1)}, u32[]{:S(2)}, u32[]{:S(2)}) collective-permute-start(bf16[1,128,1024]{2,1,0:T(8,128)(2,1)S(1)} %slice.277), channel_id=1, source_target_pairs={{0,8},{1,3},{2,10},{3,1},{4,12},{5,7},{6,14},{7,5},{8,0},{9,11},{1... | collective-permute-start | bytes 786440 | tf_op jit(solution)/shard_map/ppermute | solution.py:78
  199.9 1.6 collective-permute-start.30
  (3 other events, 14.0 us)

commit v4 on v3

--- a/solution.py
+++ b/solution.py
@@ -53,7 +53,7 @@
 def step_orders(count):
     bits = [1 << i for i in reversed(range(count.bit_length() - 1))]
     assert math.prod([2] * len(bits)) == count
-    return bits, bits[-1:] + bits[:-1]
+    return bits[:-2] + bits[:-3:-1], bits
 
 
 def place_of(offset, steps):
@@ -458,6 +458,7 @@
 def body(activations, cotangent, conv_one, mix_one, conv_two, mix_two):
     count = lax.axis_size("seq")
     orders = step_orders(count)
+    sum_orders = orders
     last_step = len(orders[0]) - 1
     middle = conv_one.shape[2]
     leading = lax.axis_index("dp") == 0
@@ -482,23 +483,26 @@
     low, high = halo(x[:, :DILATE_ONE], x[:, length - DILATE_ONE :])
     mine_e, gives_e = split_pair(cotangent, 0)
     got_e = swap_pair(gives_e)
-    ext_one = norm_ext(x, low, high)
-    got_one, got_two, ext_one = tie(got_one, got_two, ext_one)
+    got_one, got_two = tie(got_one, got_two)
     for j in range(2, last_step + 1):
         own_one, own_two = widen(own_one, got_one), widen(own_two, got_two)
-        got_one, got_two = tie(hop(own_one, orders, j), hop(own_two, orders, j - 1))
+        got_one, got_two = hop(own_one, orders, j), hop(own_two, orders, j - 1)
+        if j == last_step:
+            ext_one = norm_ext(x, low, high)
+            e = join_pair(mine_e, got_e, 1)
+            ext_one, e, got_one, got_two = tie(ext_one, e, got_one, got_two)
+        got_one, got_two = tie(got_one, got_two)
     own_one = widen(own_one, got_one)
     got_one = cross(own_one)
     own_one, got_two = tie(own_one, got_two)
     own_two = widen(own_two, got_two)
     got_two = hop(own_two, orders, last_step)
-    e = join_pair(mine_e, got_e, 1)
     pieces_one = (own_one, got_one)
     pre_one, hid_one, second_in, first, last = forward_block(
         ext_one, x, pieces_one, orders, DILATE_ONE, DILATE_TWO
     )
     low, high = halo(first, last)
-    got_two, first, last = tie(got_two, first, last)
+    got_two, low, high = tie(got_two, low, high)
     own_two = widen(own_two, got_two)
     pieces_two = (own_two, cross(own_two))
     ext_two, hid_two, dpre_two, dfirst, dlast = turn_block(
@@ -506,39 +510,41 @@
     )
 
     dlow, dhigh = halo(dfirst, dlast)
-    keep_two, send = grads_block(ext_two, hid_two, e, dpre_two, orders, DILATE_TWO, count)
+    keep_two, send = grads_block(
+        ext_two, hid_two, e, dpre_two, sum_orders, DILATE_TWO, count
+    )
     dlow, dhigh, send = tie(dlow, dhigh, send)
     got_two = cross(send)
+    total_two = fold_all(keep_two, got_two)
+    total_two, dlow, dhigh = tie(total_two, dlow, dhigh)
+    got_two = give(total_two, sum_orders, last_step)
     upstream, dpre_one, dfirst, dlast = back_block(
         dpre_two, dlow, dhigh, second_in, e, pieces_two, orders, DILATE_TWO,
         (pieces_one, pre_one, DILATE_ONE),
     )
-    got_two, dpre_one, upstream = tie(got_two, dpre_one, upstream)
-    total_two = fold_all(keep_two, got_two)
-    got_two = give(total_two, orders, last_step)
-    total_two, dpre_one = tie(total_two, dpre_one)
     keep_one, send = grads_block(ext_one, hid_one, upstream, dpre_one, orders, DILATE_ONE, count)
+    got_two, send, dfirst, dlast = tie(got_two, send, dfirst, dlast)
     got_one = cross(send)
-    dfirst, dlast, send, got_two = tie(dfirst, dlast, send, got_two)
     dlow, dhigh = halo(dfirst, dlast)
+    total_two = fold(total_two, got_two)
+    got_two = give(total_two, sum_orders, last_step - 1)
     total_one = fold_all(keep_one, got_one)
+    total_one, total_two, dlow, dhigh = tie(total_one, total_two, dlow, dhigh)
     got_one = give(total_one, orders, last_step)
-    total_one, dlow, dhigh, got_two = tie(total_one, dlow, dhigh, got_two)
     (input_grad,) = back_block(
         dpre_one, dlow, dhigh, x, upstream, pieces_one, orders, DILATE_ONE
     )
     input_grad, got_one, got_two = tie(input_grad, got_one, got_two)
     mine_g, gives_g = split_pair(input_grad, 1)
     for j in reversed(range(last_step)):
-        total_two = fold(total_two, got_two)
-        got_two = give(total_two, orders, j)
+        if j < last_step - 1:
+            total_two = fold(total_two, got_two)
+            got_two = give(total_two, sum_orders, j)
         total_one = fold(total_one, got_one)
         got_one = give(total_one, orders, j)
         if j == last_step - 1:
             total_one, gives_g = tie(total_one, gives_g)
             got_g = swap_pair(gives_g)
-        if j > 0:
-            got_one, got_two = tie(got_one, got_two)
     total_two = fold(total_two, got_two)
     grads_two = unpack(total_two[0], middle)
     grads_two, got_one, got_g = tie(grads_two, got_one, got_g)

time: 203 us -> 191 us (0.941)
  starting transfers between devices: 55.7 us -> 40.5 us
  waiting for transfers between devices: 101 us -> 105 us
    ppermute x12, waiting for transfers between devices: 75.6 us -> 58.5 us  [hop(): return lax.ppermute(value, ('seq', 'dp'), pairs)]
    ppermute x8, waiting for transfers between devices: 4.37 us -> 13.6 us  [cross(): return lax.ppermute(value, 'dp', [(0, 1), (1, 0)])]
    ppermute x12, starting transfers between devices: 23.5 us -> 15.1 us  [hop(): return lax.ppermute(value, ('seq', 'dp'), pairs)]
    ppermute x8, starting transfers between devices: 7.3 us -> 0.92 us  [cross(): return lax.ppermute(value, 'dp', [(0, 1), (1, 0)])]
    ppermute x3, waiting for transfers between devices: 5.38 us -> 11.4 us  [swap_pair(): return lax.ppermute(value, 'seq', [(i, i ^ 1) for i in range(count)])]
    ppermute x4, waiting for transfers between devices: 6.53 us -> 10.6 us  [halo(): low = lax.ppermute(last, 'seq', [(i, i + 2) for i in range(count - 2)])]
  transfers between devices with their start and end apart: 31 -> 31, of which waited for: 19 -> 21; matrix products, arithmetic and copies ran while one was open for 3% -> 3% of each run, Pallas kernels for 12% -> 15%
where the time goes in v4:
time: 191 us
  waiting for transfers between devices  105 us (55%)
  starting transfers between devices  40.5 us (21%)
  Pallas kernels  31.6 us (17%)
  other arithmetic  8.73 us (5%)
  local copies, waits for them, and re-layouts  3.5 us (2%)
    ppermute x12, waiting for transfers between devices, hop(): return lax.ppermute(value, ('seq', 'dp'), pairs)  58.5 us
    ppermute x12, starting transfers between devices, hop(): return lax.ppermute(value, ('seq', 'dp'), pairs)  15.1 us
    ppermute x4, starting transfers between devices, halo(): low = lax.ppermute(last, 'seq', [(i, i + 2) for i in range(count - 2)])  14.4 us
    pallas_call x2, Pallas kernels, back_block(): pl.pallas_call(functools.partial(back_kernel, orders, dilate, chained), o...  13.9 us
    ppermute x8, waiting for transfers between devices, cross(): return lax.ppermute(value, 'dp', [(0, 1), (1, 0)])  13.6 us
    ppermute x4, waiting for transfers between devices, halo(): high = lax.ppermute(first, 'seq', [(i + 2, i) for i in range(count - 2)])  11.4 us
    ppermute x3, waiting for transfers between devices, swap_pair(): return lax.ppermute(value, 'seq', [(i, i ^ 1) for i in range(count)])  11.4 us
    ppermute x4, waiting for transfers between devices, halo(): low = lax.ppermute(last, 'seq', [(i, i + 2) for i in range(count - 2)])  10.6 us
  transfers between devices with their start and end apart: 31, of which 21 were waited for; matrix products, arithmetic and copies ran while one was open for 3% of the time, Pallas kernels for 15%

profile of v4, /device:TPU:0, one launch (start us, length us, event | category | flops | bytes accessed | tf_op | source)
XLA Modules:
  0.0 191.0 jit_solution(17103508651579690200)
XLA Ops:
  5.0 4.0 %collective-permute-start.1 = (bf16[1,128,1024]{2,1,0:T(8,128)(2,1)S(1)}, bf16[1,128,1024]{2,1,0:T(8,128)(2,1)S(1)}, u32[]{:S(2)}, u32[]{:S(2)}) collective-permute-start(bf16[1,128,1024]{2,1,0:T(8,128)(2,1)S(1)} %maximum_bitcast_fusion), channel_id=1, source_target_pairs={{0,8},{1,9},{2,10},{3,11},{4,12},{5,13},{6,14},{7,15},{8,0},{9,1},... | collective-permute-start | bytes 786440 | tf_op jit(solution)/shard_map/ppermute | solution.py:78
  10.9 10.4 %collective-permute-done.1 = bf16[1,128,1024]{2,1,0:T(8,128)(2,1)S(1)} collective-permute-done((bf16[1,128,1024]{2,1,0:T(8,128)(2,1)S(1)}, bf16[1,128,1024]{2,1,0:T(8,128)(2,1)S(1)}, u32[]{:S(2)}, u32[]{:S(2)}) %collective-permute-start.1) | collective-permute-done | bytes 262176 | tf_op jit(solution)/shard_map/ppermute | solution.py:78
  25.3 12.2 %collective-permute-done.8 = bf16[1,128,1024]{2,1,0:T(8,128)(2,1)S(1)} collective-permute-done((bf16[1,128,1024]{2,1,0:T(8,128)(2,1)S(1)}, bf16[1,128,1024]{2,1,0:T(8,128)(2,1)S(1)}, u32[]{:S(2)}, u32[]{:S(2)}) %collective-permute-start.8) | collective-permute-done | bytes 262176 | tf_op jit(solution)/shard_map/ppermute | solution.py:78
  37.9 3.9 %collective-permute-start.3 = (bf16[1,64,1024]{2,1,0:T(8,128)(2,1)S(1)}, bf16[1,64,1024]{2,1,0:T(8,128)(2,1)S(1)}, u32[]{:S(2)}, u32[]{:S(2)}) collective-permute-start(bf16[1,64,1024]{2,1,0:T(8,128)(2,1)S(1)} %slice.178), channel_id=1, source_target_pairs={{0,4},{2,6},{4,8},{6,10},{8,12},{10,14},{1,5},{3,7},{5,9},{7,11},{... | collective-permute-start | bytes 393224 | tf_op jit(solution)/shard_map/ppermute | solution.py:99
  43.2 10.6 %collective-permute-done.3.low_ref = bf16[1,64,1024]{2,1,0:T(8,128)(2,1)S(1)} collective-permute-done((bf16[1,64,1024]{2,1,0:T(8,128)(2,1)S(1)}, bf16[1,64,1024]{2,1,0:T(8,128)(2,1)S(1)}, u32[]{:S(2)}, u32[]{:S(2)}) %collective-permute-start.3) | collective-permute-done | bytes 131104 | tf_op jit(solution)/shard_map/ppermute | solution.py:99
  53.8 2.8 %collective-permute-done.4.high_ref = bf16[1,64,1024]{2,1,0:T(8,128)(2,1)S(1)} collective-permute-done((bf16[1,64,1024]{2,1,0:T(8,128)(2,1)S(1)}, bf16[1,64,1024]{2,1,0:T(8,128)(2,1)S(1)}, u32[]{:S(2)}, u32[]{:S(2)}) %collective-permute-start.4) | collective-permute-done | bytes 131104 | tf_op jit(solution)/shard_map/ppermute | solution.py:100
  56.5 3.0 %norm_ext.1.ext = bf16[1,640,1024]{2,1,0:T(8,128)(2,1)S(1)} custom-call(bf16[1,512,1024]{2,1,0:T(8,128)(2,1)S(1)} %pad_maximum_fusion.1.x_ref.refs_3_, bf16[1,64,1024]{2,1,0:T(8,128)(2,1)S(1)} %collective-permute-done.3.low_ref, bf16[1,64,1024]{2,1,0:T(8,128)(2,1)S(1)} %collective-permute-done.4.high_ref), custom_call_target="tpu_custom_call" | custom-call | tf_op jit(solution)/shard_map/norm_ext/pallas_call | solution.py:189
  59.6 2.5 %collective-permute-start.10 = (bf16[2,128,1024]{2,1,0:T(8,128)(2,1)S(1)}, bf16[2,128,1024]{2,1,0:T(8,128)(2,1)S(1)}, u32[]{:S(2)}, u32[]{:S(2)}) collective-permute-start(bf16[2,128,1024]{2,1,0:T(8,128)(2,1)S(1)} %pad_maximum_fusion.6), channel_id=1, source_target_pairs={{0,2},{1,5},{2,0},{3,7},{4,6},{5,1},{6,4},{7,3},{8,10},{9,13},{10,... | collective-permute-start | bytes 1572872 | tf_op jit(solution)/shard_map/ppermute | solution.py:78
  62.4 6.9 %collective-permute-done.10 = bf16[2,128,1024]{2,1,0:T(8,128)(2,1)S(1)} collective-permute-done((bf16[2,128,1024]{2,1,0:T(8,128)(2,1)S(1)}, bf16[2,128,1024]{2,1,0:T(8,128)(2,1)S(1)}, u32[]{:S(2)}, u32[]{:S(2)}) %collective-permute-start.10) | collective-permute-done | bytes 524320 | tf_op jit(solution)/shard_map/ppermute | solution.py:78
  69.7 4.0 %collective-permute-done.11.other.refs_8_.refs_6_ = bf16[8,128,1024]{2,1,0:T(8,128)(2,1)S(1)} collective-permute-done((bf16[8,128,1024]{2,1,0:T(8,128)(2,1)S(1)}, bf16[8,128,1024]{2,1,0:T(8,128)(2,1)S(1)}, u32[]{:S(2)}, u32[]{:S(2)}) %collective-permute-start.11) | collective-permute-done | bytes 2097184 | tf_op jit(solution)/shard_map/ppermute | solution.py:68
  73.7 3.7 %forward_block.1 = (f32[512,512]{1,0:T(8,128)S(1)}, bf16[512,512]{1,0:T(8,128)(2,1)S(1)}, bf16[1,512,1024]{2,1,0:T(8,128)(2,1)S(1)}, bf16[1,128,1024]{2,1,0:T(8,128)(2,1)S(1)}, bf16[1,128,1024]{2,1,0:T(8,128)(2,1)S(1)}) custom-call(bf16[1,640,1024]{2,1,0:T(8,128)(2,1)S(1)} %norm_ext.1.ext, bf16[1,512,1024]{2,1,0:T(8,128)(2,1)S(1)} %pad_maximum_fusion.1.x_ref.refs_3_, ...), custom_call_target="tpu_custom_call" | custom-call | flops 2147483648 | bytes 8388608 | tf_op jit(solution)/shard_map/forward_block/pallas_call | solution.py:227
  78.7 4.6 %collective-permute-start.13 = (bf16[1,128,1024]{2,1,0:T(8,128)(2,1)S(1)}, bf16[1,128,1024]{2,1,0:T(8,128)(2,1)S(1)}, u32[]{:S(2)}, u32[]{:S(2)}) collective-permute-start(bf16[1,128,1024]{2,1,0:T(8,128)(2,1)S(1)} %get-tuple-element.82.last), channel_id=1, source_target_pairs={{0,4},{2,6},{4,8},{6,10},{8,12},{10,14},{1,5},{3,7},{5,9},{7,11},{... | collective-permute-start | bytes 786440 | tf_op jit(solution)/shard_map/ppermute | solution.py:99
  83.2 3.7 %collective-permute-done.12 = bf16[4,128,1024]{2,1,0:T(8,128)(2,1)S(1)} collective-permute-done((bf16[4,128,1024]{2,1,0:T(8,128)(2,1)S(1)}, bf16[4,128,1024]{2,1,0:T(8,128)(2,1)S(1)}, u32[]{:S(2)}, u32[]{:S(2)}) %collective-permute-start.12) | collective-permute-done | bytes 1048608 | tf_op jit(solution)/shard_map/ppermute | solution.py:78
  86.9 3.2 %collective-permute-done.14.high = bf16[1,128,1024]{2,1,0:T(8,128)(2,1)S(1)} collective-permute-done((bf16[1,128,1024]{2,1,0:T(8,128)(2,1)S(1)}, bf16[1,128,1024]{2,1,0:T(8,128)(2,1)S(1)}, u32[]{:S(2)}, u32[]{:S(2)}) %collective-permute-start.14) | collective-permute-done | bytes 262176 | tf_op jit(solution)/shard_map/ppermute | solution.py:100
  90.4 4.1 %collective-permute-done.15.other.refs_6_ = bf16[8,128,1024]{2,1,0:T(8,128)(2,1)S(1)} collective-permute-done((bf16[8,128,1024]{2,1,0:T(8,128)(2,1)S(1)}, bf16[8,128,1024]{2,1,0:T(8,128)(2,1)S(1)}, u32[]{:S(2)}, u32[]{:S(2)}) %collective-permute-start.15) | collective-permute-done | bytes 2097184 | tf_op jit(solution)/shard_map/ppermute | solution.py:68
  94.5 3.8 %turn_block.1 = (bf16[1,768,1024]{2,1,0:T(8,128)(2,1)S(1)}, bf16[512,512]{1,0:T(8,128)(2,1)S(1)}, bf16[512,512]{1,0:T(8,128)(2,1)S(1)}, bf16[1,128,512]{2,1,0:T(8,128)(2,1)S(1)}, bf16[1,128,512]{2,1,0:T(8,128)(2,1)S(1)}) custom-call(bf16[1,128,1024]{2,1,0:T(8,128)(2,1)S(1)} %get-tuple-element.81.first, bf16[1,128,1024]{2,1,0:T(8,128)(2,1)S(1)} %get-tuple-element.82.last, ...), custom_call_target="tpu_custom_call" | custom-call | flops 2147483648 | bytes 8388608 | tf_op jit(solution)/shard_map/turn_block/pallas_call | solution.py:277
  98.4 3.1 %collective-permute-start.16 = (bf16[1,128,512]{2,1,0:T(8,128)(2,1)S(1)}, bf16[1,128,512]{2,1,0:T(8,128)(2,1)S(1)}, u32[]{:S(2)}, u32[]{:S(2)}) collective-permute-start(bf16[1,128,512]{2,1,0:T(8,128)(2,1)S(1)} %get-tuple-element.93), channel_id=1, source_target_pairs={{0,4},{2,6},{4,8},{6,10},{8,12},{10,14},{1,5},{3,7},{5,9},{7,11},{... | collective-permute-start | bytes 393224 | tf_op jit(solution)/shard_map/ppermute | solution.py:99
  102.7 3.7 %grads_block.2 = (f32[8,128,1024]{2,1,0:T(8,128)S(1)}, bf16[8,128,1024]{2,1,0:T(8,128)(2,1)S(1)}) custom-call(bf16[1,768,1024]{2,1,0:T(8,128)(2,1)S(1)} %get-tuple-element.90.ext, bf16[512,512]{1,0:T(8,128)(2,1)S(1)} %get-tuple-element.91.hid, bf16[1,512,1024]{2,1,0:T(8,128)(2,1)S(1)} %pad_maximum_fusion.2.e_ref.refs_4_, ...), custom_call_target="tpu_custom_call" | custom-call | flops 2147483648 | bytes 8388608 | tf_op jit(solution)/shard_map/grads_block/pallas_call | solution.py:343
  106.4 2.2 %collective-permute-done.17.refs_2_ = bf16[1,128,512]{2,1,0:T(8,128)(2,1)S(1)} collective-permute-done((bf16[1,128,512]{2,1,0:T(8,128)(2,1)S(1)}, bf16[1,128,512]{2,1,0:T(8,128)(2,1)S(1)}, u32[]{:S(2)}, u32[]{:S(2)}) %collective-permute-start.17) | collective-permute-done | bytes 131104 | tf_op jit(solution)/shard_map/ppermute | solution.py:100
  108.6 4.2 %collective-permute-done.18 = bf16[8,128,1024]{2,1,0:T(8,128)(2,1)S(1)} collective-permute-done((bf16[8,128,1024]{2,1,0:T(8,128)(2,1)S(1)}, bf16[8,128,1024]{2,1,0:T(8,128)(2,1)S(1)}, u32[]{:S(2)}, u32[]{:S(2)}) %collective-permute-start.18) | collective-permute-done | bytes 2097184 | tf_op jit(solution)/shard_map/ppermute | solution.py:68
  115.0 7.4 %back_block.2 = (bf16[1,512,1024]{2,1,0:T(8,128)(2,1)S(1)}, bf16[512,512]{1,0:T(8,128)(2,1)S(1)}, bf16[1,64,512]{2,1,0:T(8,128)(2,1)S(1)}, bf16[1,64,512]{2,1,0:T(8,128)(2,1)S(1)}) custom-call(bf16[512,512]{1,0:T(8,128)(2,1)S(1)} %get-tuple-element.89.dpre.refs_0_, bf16[1,128,512]{2,1,0:T(8,128)(2,1)S(1)} %collective-permute-done.16.refs_1_, ...), custom_call_target="tpu_custom_call" | custom-call | flops 2147483648 | bytes 8388608 | tf_op jit(solution)/shard_map/back_block/pallas_call | solution.py:421
  122.5 3.4 %grads_block.3 = (f32[8,128,1024]{2,1,0:T(8,128)S(1)}, bf16[8,128,1024]{2,1,0:T(8,128)(2,1)S(1)}) custom-call(bf16[1,640,1024]{2,1,0:T(8,128)(2,1)S(1)} %norm_ext.1.ext, bf16[512,512]{1,0:T(8,128)(2,1)S(1)} %get-tuple-element.103.hid, bf16[1,512,1024]{2,1,0:T(8,128)(2,1)S(1)} %get-tuple-element.104.e_ref.refs_4_, ...), custom_call_target="tpu_custom_call" | custom-call | flops 2147483648 | bytes 8388608 | tf_op jit(solution)/shard_map/grads_block/pallas_call | solution.py:343
  125.9 2.9 %collective-permute-done.19 = bf16[4,128,1024]{2,1,0:T(8,128)(2,1)S(1)} collective-permute-done((bf16[4,128,1024]{2,1,0:T(8,128)(2,1)S(1)}, bf16[4,128,1024]{2,1,0:T(8,128)(2,1)S(1)}, u32[]{:S(2)}, u32[]{:S(2)}) %collective-permute-start.19) | collective-permute-done | bytes 1048608 | tf_op jit(solution)/shard_map/ppermute | solution.py:78
  128.8 2.9 %collective-permute-start.21 = (bf16[1,64,512]{2,1,0:T(8,128)(2,1)S(1)}, bf16[1,64,512]{2,1,0:T(8,128)(2,1)S(1)}, u32[]{:S(2)}, u32[]{:S(2)}) collective-permute-start(bf16[1,64,512]{2,1,0:T(8,128)(2,1)S(1)} %get-tuple-element.112), channel_id=1, source_target_pairs={{0,4},{2,6},{4,8},{6,10},{8,12},{10,14},{1,5},{3,7},{5,9},{7,11},{... | collective-permute-start | bytes 196616 | tf_op jit(solution)/shard_map/ppermute | solution.py:99
  134.5 3.3 %collective-permute-done.22.refs_2_ = bf16[1,64,512]{2,1,0:T(8,128)(2,1)S(1)} collective-permute-done((bf16[1,64,512]{2,1,0:T(8,128)(2,1)S(1)}, bf16[1,64,512]{2,1,0:T(8,128)(2,1)S(1)}, u32[]{:S(2)}, u32[]{:S(2)}) %collective-permute-start.22) | collective-permute-done | bytes 65568 | tf_op jit(solution)/shard_map/ppermute | solution.py:100
  138.0 1.8 collective-permute-start.23
  141.4 6.5 %back_block.3 = bf16[1,512,1024]{2,1,0:T(8,128)(2,1)S(1)} custom-call(bf16[512,512]{1,0:T(8,128)(2,1)S(1)} %get-tuple-element.102.dpre.refs_0_, bf16[1,64,512]{2,1,0:T(8,128)(2,1)S(1)} %collective-permute-done.21.refs_1_, bf16[1,64,512]{2,1,0:T(8,128)(2,1)S(1)} %collective-permute-done.22.refs_2_, bf16[1,512,1024]{2,1,0:T(8,128)(2,1)S(1)} %pad_maximum_fusion.1.x_ref.refs_3_, ...), custom_call_target="tpu_custom_call" | custom-call | flops 2147483648 | bytes 8388608 | tf_op jit(solution)/shard_map/back_block/pallas_call | solution.py:421
  147.9 6.9 %collective-permute-done.24 = bf16[2,128,1024]{2,1,0:T(8,128)(2,1)S(1)} collective-permute-done((bf16[2,128,1024]{2,1,0:T(8,128)(2,1)S(1)}, bf16[2,128,1024]{2,1,0:T(8,128)(2,1)S(1)}, u32[]{:S(2)}, u32[]{:S(2)}) %collective-permute-start.24) | collective-permute-done | bytes 524320 | tf_op jit(solution)/shard_map/ppermute | solution.py:78
  154.8 3.2 %collective-permute-done.23 = bf16[4,128,1024]{2,1,0:T(8,128)(2,1)S(1)} collective-permute-done((bf16[4,128,1024]{2,1,0:T(8,128)(2,1)S(1)}, bf16[4,128,1024]{2,1,0:T(8,128)(2,1)S(1)}, u32[]{:S(2)}, u32[]{:S(2)}) %collective-permute-start.23) | collective-permute-done | bytes 1048608 | tf_op jit(solution)/shard_map/ppermute | solution.py:78
  158.3 1.7 collective-permute-start.25
  161.0 10.8 %collective-permute-done.25 = bf16[1,128,1024]{2,1,0:T(8,128)(2,1)S(1)} collective-permute-done((bf16[1,128,1024]{2,1,0:T(8,128)(2,1)S(1)}, bf16[1,128,1024]{2,1,0:T(8,128)(2,1)S(1)}, u32[]{:S(2)}, u32[]{:S(2)}) %collective-permute-start.25) | collective-permute-done | bytes 262176 | tf_op jit(solution)/shard_map/ppermute | solution.py:78
  175.5 10.9 %collective-permute-done.29 = bf16[1,256,1024]{2,1,0:T(8,128)(2,1)S(1)} collective-permute-done((bf16[1,256,1024]{2,1,0:T(8,128)(2,1)S(1)}, bf16[1,256,1024]{2,1,0:T(8,128)(2,1)S(1)}, u32[]{:S(2)}, u32[]{:S(2)}) %collective-permute-start.29) | collective-permute-done | bytes 524320 | tf_op jit(solution)/shard_map/ppermute | solution.py:106
  (107 shorter events, 31.5 us)
Async XLA Ops:
  3.4 1.5 collective-permute-start
  5.0 16.2 %collective-permute-start.1 = (bf16[1,128,1024]{2,1,0:T(8,128)(2,1)S(1)}, bf16[1,128,1024]{2,1,0:T(8,128)(2,1)S(1)}, u32[]{:S(2)}, u32[]{:S(2)}) collective-permute-start(bf16[1,128,1024]{2,1,0:T(8,128)(2,1)S(1)} %maximum_bitcast_fusion), channel_id=1, source_target_pairs={{0,8},{1,9},{2,10},{3,11},{4,12},{5,13},{6,14},{7,15},{8,0},{9,1},... | collective-permute-start | bytes 786440 | tf_op jit(solution)/shard_map/ppermute | solution.py:78
  9.1 14.6 %copy-start.1 = (bf16[2,256,1024]{2,1,0:T(8,128)(2,1)S(1)}, bf16[2,256,1024]{2,1,0:T(8,128)(2,1)}, u32[]{:S(2)}) copy-start(bf16[2,256,1024]{2,1,0:T(8,128)(2,1)} %param.7) | copy-start | bytes 3145732
  9.1 13.8 %collective-permute-start.7 = (bf16[64,1024]{1,0:T(8,128)(2,1)S(1)}, bf16[64,1024]{1,0:T(8,128)(2,1)S(1)}, u32[]{:S(2)}, u32[]{:S(2)}) collective-permute-start(bf16[64,1024]{1,0:T(8,128)(2,1)S(1)} %broadcast_select_fusion.14), channel_id=1, source_target_pairs={{0,1},{1,0},{2,3},{3,2},{4,5},{5,4},{6,7},{7,6},{8,9},{9,8},{10,11... | collective-permute-start | bytes 393224 | tf_op jit(solution)/shard_map/ppermute | solution.py:68
  9.3 14.4 %collective-permute-start.2 = (bf16[1,256,1024]{2,1,0:T(8,128)(2,1)S(1)}, bf16[1,256,1024]{2,1,0:T(8,128)(2,1)S(1)}, u32[]{:S(2)}, u32[]{:S(2)}) collective-permute-start(bf16[1,256,1024]{2,1,0:T(8,128)(2,1)S(1)} %broadcast_select_fusion.10), channel_id=1, source_target_pairs={{0,2},{2,0},{4,6},{6,4},{8,10},{10,8},{12,14},{14,12},{1,3},{3,1},... | collective-permute-start | bytes 1572872 | tf_op jit(solution)/shard_map/ppermute | solution.py:106
  21.3 16.2 %collective-permute-start.6 = (bf16[2,128,1024]{2,1,0:T(8,128)(2,1)S(1)}, bf16[2,128,1024]{2,1,0:T(8,128)(2,1)S(1)}, u32[]{:S(2)}, u32[]{:S(2)}) collective-permute-start(bf16[2,128,1024]{2,1,0:T(8,128)(2,1)S(1)} %constant_dynamic-update-slice_fusion), channel_id=1, source_target_pairs={{0,2},{1,5},{2,0},{3,7},{4,6},{5,1},{6,4},{7,3},{8,10},{9,13},{10,... | collective-permute-start | bytes 1572872 | tf_op jit(solution)/shard_map/ppermute | solution.py:78
  23.0 14.5 %collective-permute-start.8 = (bf16[1,128,1024]{2,1,0:T(8,128)(2,1)S(1)}, bf16[1,128,1024]{2,1,0:T(8,128)(2,1)S(1)}, u32[]{:S(2)}, u32[]{:S(2)}) collective-permute-start(bf16[1,128,1024]{2,1,0:T(8,128)(2,1)S(1)} %maximum_bitcast_fusion.1), channel_id=1, source_target_pairs={{0,8},{1,9},{2,10},{3,11},{4,12},{5,13},{6,14},{7,15},{8,0},{9,1},... | collective-permute-start | bytes 786440 | tf_op jit(solution)/shard_map/ppermute | solution.py:78
  23.7 38.5 %collective-permute-start.5 = (bf16[1,256,1024]{2,1,0:T(8,128)(2,1)S(1)}, bf16[1,256,1024]{2,1,0:T(8,128)(2,1)S(1)}, u32[]{:S(2)}, u32[]{:S(2)}) collective-permute-start(bf16[1,256,1024]{2,1,0:T(8,128)(2,1)S(1)} %broadcast_select_fusion.6), channel_id=1, source_target_pairs={{0,2},{2,0},{4,6},{6,4},{8,10},{10,8},{12,14},{14,12},{1,3},{3,1},... | collective-permute-start | bytes 1572872 | tf_op jit(solution)/shard_map/ppermute | solution.py:106
  37.6 31.7 %collective-permute-start.9 = (bf16[4,128,1024]{2,1,0:T(8,128)(2,1)S(1)}, bf16[4,128,1024]{2,1,0:T(8,128)(2,1)S(1)}, u32[]{:S(2)}, u32[]{:S(2)}) collective-permute-start(bf16[4,128,1024]{2,1,0:T(8,128)(2,1)S(1)} %pad_maximum_fusion.3), channel_id=1, source_target_pairs={{0,4},{1,3},{2,6},{3,1},{4,0},{5,7},{6,2},{7,5},{8,12},{9,11},{10,... | collective-permute-start | bytes 3145736 | tf_op jit(solution)/shard_map/ppermute | solution.py:78
  37.9 15.9 %collective-permute-start.3 = (bf16[1,64,1024]{2,1,0:T(8,128)(2,1)S(1)}, bf16[1,64,1024]{2,1,0:T(8,128)(2,1)S(1)}, u32[]{:S(2)}, u32[]{:S(2)}) collective-permute-start(bf16[1,64,1024]{2,1,0:T(8,128)(2,1)S(1)} %slice.178), channel_id=1, source_target_pairs={{0,4},{2,6},{4,8},{6,10},{8,12},{10,14},{1,5},{3,7},{5,9},{7,11},{... | collective-permute-start | bytes 393224 | tf_op jit(solution)/shard_map/ppermute | solution.py:99
  41.8 14.8 %collective-permute-start.4 = (bf16[1,64,1024]{2,1,0:T(8,128)(2,1)S(1)}, bf16[1,64,1024]{2,1,0:T(8,128)(2,1)S(1)}, u32[]{:S(2)}, u32[]{:S(2)}) collective-permute-start(bf16[1,64,1024]{2,1,0:T(8,128)(2,1)S(1)} %slice.179), channel_id=1, source_target_pairs={{4,0},{6,2},{8,4},{10,6},{12,8},{14,10},{5,1},{7,3},{9,5},{11,7},{... | collective-permute-start | bytes 393224 | tf_op jit(solution)/shard_map/ppermute | solution.py:100
  59.6 9.7 %collective-permute-start.10 = (bf16[2,128,1024]{2,1,0:T(8,128)(2,1)S(1)}, bf16[2,128,1024]{2,1,0:T(8,128)(2,1)S(1)}, u32[]{:S(2)}, u32[]{:S(2)}) collective-permute-start(bf16[2,128,1024]{2,1,0:T(8,128)(2,1)S(1)} %pad_maximum_fusion.6), channel_id=1, source_target_pairs={{0,2},{1,5},{2,0},{3,7},{4,6},{5,1},{6,4},{7,3},{8,10},{9,13},{10,... | collective-permute-start | bytes 1572872 | tf_op jit(solution)/shard_map/ppermute | solution.py:78
  69.4 4.2 %collective-permute-start.11 = (bf16[8,128,1024]{2,1,0:T(8,128)(2,1)S(1)}, bf16[8,128,1024]{2,1,0:T(8,128)(2,1)S(1)}, u32[]{:S(2)}, u32[]{:S(2)}) collective-permute-start(bf16[8,128,1024]{2,1,0:T(8,128)(2,1)S(1)} %constant_dynamic-update-slice_fusion.2.own.refs_7_.refs_5_), channel_id=1, source_target_pairs={{0,1},{1,0},{2,3},{3,2},{4,5},{5,4},{6,7},{7,6},{8,9},{9,8},{10,11... | collective-permute-start | bytes 6291464 | tf_op jit(solution)/shard_map/ppermute | solution.py:68
  69.6 17.3 %collective-permute-start.12 = (bf16[4,128,1024]{2,1,0:T(8,128)(2,1)S(1)}, bf16[4,128,1024]{2,1,0:T(8,128)(2,1)S(1)}, u32[]{:S(2)}, u32[]{:S(2)}) collective-permute-start(bf16[4,128,1024]{2,1,0:T(8,128)(2,1)S(1)} %pad_maximum_fusion.4), channel_id=1, source_target_pairs={{0,4},{1,3},{2,6},{3,1},{4,0},{5,7},{6,2},{7,5},{8,12},{9,11},{10,... | collective-permute-start | bytes 3145736 | tf_op jit(solution)/shard_map/ppermute | solution.py:78
  77.4 12.7 %collective-permute-start.14 = (bf16[1,128,1024]{2,1,0:T(8,128)(2,1)S(1)}, bf16[1,128,1024]{2,1,0:T(8,128)(2,1)S(1)}, u32[]{:S(2)}, u32[]{:S(2)}) collective-permute-start(bf16[1,128,1024]{2,1,0:T(8,128)(2,1)S(1)} %get-tuple-element.81.first), channel_id=1, source_target_pairs={{4,0},{6,2},{8,4},{10,6},{12,8},{14,10},{5,1},{7,3},{9,5},{11,7},{... | collective-permute-start | bytes 786440 | tf_op jit(solution)/shard_map/ppermute | solution.py:100
  78.7 11.4 %collective-permute-start.13 = (bf16[1,128,1024]{2,1,0:T(8,128)(2,1)S(1)}, bf16[1,128,1024]{2,1,0:T(8,128)(2,1)S(1)}, u32[]{:S(2)}, u32[]{:S(2)}) collective-permute-start(bf16[1,128,1024]{2,1,0:T(8,128)(2,1)S(1)} %get-tuple-element.82.last), channel_id=1, source_target_pairs={{0,4},{2,6},{4,8},{6,10},{8,12},{10,14},{1,5},{3,7},{5,9},{7,11},{... | collective-permute-start | bytes 786440 | tf_op jit(solution)/shard_map/ppermute | solution.py:99
  90.3 4.2 %collective-permute-start.15 = (bf16[8,128,1024]{2,1,0:T(8,128)(2,1)S(1)}, bf16[8,128,1024]{2,1,0:T(8,128)(2,1)S(1)}, u32[]{:S(2)}, u32[]{:S(2)}) collective-permute-start(bf16[8,128,1024]{2,1,0:T(8,128)(2,1)S(1)} %pad_maximum_fusion.own.refs_5_), channel_id=1, source_target_pairs={{0,1},{1,0},{2,3},{3,2},{4,5},{5,4},{6,7},{7,6},{8,9},{9,8},{10,11... | collective-permute-start | bytes 6291464 | tf_op jit(solution)/shard_map/ppermute | solution.py:68
  98.4 8.1 %collective-permute-start.16 = (bf16[1,128,512]{2,1,0:T(8,128)(2,1)S(1)}, bf16[1,128,512]{2,1,0:T(8,128)(2,1)S(1)}, u32[]{:S(2)}, u32[]{:S(2)}) collective-permute-start(bf16[1,128,512]{2,1,0:T(8,128)(2,1)S(1)} %get-tuple-element.93), channel_id=1, source_target_pairs={{0,4},{2,6},{4,8},{6,10},{8,12},{10,14},{1,5},{3,7},{5,9},{7,11},{... | collective-permute-start | bytes 393224 | tf_op jit(solution)/shard_map/ppermute | solution.py:99
  101.4 7.2 %collective-permute-start.17 = (bf16[1,128,512]{2,1,0:T(8,128)(2,1)S(1)}, bf16[1,128,512]{2,1,0:T(8,128)(2,1)S(1)}, u32[]{:S(2)}, u32[]{:S(2)}) collective-permute-start(bf16[1,128,512]{2,1,0:T(8,128)(2,1)S(1)} %get-tuple-element.94), channel_id=1, source_target_pairs={{4,0},{6,2},{8,4},{10,6},{12,8},{14,10},{5,1},{7,3},{9,5},{11,7},{... | collective-permute-start | bytes 393224 | tf_op jit(solution)/shard_map/ppermute | solution.py:100
  108.6 4.2 %collective-permute-start.18 = (bf16[8,128,1024]{2,1,0:T(8,128)(2,1)S(1)}, bf16[8,128,1024]{2,1,0:T(8,128)(2,1)S(1)}, u32[]{:S(2)}, u32[]{:S(2)}) collective-permute-start(bf16[8,128,1024]{2,1,0:T(8,128)(2,1)S(1)} %get-tuple-element.96), channel_id=1, source_target_pairs={{0,1},{1,0},{2,3},{3,2},{4,5},{5,4},{6,7},{7,6},{8,9},{9,8},{10,11... | collective-permute-start | bytes 6291464 | tf_op jit(solution)/shard_map/ppermute | solution.py:68
  114.0 14.9 %collective-permute-start.19 = (bf16[4,128,1024]{2,1,0:T(8,128)(2,1)S(1)}, bf16[4,128,1024]{2,1,0:T(8,128)(2,1)S(1)}, u32[]{:S(2)}, u32[]{:S(2)}) collective-permute-start(bf16[4,128,1024]{2,1,0:T(8,128)(2,1)S(1)} %slice.273), channel_id=1, source_target_pairs={{0,4},{1,3},{2,6},{3,1},{4,0},{5,7},{6,2},{7,5},{8,12},{9,11},{10,... | collective-permute-start | bytes 3145736 | tf_op jit(solution)/shard_map/ppermute | solution.py:78
  128.8 4.6 %collective-permute-start.20 = (bf16[8,128,1024]{2,1,0:T(8,128)(2,1)S(1)}, bf16[8,128,1024]{2,1,0:T(8,128)(2,1)S(1)}, u32[]{:S(2)}, u32[]{:S(2)}) collective-permute-start(bf16[8,128,1024]{2,1,0:T(8,128)(2,1)S(1)} %get-tuple-element.110), channel_id=1, source_target_pairs={{0,1},{1,0},{2,3},{3,2},{4,5},{5,4},{6,7},{7,6},{8,9},{9,8},{10,11... | collective-permute-start | bytes 6291464 | tf_op jit(solution)/shard_map/ppermute | solution.py:68
  128.8 5.7 %collective-permute-start.21 = (bf16[1,64,512]{2,1,0:T(8,128)(2,1)S(1)}, bf16[1,64,512]{2,1,0:T(8,128)(2,1)S(1)}, u32[]{:S(2)}, u32[]{:S(2)}) collective-permute-start(bf16[1,64,512]{2,1,0:T(8,128)(2,1)S(1)} %get-tuple-element.112), channel_id=1, source_target_pairs={{0,4},{2,6},{4,8},{6,10},{8,12},{10,14},{1,5},{3,7},{5,9},{7,11},{... | collective-permute-start | bytes 196616 | tf_op jit(solution)/shard_map/ppermute | solution.py:99
  131.7 6.2 %collective-permute-start.22 = (bf16[1,64,512]{2,1,0:T(8,128)(2,1)S(1)}, bf16[1,64,512]{2,1,0:T(8,128)(2,1)S(1)}, u32[]{:S(2)}, u32[]{:S(2)}) collective-permute-start(bf16[1,64,512]{2,1,0:T(8,128)(2,1)S(1)} %get-tuple-element.113), channel_id=1, source_target_pairs={{4,0},{6,2},{8,4},{10,6},{12,8},{14,10},{5,1},{7,3},{9,5},{11,7},{... | collective-permute-start | bytes 196616 | tf_op jit(solution)/shard_map/ppermute | solution.py:100
  138.0 20.0 %collective-permute-start.23 = (bf16[4,128,1024]{2,1,0:T(8,128)(2,1)S(1)}, bf16[4,128,1024]{2,1,0:T(8,128)(2,1)S(1)}, u32[]{:S(2)}, u32[]{:S(2)}) collective-permute-start(bf16[4,128,1024]{2,1,0:T(8,128)(2,1)S(1)} %slice.272), channel_id=1, source_target_pairs={{0,4},{1,3},{2,6},{3,1},{4,0},{5,7},{6,2},{7,5},{8,12},{9,11},{10,... | collective-permute-start | bytes 3145736 | tf_op jit(solution)/shard_map/ppermute | solution.py:78
  139.9 14.9 %collective-permute-start.24 = (bf16[2,128,1024]{2,1,0:T(8,128)(2,1)S(1)}, bf16[2,128,1024]{2,1,0:T(8,128)(2,1)S(1)}, u32[]{:S(2)}, u32[]{:S(2)}) collective-permute-start(bf16[2,128,1024]{2,1,0:T(8,128)(2,1)S(1)} %slice.275), channel_id=1, source_target_pairs={{0,2},{1,5},{2,0},{3,7},{4,6},{5,1},{6,4},{7,3},{8,10},{9,13},{10,... | collective-permute-start | bytes 1572872 | tf_op jit(solution)/shard_map/ppermute | solution.py:78
  158.3 13.5 %collective-permute-start.25 = (bf16[1,128,1024]{2,1,0:T(8,128)(2,1)S(1)}, bf16[1,128,1024]{2,1,0:T(8,128)(2,1)S(1)}, u32[]{:S(2)}, u32[]{:S(2)}) collective-permute-start(bf16[1,128,1024]{2,1,0:T(8,128)(2,1)S(1)} %slice.277), channel_id=1, source_target_pairs={{0,8},{1,9},{2,10},{3,11},{4,12},{5,13},{6,14},{7,15},{8,0},{9,1},... | collective-permute-start | bytes 786440 | tf_op jit(solution)/shard_map/ppermute | solution.py:78
  160.4 13.4 %collective-permute-start.27 = (bf16[2,128,1024]{2,1,0:T(8,128)(2,1)S(1)}, bf16[2,128,1024]{2,1,0:T(8,128)(2,1)S(1)}, u32[]{:S(2)}, u32[]{:S(2)}) collective-permute-start(bf16[2,128,1024]{2,1,0:T(8,128)(2,1)S(1)} %slice.274), channel_id=1, source_target_pairs={{0,2},{1,5},{2,0},{3,7},{4,6},{5,1},{6,4},{7,3},{8,10},{9,13},{10,... | collective-permute-start | bytes 1572872 | tf_op jit(solution)/shard_map/ppermute | solution.py:78
  171.9 1.8 collective-permute-start.26
  172.0 14.4 %collective-permute-start.29 = (bf16[1,256,1024]{2,1,0:T(8,128)(2,1)S(1)}, bf16[1,256,1024]{2,1,0:T(8,128)(2,1)S(1)}, u32[]{:S(2)}, u32[]{:S(2)}) collective-permute-start(bf16[1,256,1024]{2,1,0:T(8,128)(2,1)S(1)} %broadcast_select_fusion.2), channel_id=1, source_target_pairs={{0,2},{2,0},{4,6},{6,4},{8,10},{10,8},{12,14},{14,12},{1,3},{3,1},... | collective-permute-start | bytes 1572872 | tf_op jit(solution)/shard_map/ppermute | solution.py:106
  174.0 13.8 %collective-permute-start.28 = (bf16[1,128,1024]{2,1,0:T(8,128)(2,1)S(1)}, bf16[1,128,1024]{2,1,0:T(8,128)(2,1)S(1)}, u32[]{:S(2)}, u32[]{:S(2)}) collective-permute-start(bf16[1,128,1024]{2,1,0:T(8,128)(2,1)S(1)} %slice.276), channel_id=1, source_target_pairs={{0,8},{1,9},{2,10},{3,11},{4,12},{5,13},{6,14},{7,15},{8,0},{9,1},... | collective-permute-start | bytes 786440 | tf_op jit(solution)/shard_map/ppermute | solution.py:78
  187.9 1.6 collective-permute-start.30
  (3 other events, 21.3 us)

commit v5 on v4

--- a/solution.py
+++ b/solution.py
@@ -168,7 +168,7 @@
 
 
 def norm_rows(source, w, start, size, target, put):
-    @pl.loop(0, size // 32)
+    @pl.loop(0, size // 32, unroll=2)
     def _(i):
         rows = pl.multiple_of(i * 32, 32)
         v = source[w, pl.ds(start + rows, 32), :].astype(F32)
@@ -377,7 +377,7 @@
     with_weights(pieces, orders, middle, run)
     for w in range(windows):
 
-        @pl.loop(0, length // 32)
+        @pl.loop(0, length // 32, unroll=2)
         def _(i):
             rows = pl.ds(pl.multiple_of(i * 32, 32), 32)
             v = x_ref[w, rows, :].astype(F32)
@@ -468,11 +468,11 @@
         got = cross(jnp.where(leading, second, first))
         return ordered(leading, jnp.where(leading, first, second), got)[None]
 
+    mine_x, gives_x = split_pair(activations, 0)
+    got_x = swap_pair(gives_x)
     own_one = chip_part(conv_one, mix_one)
     got_one = hop(own_one, orders, 0)
-    activations, conv_two, mix_two, own_one = tie(activations, conv_two, mix_two, own_one)
-    mine_x, gives_x = split_pair(activations, 0)
-    got_x = swap_pair(gives_x)
+    conv_two, mix_two, own_one = tie(conv_two, mix_two, own_one)
     own_two = chip_part(conv_two, mix_two)
     own_one = widen(own_one, got_one)
     got_one = hop(own_one, orders, 1)
@@ -483,14 +483,13 @@
     low, high = halo(x[:, :DILATE_ONE], x[:, length - DILATE_ONE :])
     mine_e, gives_e = split_pair(cotangent, 0)
     got_e = swap_pair(gives_e)
-    got_one, got_two = tie(got_one, got_two)
+    ext_one = norm_ext(x, low, high)
+    got_one, got_two, ext_one, got_e = tie(got_one, got_two, ext_one, got_e)
     for j in range(2, last_step + 1):
         own_one, own_two = widen(own_one, got_one), widen(own_two, got_two)
         got_one, got_two = hop(own_one, orders, j), hop(own_two, orders, j - 1)
         if j == last_step:
-            ext_one = norm_ext(x, low, high)
             e = join_pair(mine_e, got_e, 1)
-            ext_one, e, got_one, got_two = tie(ext_one, e, got_one, got_two)
         got_one, got_two = tie(got_one, got_two)
     own_one = widen(own_one, got_one)
     got_one = cross(own_one)
@@ -543,7 +542,7 @@
         total_one = fold(total_one, got_one)
         got_one = give(total_one, orders, j)
         if j == last_step - 1:
-            total_one, gives_g = tie(total_one, gives_g)
+            got_one, gives_g = tie(got_one, gives_g)
             got_g = swap_pair(gives_g)
     total_two = fold(total_two, got_two)
     grads_two = unpack(total_two[0], middle)

time: 191 us -> 185 us (0.969)
  Pallas kernels: 31.6 us -> 26.6 us
  waiting for transfers between devices: 105 us -> 102 us
    ppermute x12, waiting for transfers between devices: 58.5 us -> 74 us  [hop(): return lax.ppermute(value, ('seq', 'dp'), pairs)]
    ppermute x3, waiting for transfers between devices: 11.4 us -> 2.42 us  [swap_pair(): return lax.ppermute(value, 'seq', [(i, i ^ 1) for i in range(count)])]
    ppermute x4, waiting for transfers between devices: 10.6 us -> 2.56 us  [halo(): low = lax.ppermute(last, 'seq', [(i, i + 2) for i in range(count - 2)])]
    pallas_call x2, Pallas kernels: 13.9 us -> 10.9 us  [back_block(): pl.pallas_call(functools.partial(back_kernel, orders, dilate, chained), o...]
    ppermute x4, starting transfers between devices: 14.4 us -> 16.7 us  [halo(): low = lax.ppermute(last, 'seq', [(i, i + 2) for i in range(count - 2)])]
  transfers between devices with their start and end apart: 31 -> 31, of which waited for: 21 -> 21; matrix products, arithmetic and copies ran while one was open for 3% -> 4% of each run, Pallas kernels for 15% -> 13%
where the time goes in v5:
time: 185 us; the launch traced here: 184 us
  waiting for transfers between devices  102 us (55%)
  starting transfers between devices  41.1 us (22%)
  Pallas kernels  26.6 us (14%)
  other arithmetic  9.9 us (5%)
  local copies, waits for them, and re-layouts  3.47 us (2%)
    ppermute x12, waiting for transfers between devices, hop(): return lax.ppermute(value, ('seq', 'dp'), pairs)  74 us
    ppermute x4, starting transfers between devices, halo(): low = lax.ppermute(last, 'seq', [(i, i + 2) for i in range(count - 2)])  16.7 us
    ppermute x12, starting transfers between devices, hop(): return lax.ppermute(value, ('seq', 'dp'), pairs)  13.3 us
    ppermute x8, waiting for transfers between devices, cross(): return lax.ppermute(value, 'dp', [(0, 1), (1, 0)])  11.7 us
    ppermute x4, waiting for transfers between devices, halo(): high = lax.ppermute(first, 'seq', [(i + 2, i) for i in range(count - 2)])  11.5 us
    pallas_call x2, Pallas kernels, back_block(): pl.pallas_call(functools.partial(back_kernel, orders, dilate, chained), o...  10.9 us
    pallas_call x2, Pallas kernels, grads_block(): pl.pallas_call(functools.partial(grads_kernel, orders, dilate), out_shape...  7.08 us
    ppermute x4, starting transfers between devices, halo(): high = lax.ppermute(first, 'seq', [(i + 2, i) for i in range(count - 2)])  5.39 us
  transfers between devices with their start and end apart: 31, of which 21 were waited for; matrix products, arithmetic and copies ran while one was open for 4% of the time, Pallas kernels for 13%

profile of v5, /device:TPU:0, one launch (start us, length us, event | category | flops | bytes accessed | tf_op | source)
XLA Modules:
  0.0 184.5 jit_solution(17553121984581382095)
XLA Ops:
  5.1 2.6 %collective-permute-start.5 = (bf16[1,256,1024]{2,1,0:T(8,128)(2,1)S(1)}, bf16[1,256,1024]{2,1,0:T(8,128)(2,1)S(1)}, u32[]{:S(2)}, u32[]{:S(2)}) collective-permute-start(bf16[1,256,1024]{2,1,0:T(8,128)(2,1)S(1)} %broadcast_select_fusion.10), channel_id=1, source_target_pairs={{0,2},{2,0},{4,6},{6,4},{8,10},{10,8},{12,14},{14,12},{1,3},{3,1},... | collective-permute-start | bytes 1572872 | tf_op jit(solution)/shard_map/ppermute | solution.py:106
  8.2 2.6 %collective-permute-start.1 = (bf16[1,128,1024]{2,1,0:T(8,128)(2,1)S(1)}, bf16[1,128,1024]{2,1,0:T(8,128)(2,1)S(1)}, u32[]{:S(2)}, u32[]{:S(2)}) collective-permute-start(bf16[1,128,1024]{2,1,0:T(8,128)(2,1)S(1)} %maximum_bitcast_fusion), channel_id=1, source_target_pairs={{0,8},{1,9},{2,10},{3,11},{4,12},{5,13},{6,14},{7,15},{8,0},{9,1},... | collective-permute-start | bytes 786440 | tf_op jit(solution)/shard_map/ppermute | solution.py:78
  10.9 12.3 %collective-permute-done.1 = bf16[1,128,1024]{2,1,0:T(8,128)(2,1)S(1)} collective-permute-done((bf16[1,128,1024]{2,1,0:T(8,128)(2,1)S(1)}, bf16[1,128,1024]{2,1,0:T(8,128)(2,1)S(1)}, u32[]{:S(2)}, u32[]{:S(2)}) %collective-permute-start.1) | collective-permute-done | bytes 262176 | tf_op jit(solution)/shard_map/ppermute | solution.py:78
  25.8 5.9 %collective-permute-start.6 = (bf16[1,64,1024]{2,1,0:T(8,128)(2,1)S(1)}, bf16[1,64,1024]{2,1,0:T(8,128)(2,1)S(1)}, u32[]{:S(2)}, u32[]{:S(2)}) collective-permute-start(bf16[1,64,1024]{2,1,0:T(8,128)(2,1)S(1)} %slice.178), channel_id=1, source_target_pairs={{0,4},{2,6},{4,8},{6,10},{8,12},{10,14},{1,5},{3,7},{5,9},{7,11},{... | collective-permute-start | bytes 393224 | tf_op jit(solution)/shard_map/ppermute | solution.py:99
  33.1 2.5 %collective-permute-done.6.low_ref = bf16[1,64,1024]{2,1,0:T(8,128)(2,1)S(1)} collective-permute-done((bf16[1,64,1024]{2,1,0:T(8,128)(2,1)S(1)}, bf16[1,64,1024]{2,1,0:T(8,128)(2,1)S(1)}, u32[]{:S(2)}, u32[]{:S(2)}) %collective-permute-start.6) | collective-permute-done | bytes 131104 | tf_op jit(solution)/shard_map/ppermute | solution.py:99
  35.6 3.4 %collective-permute-done.7.high_ref = bf16[1,64,1024]{2,1,0:T(8,128)(2,1)S(1)} collective-permute-done((bf16[1,64,1024]{2,1,0:T(8,128)(2,1)S(1)}, bf16[1,64,1024]{2,1,0:T(8,128)(2,1)S(1)}, u32[]{:S(2)}, u32[]{:S(2)}) %collective-permute-start.7) | collective-permute-done | bytes 131104 | tf_op jit(solution)/shard_map/ppermute | solution.py:100
  39.0 1.9 %norm_ext.1.ext = bf16[1,640,1024]{2,1,0:T(8,128)(2,1)S(1)} custom-call(bf16[1,512,1024]{2,1,0:T(8,128)(2,1)S(1)} %pad_maximum_fusion.1.x_ref.refs_3_, bf16[1,64,1024]{2,1,0:T(8,128)(2,1)S(1)} %collective-permute-done.6.low_ref, bf16[1,64,1024]{2,1,0:T(8,128)(2,1)S(1)} %collective-permute-done.7.high_ref), custom_call_target="tpu_custom_call" | custom-call | tf_op jit(solution)/shard_map/norm_ext/pallas_call | solution.py:189
  41.2 2.4 %collective-permute-done.8 = bf16[1,256,1024]{2,1,0:T(8,128)(2,1)S(1)} collective-permute-done((bf16[1,256,1024]{2,1,0:T(8,128)(2,1)S(1)}, bf16[1,256,1024]{2,1,0:T(8,128)(2,1)S(1)}, u32[]{:S(2)}, u32[]{:S(2)}) %collective-permute-start.8) | collective-permute-done | bytes 524320 | tf_op jit(solution)/shard_map/ppermute | solution.py:106
  47.0 13.2 %collective-permute-done.10 = bf16[2,128,1024]{2,1,0:T(8,128)(2,1)S(1)} collective-permute-done((bf16[2,128,1024]{2,1,0:T(8,128)(2,1)S(1)}, bf16[2,128,1024]{2,1,0:T(8,128)(2,1)S(1)}, u32[]{:S(2)}, u32[]{:S(2)}) %collective-permute-start.10) | collective-permute-done | bytes 524320 | tf_op jit(solution)/shard_map/ppermute | solution.py:78
  60.2 3.8 %collective-permute-done.9 = bf16[4,128,1024]{2,1,0:T(8,128)(2,1)S(1)} collective-permute-done((bf16[4,128,1024]{2,1,0:T(8,128)(2,1)S(1)}, bf16[4,128,1024]{2,1,0:T(8,128)(2,1)S(1)}, u32[]{:S(2)}, u32[]{:S(2)}) %collective-permute-start.9) | collective-permute-done | bytes 1048608 | tf_op jit(solution)/shard_map/ppermute | solution.py:78
  64.3 1.8 collective-permute-start.12
  66.0 2.3 %collective-permute-done.11.other.refs_8_.refs_6_ = bf16[8,128,1024]{2,1,0:T(8,128)(2,1)S(1)} collective-permute-done((bf16[8,128,1024]{2,1,0:T(8,128)(2,1)S(1)}, bf16[8,128,1024]{2,1,0:T(8,128)(2,1)S(1)}, u32[]{:S(2)}, u32[]{:S(2)}) %collective-permute-start.11) | collective-permute-done | bytes 2097184 | tf_op jit(solution)/shard_map/ppermute | solution.py:68
  68.3 3.3 %forward_block.1 = (f32[512,512]{1,0:T(8,128)S(1)}, bf16[512,512]{1,0:T(8,128)(2,1)S(1)}, bf16[1,512,1024]{2,1,0:T(8,128)(2,1)S(1)}, bf16[1,128,1024]{2,1,0:T(8,128)(2,1)S(1)}, bf16[1,128,1024]{2,1,0:T(8,128)(2,1)S(1)}) custom-call(bf16[1,640,1024]{2,1,0:T(8,128)(2,1)S(1)} %norm_ext.1.ext, bf16[1,512,1024]{2,1,0:T(8,128)(2,1)S(1)} %pad_maximum_fusion.1.x_ref.refs_3_, ...), custom_call_target="tpu_custom_call" | custom-call | flops 2147483648 | bytes 8388608 | tf_op jit(solution)/shard_map/forward_block/pallas_call | solution.py:227
  72.9 4.6 %collective-permute-start.13 = (bf16[1,128,1024]{2,1,0:T(8,128)(2,1)S(1)}, bf16[1,128,1024]{2,1,0:T(8,128)(2,1)S(1)}, u32[]{:S(2)}, u32[]{:S(2)}) collective-permute-start(bf16[1,128,1024]{2,1,0:T(8,128)(2,1)S(1)} %get-tuple-element.76.last), channel_id=1, source_target_pairs={{0,4},{2,6},{4,8},{6,10},{8,12},{10,14},{1,5},{3,7},{5,9},{7,11},{... | collective-permute-start | bytes 786440 | tf_op jit(solution)/shard_map/ppermute | solution.py:99
  77.5 4.5 %collective-permute-done.12 = bf16[4,128,1024]{2,1,0:T(8,128)(2,1)S(1)} collective-permute-done((bf16[4,128,1024]{2,1,0:T(8,128)(2,1)S(1)}, bf16[4,128,1024]{2,1,0:T(8,128)(2,1)S(1)}, u32[]{:S(2)}, u32[]{:S(2)}) %collective-permute-start.12) | collective-permute-done | bytes 1048608 | tf_op jit(solution)/shard_map/ppermute | solution.py:78
  81.9 2.8 %collective-permute-done.14.high = bf16[1,128,1024]{2,1,0:T(8,128)(2,1)S(1)} collective-permute-done((bf16[1,128,1024]{2,1,0:T(8,128)(2,1)S(1)}, bf16[1,128,1024]{2,1,0:T(8,128)(2,1)S(1)}, u32[]{:S(2)}, u32[]{:S(2)}) %collective-permute-start.14) | collective-permute-done | bytes 262176 | tf_op jit(solution)/shard_map/ppermute | solution.py:100
  85.2 4.0 %collective-permute-done.15.other.refs_6_ = bf16[8,128,1024]{2,1,0:T(8,128)(2,1)S(1)} collective-permute-done((bf16[8,128,1024]{2,1,0:T(8,128)(2,1)S(1)}, bf16[8,128,1024]{2,1,0:T(8,128)(2,1)S(1)}, u32[]{:S(2)}, u32[]{:S(2)}) %collective-permute-start.15) | collective-permute-done | bytes 2097184 | tf_op jit(solution)/shard_map/ppermute | solution.py:68
  89.2 3.4 %turn_block.1 = (bf16[1,768,1024]{2,1,0:T(8,128)(2,1)S(1)}, bf16[512,512]{1,0:T(8,128)(2,1)S(1)}, bf16[512,512]{1,0:T(8,128)(2,1)S(1)}, bf16[1,128,512]{2,1,0:T(8,128)(2,1)S(1)}, bf16[1,128,512]{2,1,0:T(8,128)(2,1)S(1)}) custom-call(bf16[1,128,1024]{2,1,0:T(8,128)(2,1)S(1)} %get-tuple-element.75.first, bf16[1,128,1024]{2,1,0:T(8,128)(2,1)S(1)} %get-tuple-element.76.last, ...), custom_call_target="tpu_custom_call" | custom-call | flops 2147483648 | bytes 8388608 | tf_op jit(solution)/shard_map/turn_block/pallas_call | solution.py:277
  92.6 3.6 %collective-permute-start.16 = (bf16[1,128,512]{2,1,0:T(8,128)(2,1)S(1)}, bf16[1,128,512]{2,1,0:T(8,128)(2,1)S(1)}, u32[]{:S(2)}, u32[]{:S(2)}) collective-permute-start(bf16[1,128,512]{2,1,0:T(8,128)(2,1)S(1)} %get-tuple-element.87), channel_id=1, source_target_pairs={{0,4},{2,6},{4,8},{6,10},{8,12},{10,14},{1,5},{3,7},{5,9},{7,11},{... | collective-permute-start | bytes 393224 | tf_op jit(solution)/shard_map/ppermute | solution.py:99
  97.5 3.7 %grads_block.2 = (f32[8,128,1024]{2,1,0:T(8,128)S(1)}, bf16[8,128,1024]{2,1,0:T(8,128)(2,1)S(1)}) custom-call(bf16[1,768,1024]{2,1,0:T(8,128)(2,1)S(1)} %get-tuple-element.84.ext, bf16[512,512]{1,0:T(8,128)(2,1)S(1)} %get-tuple-element.85.hid, bf16[1,512,1024]{2,1,0:T(8,128)(2,1)S(1)} %pad_maximum_fusion.4.e_ref.refs_4_, ...), custom_call_target="tpu_custom_call" | custom-call | flops 2147483648 | bytes 8388608 | tf_op jit(solution)/shard_map/grads_block/pallas_call | solution.py:343
  101.2 2.2 %collective-permute-done.17.refs_2_ = bf16[1,128,512]{2,1,0:T(8,128)(2,1)S(1)} collective-permute-done((bf16[1,128,512]{2,1,0:T(8,128)(2,1)S(1)}, bf16[1,128,512]{2,1,0:T(8,128)(2,1)S(1)}, u32[]{:S(2)}, u32[]{:S(2)}) %collective-permute-start.17) | collective-permute-done | bytes 131104 | tf_op jit(solution)/shard_map/ppermute | solution.py:100
  103.3 4.2 %collective-permute-done.18 = bf16[8,128,1024]{2,1,0:T(8,128)(2,1)S(1)} collective-permute-done((bf16[8,128,1024]{2,1,0:T(8,128)(2,1)S(1)}, bf16[8,128,1024]{2,1,0:T(8,128)(2,1)S(1)}, u32[]{:S(2)}, u32[]{:S(2)}) %collective-permute-start.18) | collective-permute-done | bytes 2097184 | tf_op jit(solution)/shard_map/ppermute | solution.py:68
  109.5 6.1 %back_block.2 = (bf16[1,512,1024]{2,1,0:T(8,128)(2,1)S(1)}, bf16[512,512]{1,0:T(8,128)(2,1)S(1)}, bf16[1,64,512]{2,1,0:T(8,128)(2,1)S(1)}, bf16[1,64,512]{2,1,0:T(8,128)(2,1)S(1)}) custom-call(bf16[512,512]{1,0:T(8,128)(2,1)S(1)} %get-tuple-element.83.dpre.refs_0_, bf16[1,128,512]{2,1,0:T(8,128)(2,1)S(1)} %collective-permute-done.16.refs_1_, ...), custom_call_target="tpu_custom_call" | custom-call | flops 2147483648 | bytes 8388608 | tf_op jit(solution)/shard_map/back_block/pallas_call | solution.py:421
  115.6 3.4 %grads_block.3 = (f32[8,128,1024]{2,1,0:T(8,128)S(1)}, bf16[8,128,1024]{2,1,0:T(8,128)(2,1)S(1)}) custom-call(bf16[1,640,1024]{2,1,0:T(8,128)(2,1)S(1)} %norm_ext.1.ext, bf16[512,512]{1,0:T(8,128)(2,1)S(1)} %get-tuple-element.97.hid, bf16[1,512,1024]{2,1,0:T(8,128)(2,1)S(1)} %get-tuple-element.98.e_ref.refs_4_, ...), custom_call_target="tpu_custom_call" | custom-call | flops 2147483648 | bytes 8388608 | tf_op jit(solution)/shard_map/grads_block/pallas_call | solution.py:343
  119.0 4.6 %collective-permute-done.19 = bf16[4,128,1024]{2,1,0:T(8,128)(2,1)S(1)} collective-permute-done((bf16[4,128,1024]{2,1,0:T(8,128)(2,1)S(1)}, bf16[4,128,1024]{2,1,0:T(8,128)(2,1)S(1)}, u32[]{:S(2)}, u32[]{:S(2)}) %collective-permute-start.19) | collective-permute-done | bytes 1048608 | tf_op jit(solution)/shard_map/ppermute | solution.py:78
  123.6 2.6 %collective-permute-start.21 = (bf16[1,64,512]{2,1,0:T(8,128)(2,1)S(1)}, bf16[1,64,512]{2,1,0:T(8,128)(2,1)S(1)}, u32[]{:S(2)}, u32[]{:S(2)}) collective-permute-start(bf16[1,64,512]{2,1,0:T(8,128)(2,1)S(1)} %get-tuple-element.106), channel_id=1, source_target_pairs={{0,4},{2,6},{4,8},{6,10},{8,12},{10,14},{1,5},{3,7},{5,9},{7,11},{... | collective-permute-start | bytes 196616 | tf_op jit(solution)/shard_map/ppermute | solution.py:99
  129.3 3.1 %collective-permute-done.22.refs_2_ = bf16[1,64,512]{2,1,0:T(8,128)(2,1)S(1)} collective-permute-done((bf16[1,64,512]{2,1,0:T(8,128)(2,1)S(1)}, bf16[1,64,512]{2,1,0:T(8,128)(2,1)S(1)}, u32[]{:S(2)}, u32[]{:S(2)}) %collective-permute-start.22) | collective-permute-done | bytes 65568 | tf_op jit(solution)/shard_map/ppermute | solution.py:100
  134.5 4.9 %back_block.3 = bf16[1,512,1024]{2,1,0:T(8,128)(2,1)S(1)} custom-call(bf16[512,512]{1,0:T(8,128)(2,1)S(1)} %get-tuple-element.96.dpre.refs_0_, bf16[1,64,512]{2,1,0:T(8,128)(2,1)S(1)} %collective-permute-done.21.refs_1_, bf16[1,64,512]{2,1,0:T(8,128)(2,1)S(1)} %collective-permute-done.22.refs_2_, bf16[1,512,1024]{2,1,0:T(8,128)(2,1)S(1)} %pad_maximum_fusion.1.x_ref.refs_3_, ...), custom_call_target="tpu_custom_call" | custom-call | flops 2147483648 | bytes 8388608 | tf_op jit(solution)/shard_map/back_block/pallas_call | solution.py:421
  139.4 8.8 %collective-permute-done.24 = bf16[2,128,1024]{2,1,0:T(8,128)(2,1)S(1)} collective-permute-done((bf16[2,128,1024]{2,1,0:T(8,128)(2,1)S(1)}, bf16[2,128,1024]{2,1,0:T(8,128)(2,1)S(1)}, u32[]{:S(2)}, u32[]{:S(2)}) %collective-permute-start.24) | collective-permute-done | bytes 524320 | tf_op jit(solution)/shard_map/ppermute | solution.py:78
  148.2 3.1 %collective-permute-done.23 = bf16[4,128,1024]{2,1,0:T(8,128)(2,1)S(1)} collective-permute-done((bf16[4,128,1024]{2,1,0:T(8,128)(2,1)S(1)}, bf16[4,128,1024]{2,1,0:T(8,128)(2,1)S(1)}, u32[]{:S(2)}, u32[]{:S(2)}) %collective-permute-start.23) | collective-permute-done | bytes 1048608 | tf_op jit(solution)/shard_map/ppermute | solution.py:78
  154.4 11.9 %collective-permute-done.25 = bf16[1,128,1024]{2,1,0:T(8,128)(2,1)S(1)} collective-permute-done((bf16[1,128,1024]{2,1,0:T(8,128)(2,1)S(1)}, bf16[1,128,1024]{2,1,0:T(8,128)(2,1)S(1)}, u32[]{:S(2)}, u32[]{:S(2)}) %collective-permute-start.25) | collective-permute-done | bytes 262176 | tf_op jit(solution)/shard_map/ppermute | solution.py:78
  169.7 11.5 %collective-permute-done.28 = bf16[1,128,1024]{2,1,0:T(8,128)(2,1)S(1)} collective-permute-done((bf16[1,128,1024]{2,1,0:T(8,128)(2,1)S(1)}, bf16[1,128,1024]{2,1,0:T(8,128)(2,1)S(1)}, u32[]{:S(2)}, u32[]{:S(2)}) %collective-permute-start.28) | collective-permute-done | bytes 262176 | tf_op jit(solution)/shard_map/ppermute | solution.py:78
  (107 shorter events, 32.3 us)
Async XLA Ops:
  3.3 4.4 %collective-permute-start = (bf16[64,1024]{1,0:T(8,128)(2,1)S(1)}, bf16[64,1024]{1,0:T(8,128)(2,1)S(1)}, u32[]{:S(2)}, u32[]{:S(2)}) collective-permute-start(bf16[64,1024]{1,0:T(8,128)(2,1)S(1)} %broadcast_select_fusion.18), channel_id=1, source_target_pairs={{0,1},{1,0},{2,3},{3,2},{4,5},{5,4},{6,7},{7,6},{8,9},{9,8},{10,11... | collective-permute-start | bytes 393224 | tf_op jit(solution)/shard_map/ppermute | solution.py:68
  5.1 18.7 %copy-start.1 = (bf16[2,256,1024]{2,1,0:T(8,128)(2,1)S(1)}, bf16[2,256,1024]{2,1,0:T(8,128)(2,1)}, u32[]{:S(2)}) copy-start(bf16[2,256,1024]{2,1,0:T(8,128)(2,1)} %param.7) | copy-start | bytes 3145732
  5.1 18.7 %collective-permute-start.5 = (bf16[1,256,1024]{2,1,0:T(8,128)(2,1)S(1)}, bf16[1,256,1024]{2,1,0:T(8,128)(2,1)S(1)}, u32[]{:S(2)}, u32[]{:S(2)}) collective-permute-start(bf16[1,256,1024]{2,1,0:T(8,128)(2,1)S(1)} %broadcast_select_fusion.10), channel_id=1, source_target_pairs={{0,2},{2,0},{4,6},{6,4},{8,10},{10,8},{12,14},{14,12},{1,3},{3,1},... | collective-permute-start | bytes 1572872 | tf_op jit(solution)/shard_map/ppermute | solution.py:106
  8.0 2.9 %collective-permute-start.3 = (bf16[64,1024]{1,0:T(8,128)(2,1)S(1)}, bf16[64,1024]{1,0:T(8,128)(2,1)S(1)}, u32[]{:S(2)}, u32[]{:S(2)}) collective-permute-start(bf16[64,1024]{1,0:T(8,128)(2,1)S(1)} %broadcast_select_fusion.14), channel_id=1, source_target_pairs={{0,1},{1,0},{2,3},{3,2},{4,5},{5,4},{6,7},{7,6},{8,9},{9,8},{10,11... | collective-permute-start | bytes 393224 | tf_op jit(solution)/shard_map/ppermute | solution.py:68
  8.2 15.0 %collective-permute-start.1 = (bf16[1,128,1024]{2,1,0:T(8,128)(2,1)S(1)}, bf16[1,128,1024]{2,1,0:T(8,128)(2,1)S(1)}, u32[]{:S(2)}, u32[]{:S(2)}) collective-permute-start(bf16[1,128,1024]{2,1,0:T(8,128)(2,1)S(1)} %maximum_bitcast_fusion), channel_id=1, source_target_pairs={{0,8},{1,9},{2,10},{3,11},{4,12},{5,13},{6,14},{7,15},{8,0},{9,1},... | collective-permute-start | bytes 786440 | tf_op jit(solution)/shard_map/ppermute | solution.py:78
  23.3 17.9 %collective-permute-start.2 = (bf16[2,128,1024]{2,1,0:T(8,128)(2,1)S(1)}, bf16[2,128,1024]{2,1,0:T(8,128)(2,1)S(1)}, u32[]{:S(2)}, u32[]{:S(2)}) collective-permute-start(bf16[2,128,1024]{2,1,0:T(8,128)(2,1)S(1)} %constant_dynamic-update-slice_fusion), channel_id=1, source_target_pairs={{0,2},{1,5},{2,0},{3,7},{4,6},{5,1},{6,4},{7,3},{8,10},{9,13},{10,... | collective-permute-start | bytes 1572872 | tf_op jit(solution)/shard_map/ppermute | solution.py:78
  23.9 19.7 %collective-permute-start.8 = (bf16[1,256,1024]{2,1,0:T(8,128)(2,1)S(1)}, bf16[1,256,1024]{2,1,0:T(8,128)(2,1)S(1)}, u32[]{:S(2)}, u32[]{:S(2)}) collective-permute-start(bf16[1,256,1024]{2,1,0:T(8,128)(2,1)S(1)} %broadcast_select_fusion.7), channel_id=1, source_target_pairs={{0,2},{2,0},{4,6},{6,4},{8,10},{10,8},{12,14},{14,12},{1,3},{3,1},... | collective-permute-start | bytes 1572872 | tf_op jit(solution)/shard_map/ppermute | solution.py:106
  25.5 15.6 %collective-permute-start.4 = (bf16[1,128,1024]{2,1,0:T(8,128)(2,1)S(1)}, bf16[1,128,1024]{2,1,0:T(8,128)(2,1)S(1)}, u32[]{:S(2)}, u32[]{:S(2)}) collective-permute-start(bf16[1,128,1024]{2,1,0:T(8,128)(2,1)S(1)} %maximum_bitcast_fusion.1), channel_id=1, source_target_pairs={{0,8},{1,9},{2,10},{3,11},{4,12},{5,13},{6,14},{7,15},{8,0},{9,1},... | collective-permute-start | bytes 786440 | tf_op jit(solution)/shard_map/ppermute | solution.py:78
  25.8 9.9 %collective-permute-start.6 = (bf16[1,64,1024]{2,1,0:T(8,128)(2,1)S(1)}, bf16[1,64,1024]{2,1,0:T(8,128)(2,1)S(1)}, u32[]{:S(2)}, u32[]{:S(2)}) collective-permute-start(bf16[1,64,1024]{2,1,0:T(8,128)(2,1)S(1)} %slice.178), channel_id=1, source_target_pairs={{0,4},{2,6},{4,8},{6,10},{8,12},{10,14},{1,5},{3,7},{5,9},{7,11},{... | collective-permute-start | bytes 393224 | tf_op jit(solution)/shard_map/ppermute | solution.py:99
  31.7 7.3 %collective-permute-start.7 = (bf16[1,64,1024]{2,1,0:T(8,128)(2,1)S(1)}, bf16[1,64,1024]{2,1,0:T(8,128)(2,1)S(1)}, u32[]{:S(2)}, u32[]{:S(2)}) collective-permute-start(bf16[1,64,1024]{2,1,0:T(8,128)(2,1)S(1)} %slice.179), channel_id=1, source_target_pairs={{4,0},{6,2},{8,4},{10,6},{12,8},{14,10},{5,1},{7,3},{9,5},{11,7},{... | collective-permute-start | bytes 393224 | tf_op jit(solution)/shard_map/ppermute | solution.py:100
  43.7 20.3 %collective-permute-start.9 = (bf16[4,128,1024]{2,1,0:T(8,128)(2,1)S(1)}, bf16[4,128,1024]{2,1,0:T(8,128)(2,1)S(1)}, u32[]{:S(2)}, u32[]{:S(2)}) collective-permute-start(bf16[4,128,1024]{2,1,0:T(8,128)(2,1)S(1)} %pad_maximum_fusion.2), channel_id=1, source_target_pairs={{0,4},{1,3},{2,6},{3,1},{4,0},{5,7},{6,2},{7,5},{8,12},{9,11},{10,... | collective-permute-start | bytes 3145736 | tf_op jit(solution)/shard_map/ppermute | solution.py:78
  45.3 14.9 %collective-permute-start.10 = (bf16[2,128,1024]{2,1,0:T(8,128)(2,1)S(1)}, bf16[2,128,1024]{2,1,0:T(8,128)(2,1)S(1)}, u32[]{:S(2)}, u32[]{:S(2)}) collective-permute-start(bf16[2,128,1024]{2,1,0:T(8,128)(2,1)S(1)} %pad_maximum_fusion.6), channel_id=1, source_target_pairs={{0,2},{1,5},{2,0},{3,7},{4,6},{5,1},{6,4},{7,3},{8,10},{9,13},{10,... | collective-permute-start | bytes 1572872 | tf_op jit(solution)/shard_map/ppermute | solution.py:78
  64.1 4.2 %collective-permute-start.11 = (bf16[8,128,1024]{2,1,0:T(8,128)(2,1)S(1)}, bf16[8,128,1024]{2,1,0:T(8,128)(2,1)S(1)}, u32[]{:S(2)}, u32[]{:S(2)}) collective-permute-start(bf16[8,128,1024]{2,1,0:T(8,128)(2,1)S(1)} %constant_dynamic-update-slice_fusion.2.own.refs_7_.refs_5_), channel_id=1, source_target_pairs={{0,1},{1,0},{2,3},{3,2},{4,5},{5,4},{6,7},{7,6},{8,9},{9,8},{10,11... | collective-permute-start | bytes 6291464 | tf_op jit(solution)/shard_map/ppermute | solution.py:68
  64.3 17.7 %collective-permute-start.12 = (bf16[4,128,1024]{2,1,0:T(8,128)(2,1)S(1)}, bf16[4,128,1024]{2,1,0:T(8,128)(2,1)S(1)}, u32[]{:S(2)}, u32[]{:S(2)}) collective-permute-start(bf16[4,128,1024]{2,1,0:T(8,128)(2,1)S(1)} %pad_maximum_fusion.3), channel_id=1, source_target_pairs={{0,4},{1,3},{2,6},{3,1},{4,0},{5,7},{6,2},{7,5},{8,12},{9,11},{10,... | collective-permute-start | bytes 3145736 | tf_op jit(solution)/shard_map/ppermute | solution.py:78
  71.6 13.2 %collective-permute-start.14 = (bf16[1,128,1024]{2,1,0:T(8,128)(2,1)S(1)}, bf16[1,128,1024]{2,1,0:T(8,128)(2,1)S(1)}, u32[]{:S(2)}, u32[]{:S(2)}) collective-permute-start(bf16[1,128,1024]{2,1,0:T(8,128)(2,1)S(1)} %get-tuple-element.75.first), channel_id=1, source_target_pairs={{4,0},{6,2},{8,4},{10,6},{12,8},{14,10},{5,1},{7,3},{9,5},{11,7},{... | collective-permute-start | bytes 786440 | tf_op jit(solution)/shard_map/ppermute | solution.py:100
  72.9 11.9 %collective-permute-start.13 = (bf16[1,128,1024]{2,1,0:T(8,128)(2,1)S(1)}, bf16[1,128,1024]{2,1,0:T(8,128)(2,1)S(1)}, u32[]{:S(2)}, u32[]{:S(2)}) collective-permute-start(bf16[1,128,1024]{2,1,0:T(8,128)(2,1)S(1)} %get-tuple-element.76.last), channel_id=1, source_target_pairs={{0,4},{2,6},{4,8},{6,10},{8,12},{10,14},{1,5},{3,7},{5,9},{7,11},{... | collective-permute-start | bytes 786440 | tf_op jit(solution)/shard_map/ppermute | solution.py:99
  85.0 4.2 %collective-permute-start.15 = (bf16[8,128,1024]{2,1,0:T(8,128)(2,1)S(1)}, bf16[8,128,1024]{2,1,0:T(8,128)(2,1)S(1)}, u32[]{:S(2)}, u32[]{:S(2)}) collective-permute-start(bf16[8,128,1024]{2,1,0:T(8,128)(2,1)S(1)} %pad_maximum_fusion.own.refs_5_), channel_id=1, source_target_pairs={{0,1},{1,0},{2,3},{3,2},{4,5},{5,4},{6,7},{7,6},{8,9},{9,8},{10,11... | collective-permute-start | bytes 6291464 | tf_op jit(solution)/shard_map/ppermute | solution.py:68
  92.6 8.6 %collective-permute-start.16 = (bf16[1,128,512]{2,1,0:T(8,128)(2,1)S(1)}, bf16[1,128,512]{2,1,0:T(8,128)(2,1)S(1)}, u32[]{:S(2)}, u32[]{:S(2)}) collective-permute-start(bf16[1,128,512]{2,1,0:T(8,128)(2,1)S(1)} %get-tuple-element.87), channel_id=1, source_target_pairs={{0,4},{2,6},{4,8},{6,10},{8,12},{10,14},{1,5},{3,7},{5,9},{7,11},{... | collective-permute-start | bytes 393224 | tf_op jit(solution)/shard_map/ppermute | solution.py:99
  96.2 7.2 %collective-permute-start.17 = (bf16[1,128,512]{2,1,0:T(8,128)(2,1)S(1)}, bf16[1,128,512]{2,1,0:T(8,128)(2,1)S(1)}, u32[]{:S(2)}, u32[]{:S(2)}) collective-permute-start(bf16[1,128,512]{2,1,0:T(8,128)(2,1)S(1)} %get-tuple-element.88), channel_id=1, source_target_pairs={{4,0},{6,2},{8,4},{10,6},{12,8},{14,10},{5,1},{7,3},{9,5},{11,7},{... | collective-permute-start | bytes 393224 | tf_op jit(solution)/shard_map/ppermute | solution.py:100
  103.3 4.2 %collective-permute-start.18 = (bf16[8,128,1024]{2,1,0:T(8,128)(2,1)S(1)}, bf16[8,128,1024]{2,1,0:T(8,128)(2,1)S(1)}, u32[]{:S(2)}, u32[]{:S(2)}) collective-permute-start(bf16[8,128,1024]{2,1,0:T(8,128)(2,1)S(1)} %get-tuple-element.90), channel_id=1, source_target_pairs={{0,1},{1,0},{2,3},{3,2},{4,5},{5,4},{6,7},{7,6},{8,9},{9,8},{10,11... | collective-permute-start | bytes 6291464 | tf_op jit(solution)/shard_map/ppermute | solution.py:68
  108.7 14.9 %collective-permute-start.19 = (bf16[4,128,1024]{2,1,0:T(8,128)(2,1)S(1)}, bf16[4,128,1024]{2,1,0:T(8,128)(2,1)S(1)}, u32[]{:S(2)}, u32[]{:S(2)}) collective-permute-start(bf16[4,128,1024]{2,1,0:T(8,128)(2,1)S(1)} %slice.274), channel_id=1, source_target_pairs={{0,4},{1,3},{2,6},{3,1},{4,0},{5,7},{6,2},{7,5},{8,12},{9,11},{10,... | collective-permute-start | bytes 3145736 | tf_op jit(solution)/shard_map/ppermute | solution.py:78
  123.6 4.6 %collective-permute-start.20 = (bf16[8,128,1024]{2,1,0:T(8,128)(2,1)S(1)}, bf16[8,128,1024]{2,1,0:T(8,128)(2,1)S(1)}, u32[]{:S(2)}, u32[]{:S(2)}) collective-permute-start(bf16[8,128,1024]{2,1,0:T(8,128)(2,1)S(1)} %get-tuple-element.104), channel_id=1, source_target_pairs={{0,1},{1,0},{2,3},{3,2},{4,5},{5,4},{6,7},{7,6},{8,9},{9,8},{10,11... | collective-permute-start | bytes 6291464 | tf_op jit(solution)/shard_map/ppermute | solution.py:68
  123.6 5.7 %collective-permute-start.21 = (bf16[1,64,512]{2,1,0:T(8,128)(2,1)S(1)}, bf16[1,64,512]{2,1,0:T(8,128)(2,1)S(1)}, u32[]{:S(2)}, u32[]{:S(2)}) collective-permute-start(bf16[1,64,512]{2,1,0:T(8,128)(2,1)S(1)} %get-tuple-element.106), channel_id=1, source_target_pairs={{0,4},{2,6},{4,8},{6,10},{8,12},{10,14},{1,5},{3,7},{5,9},{7,11},{... | collective-permute-start | bytes 196616 | tf_op jit(solution)/shard_map/ppermute | solution.py:99
  126.2 6.2 %collective-permute-start.22 = (bf16[1,64,512]{2,1,0:T(8,128)(2,1)S(1)}, bf16[1,64,512]{2,1,0:T(8,128)(2,1)S(1)}, u32[]{:S(2)}, u32[]{:S(2)}) collective-permute-start(bf16[1,64,512]{2,1,0:T(8,128)(2,1)S(1)} %get-tuple-element.107), channel_id=1, source_target_pairs={{4,0},{6,2},{8,4},{10,6},{12,8},{14,10},{5,1},{7,3},{9,5},{11,7},{... | collective-permute-start | bytes 196616 | tf_op jit(solution)/shard_map/ppermute | solution.py:100
  132.5 18.8 %collective-permute-start.23 = (bf16[4,128,1024]{2,1,0:T(8,128)(2,1)S(1)}, bf16[4,128,1024]{2,1,0:T(8,128)(2,1)S(1)}, u32[]{:S(2)}, u32[]{:S(2)}) collective-permute-start(bf16[4,128,1024]{2,1,0:T(8,128)(2,1)S(1)} %slice.273), channel_id=1, source_target_pairs={{0,4},{1,3},{2,6},{3,1},{4,0},{5,7},{6,2},{7,5},{8,12},{9,11},{10,... | collective-permute-start | bytes 3145736 | tf_op jit(solution)/shard_map/ppermute | solution.py:78
  133.3 14.9 %collective-permute-start.24 = (bf16[2,128,1024]{2,1,0:T(8,128)(2,1)S(1)}, bf16[2,128,1024]{2,1,0:T(8,128)(2,1)S(1)}, u32[]{:S(2)}, u32[]{:S(2)}) collective-permute-start(bf16[2,128,1024]{2,1,0:T(8,128)(2,1)S(1)} %slice.276), channel_id=1, source_target_pairs={{0,2},{1,5},{2,0},{3,7},{4,6},{5,1},{6,4},{7,3},{8,10},{9,13},{10,... | collective-permute-start | bytes 1572872 | tf_op jit(solution)/shard_map/ppermute | solution.py:78
  151.6 14.7 %collective-permute-start.25 = (bf16[1,128,1024]{2,1,0:T(8,128)(2,1)S(1)}, bf16[1,128,1024]{2,1,0:T(8,128)(2,1)S(1)}, u32[]{:S(2)}, u32[]{:S(2)}) collective-permute-start(bf16[1,128,1024]{2,1,0:T(8,128)(2,1)S(1)} %slice.278), channel_id=1, source_target_pairs={{0,8},{1,9},{2,10},{3,11},{4,12},{5,13},{6,14},{7,15},{8,0},{9,1},... | collective-permute-start | bytes 786440 | tf_op jit(solution)/shard_map/ppermute | solution.py:78
  153.4 13.1 %collective-permute-start.27 = (bf16[2,128,1024]{2,1,0:T(8,128)(2,1)S(1)}, bf16[2,128,1024]{2,1,0:T(8,128)(2,1)S(1)}, u32[]{:S(2)}, u32[]{:S(2)}) collective-permute-start(bf16[2,128,1024]{2,1,0:T(8,128)(2,1)S(1)} %slice.275), channel_id=1, source_target_pairs={{0,2},{1,5},{2,0},{3,7},{4,6},{5,1},{6,4},{7,3},{8,10},{9,13},{10,... | collective-permute-start | bytes 1572872 | tf_op jit(solution)/shard_map/ppermute | solution.py:78
  166.4 1.6 collective-permute-start.26
  166.5 14.7 %collective-permute-start.29 = (bf16[1,256,1024]{2,1,0:T(8,128)(2,1)S(1)}, bf16[1,256,1024]{2,1,0:T(8,128)(2,1)S(1)}, u32[]{:S(2)}, u32[]{:S(2)}) collective-permute-start(bf16[1,256,1024]{2,1,0:T(8,128)(2,1)S(1)} %broadcast_select_fusion.2), channel_id=1, source_target_pairs={{0,2},{2,0},{4,6},{6,4},{8,10},{10,8},{12,14},{14,12},{1,3},{3,1},... | collective-permute-start | bytes 1572872 | tf_op jit(solution)/shard_map/ppermute | solution.py:106
  168.1 13.1 %collective-permute-start.28 = (bf16[1,128,1024]{2,1,0:T(8,128)(2,1)S(1)}, bf16[1,128,1024]{2,1,0:T(8,128)(2,1)S(1)}, u32[]{:S(2)}, u32[]{:S(2)}) collective-permute-start(bf16[1,128,1024]{2,1,0:T(8,128)(2,1)S(1)} %slice.277), channel_id=1, source_target_pairs={{0,8},{1,9},{2,10},{3,11},{4,12},{5,13},{6,14},{7,15},{8,0},{9,1},... | collective-permute-start | bytes 786440 | tf_op jit(solution)/shard_map/ppermute | solution.py:78
  181.3 1.6 collective-permute-start.30
  (3 other events, 31.2 us)

commit v6 on v5

--- a/solution.py
+++ b/solution.py
@@ -12,6 +12,10 @@
 DILATE_TWO = 128
 BF = jnp.bfloat16
 F32 = jnp.float32
+GATHER_ONE = ((0, 2, 1), (0, 1, 2))
+GATHER_TWO = ((0, 2, 1), (0, 1, 2))
+SUM_ONE = ((0, 2, 1), (0, 1, 2))
+SUM_TWO = ((0, 2, 1), (1, 0, 2))
 ROOT = math.sqrt(2.0 / math.pi)
 CUBE = 0.044715
 VMEM = pl.BlockSpec(memory_space=pltpu.VMEM)
@@ -50,9 +54,11 @@
     return lax.optimization_barrier(values)
 
 
-def step_orders(count):
+def step_orders(count, ranks):
     bits = [1 << i for i in reversed(range(count.bit_length() - 1))]
     assert math.prod([2] * len(bits)) == count
+    if len(bits) == len(ranks[0]):
+        return tuple([bits[i] for i in order] for order in ranks)
     return bits[:-2] + bits[:-3:-1], bits
 
 
@@ -168,7 +174,7 @@
 
 
 def norm_rows(source, w, start, size, target, put):
-    @pl.loop(0, size // 32, unroll=2)
+    @pl.loop(0, size // 32, unroll=4)
     def _(i):
         rows = pl.multiple_of(i * 32, 32)
         v = source[w, pl.ds(start + rows, 32), :].astype(F32)
@@ -352,7 +358,8 @@
     )(ext, hid, e, dpre)
 
 
-def back_kernel(orders, dilate, chained, *refs):
+def back_kernel(orders, dilate, orders_m, *refs):
+    chained = orders_m is not None
     dpre, low, high, x_ref, e_ref = refs[:5]
     pieces = refs[5:7]
     if chained:
@@ -377,7 +384,7 @@
     with_weights(pieces, orders, middle, run)
     for w in range(windows):
 
-        @pl.loop(0, length // 32, unroll=2)
+        @pl.loop(0, length // 32, unroll=4)
         def _(i):
             rows = pl.ds(pl.multiple_of(i * 32, 32), 32)
             v = x_ref[w, rows, :].astype(F32)
@@ -397,7 +404,7 @@
                 rows = slice(w * length, (w + 1) * length)
                 dprev[rows, :] = (gelu_slope(pre_ref[rows, :]) * dhid).astype(BF)
 
-        with_weights(pieces_m, orders, middle, turn)
+        with_weights(pieces_m, orders_m, middle, turn)
         edge = dfirst.shape[1]
         for w in range(windows):
             dfirst[w] = dprev[w * length : w * length + edge, :]
@@ -407,11 +414,11 @@
 def back_block(dpre, low, high, x, e, pieces, orders, dilate, previous=None):
     windows, length, width = x.shape
     flat, middle = dpre.shape
-    chained = previous is not None
+    chained, orders_m = previous is not None, None
     operands = [dpre, low, high, x, e, *pieces]
     shapes = [jax.ShapeDtypeStruct(x.shape, BF)]
     if chained:
-        others, pre, edge = previous
+        others, orders_m, pre, edge = previous
         operands += [*others, pre]
         shapes += [
             jax.ShapeDtypeStruct((flat, middle), BF),
@@ -419,7 +426,7 @@
             jax.ShapeDtypeStruct((windows, edge, middle), BF),
         ]
     return pl.pallas_call(
-        functools.partial(back_kernel, orders, dilate, chained),
+        functools.partial(back_kernel, orders, dilate, orders_m),
         out_shape=tuple(shapes),
         in_specs=[VMEM] * len(operands),
         out_specs=(VMEM,) * len(shapes),
@@ -457,8 +464,10 @@
 
 def body(activations, cotangent, conv_one, mix_one, conv_two, mix_two):
     count = lax.axis_size("seq")
-    orders = step_orders(count)
-    sum_orders = orders
+    orders = step_orders(count, GATHER_ONE)
+    orders_two = step_orders(count, GATHER_TWO)
+    sums_one = step_orders(count, SUM_ONE)
+    sums_two = step_orders(count, SUM_TWO)
     last_step = len(orders[0]) - 1
     middle = conv_one.shape[2]
     leading = lax.axis_index("dp") == 0
@@ -476,7 +485,7 @@
     own_two = chip_part(conv_two, mix_two)
     own_one = widen(own_one, got_one)
     got_one = hop(own_one, orders, 1)
-    got_two = hop(own_two, orders, 0)
+    got_two = hop(own_two, orders_two, 0)
     own_one, cotangent, got_x = tie(own_one, cotangent, got_x)
     x = join_pair(mine_x, got_x, 1)
     length = x.shape[1]
@@ -487,7 +496,7 @@
     got_one, got_two, ext_one, got_e = tie(got_one, got_two, ext_one, got_e)
     for j in range(2, last_step + 1):
         own_one, own_two = widen(own_one, got_one), widen(own_two, got_two)
-        got_one, got_two = hop(own_one, orders, j), hop(own_two, orders, j - 1)
+        got_one, got_two = hop(own_one, orders, j), hop(own_two, orders_two, j - 1)
         if j == last_step:
             e = join_pair(mine_e, got_e, 1)
         got_one, got_two = tie(got_one, got_two)
@@ -495,7 +504,7 @@
     got_one = cross(own_one)
     own_one, got_two = tie(own_one, got_two)
     own_two = widen(own_two, got_two)
-    got_two = hop(own_two, orders, last_step)
+    got_two = hop(own_two, orders_two, last_step)
     pieces_one = (own_one, got_one)
     pre_one, hid_one, second_in, first, last = forward_block(
         ext_one, x, pieces_one, orders, DILATE_ONE, DILATE_TWO
@@ -505,31 +514,32 @@
     own_two = widen(own_two, got_two)
     pieces_two = (own_two, cross(own_two))
     ext_two, hid_two, dpre_two, dfirst, dlast = turn_block(
-        first, last, low, high, second_in, e, pieces_two, orders, DILATE_TWO
+        first, last, low, high, second_in, e, pieces_two, orders_two, DILATE_TWO
     )
 
     dlow, dhigh = halo(dfirst, dlast)
     keep_two, send = grads_block(
-        ext_two, hid_two, e, dpre_two, sum_orders, DILATE_TWO, count
+        ext_two, hid_two, e, dpre_two, sums_two, DILATE_TWO, count
     )
     dlow, dhigh, send = tie(dlow, dhigh, send)
     got_two = cross(send)
+    upstream, dpre_one, dfirst, dlast = back_block(
+        dpre_two, dlow, dhigh, second_in, e, pieces_two, orders_two, DILATE_TWO,
+        (pieces_one, orders, pre_one, DILATE_ONE),
+    )
+    got_two, dpre_one, upstream = tie(got_two, dpre_one, upstream)
     total_two = fold_all(keep_two, got_two)
-    total_two, dlow, dhigh = tie(total_two, dlow, dhigh)
-    got_two = give(total_two, sum_orders, last_step)
-    upstream, dpre_one, dfirst, dlast = back_block(
-        dpre_two, dlow, dhigh, second_in, e, pieces_two, orders, DILATE_TWO,
-        (pieces_one, pre_one, DILATE_ONE),
-    )
-    keep_one, send = grads_block(ext_one, hid_one, upstream, dpre_one, orders, DILATE_ONE, count)
-    got_two, send, dfirst, dlast = tie(got_two, send, dfirst, dlast)
+    total_two, dpre_one = tie(total_two, dpre_one)
+    got_two = give(total_two, sums_two, last_step)
+    keep_one, send = grads_block(ext_one, hid_one, upstream, dpre_one, sums_one, DILATE_ONE, count)
     got_one = cross(send)
+    dfirst, dlast, send = tie(dfirst, dlast, send)
     dlow, dhigh = halo(dfirst, dlast)
+    total_one = fold_all(keep_one, got_one)
+    got_two, total_one, dlow, dhigh = tie(got_two, total_one, dlow, dhigh)
+    got_one = give(total_one, sums_one, last_step)
     total_two = fold(total_two, got_two)
-    got_two = give(total_two, sum_orders, last_step - 1)
-    total_one = fold_all(keep_one, got_one)
-    total_one, total_two, dlow, dhigh = tie(total_one, total_two, dlow, dhigh)
-    got_one = give(total_one, orders, last_step)
+    got_two = give(total_two, sums_two, last_step - 1)
     (input_grad,) = back_block(
         dpre_one, dlow, dhigh, x, upstream, pieces_one, orders, DILATE_ONE
     )
@@ -538,9 +548,9 @@
     for j in reversed(range(last_step)):
         if j < last_step - 1:
             total_two = fold(total_two, got_two)
-            got_two = give(total_two, sum_orders, j)
+            got_two = give(total_two, sums_two, j)
         total_one = fold(total_one, got_one)
-        got_one = give(total_one, orders, j)
+        got_one = give(total_one, sums_one, j)
         if j == last_step - 1:
             got_one, gives_g = tie(got_one, gives_g)
             got_g = swap_pair(gives_g)

time: 185 us -> 180 us (0.973)
  waiting for transfers between devices: 102 us -> 99.5 us
    ppermute x4, waiting for transfers between devices: 2.56 us -> 10.4 us  [halo(): low = lax.ppermute(last, 'seq', [(i, i + 2) for i in range(count - 2)])]
    ppermute x12, waiting for transfers between devices: 74 us -> 68.7 us  [hop(): return lax.ppermute(value, ('seq', 'dp'), pairs)]
    ppermute x8, waiting for transfers between devices: 11.7 us -> 7.49 us  [cross(): return lax.ppermute(value, 'dp', [(0, 1), (1, 0)])]
  transfers between devices with their start and end apart: 31 -> 31, of which waited for: 21 -> 20; matrix products, arithmetic and copies ran while one was open for 4% -> 4% of each run, Pallas kernels for 13% -> 10%
where the time goes in v6:
time: 180 us
  waiting for transfers between devices  99.5 us (55%)
  starting transfers between devices  41.2 us (23%)
  Pallas kernels  24.8 us (14%)
  other arithmetic  9.78 us (5%)
  local copies, waits for them, and re-layouts  3.47 us (2%)
    ppermute x12, waiting for transfers between devices, hop(): return lax.ppermute(value, ('seq', 'dp'), pairs)  68.7 us
    ppermute x4, starting transfers between devices, halo(): low = lax.ppermute(last, 'seq', [(i, i + 2) for i in range(count - 2)])  17.4 us
    ppermute x12, starting transfers between devices, hop(): return lax.ppermute(value, ('seq', 'dp'), pairs)  12 us
    ppermute x4, waiting for transfers between devices, halo(): low = lax.ppermute(last, 'seq', [(i, i + 2) for i in range(count - 2)])  10.4 us
    ppermute x4, waiting for transfers between devices, halo(): high = lax.ppermute(first, 'seq', [(i + 2, i) for i in range(count - 2)])  10.3 us
    pallas_call x2, Pallas kernels, back_block(): pl.pallas_call(functools.partial(back_kernel, orders, dilate, orders_m),...  9.8 us
    ppermute x8, waiting for transfers between devices, cross(): return lax.ppermute(value, 'dp', [(0, 1), (1, 0)])  7.49 us
    pallas_call x2, Pallas kernels, grads_block(): pl.pallas_call(functools.partial(grads_kernel, orders, dilate), out_shape...  7.05 us
  transfers between devices with their start and end apart: 31, of which 20 were waited for; matrix products, arithmetic and copies ran while one was open for 4% of the time, Pallas kernels for 10%

profile of v6, /device:TPU:0, one launch (start us, length us, event | category | flops | bytes accessed | tf_op | source)
XLA Modules:
  0.0 179.9 jit_solution(3205170824960334070)
XLA Ops:
  5.1 2.6 %collective-permute-start.5 = (bf16[1,256,1024]{2,1,0:T(8,128)(2,1)S(1)}, bf16[1,256,1024]{2,1,0:T(8,128)(2,1)S(1)}, u32[]{:S(2)}, u32[]{:S(2)}) collective-permute-start(bf16[1,256,1024]{2,1,0:T(8,128)(2,1)S(1)} %broadcast_select_fusion.10), channel_id=1, source_target_pairs={{0,2},{2,0},{4,6},{6,4},{8,10},{10,8},{12,14},{14,12},{1,3},{3,1},... | collective-permute-start | bytes 1572872 | tf_op jit(solution)/shard_map/ppermute | solution.py:112
  8.2 2.6 %collective-permute-start.1 = (bf16[1,128,1024]{2,1,0:T(8,128)(2,1)S(1)}, bf16[1,128,1024]{2,1,0:T(8,128)(2,1)S(1)}, u32[]{:S(2)}, u32[]{:S(2)}) collective-permute-start(bf16[1,128,1024]{2,1,0:T(8,128)(2,1)S(1)} %maximum_bitcast_fusion), channel_id=1, source_target_pairs={{0,8},{1,9},{2,10},{3,11},{4,12},{5,13},{6,14},{7,15},{8,0},{9,1},... | collective-permute-start | bytes 786440 | tf_op jit(solution)/shard_map/ppermute | solution.py:84
  10.9 12.3 %collective-permute-done.1 = bf16[1,128,1024]{2,1,0:T(8,128)(2,1)S(1)} collective-permute-done((bf16[1,128,1024]{2,1,0:T(8,128)(2,1)S(1)}, bf16[1,128,1024]{2,1,0:T(8,128)(2,1)S(1)}, u32[]{:S(2)}, u32[]{:S(2)}) %collective-permute-start.1) | collective-permute-done | bytes 262176 | tf_op jit(solution)/shard_map/ppermute | solution.py:84
  25.8 5.9 %collective-permute-start.6 = (bf16[1,64,1024]{2,1,0:T(8,128)(2,1)S(1)}, bf16[1,64,1024]{2,1,0:T(8,128)(2,1)S(1)}, u32[]{:S(2)}, u32[]{:S(2)}) collective-permute-start(bf16[1,64,1024]{2,1,0:T(8,128)(2,1)S(1)} %slice.178), channel_id=1, source_target_pairs={{0,4},{2,6},{4,8},{6,10},{8,12},{10,14},{1,5},{3,7},{5,9},{7,11},{... | collective-permute-start | bytes 393224 | tf_op jit(solution)/shard_map/ppermute | solution.py:105
  33.1 2.5 %collective-permute-done.6.low_ref = bf16[1,64,1024]{2,1,0:T(8,128)(2,1)S(1)} collective-permute-done((bf16[1,64,1024]{2,1,0:T(8,128)(2,1)S(1)}, bf16[1,64,1024]{2,1,0:T(8,128)(2,1)S(1)}, u32[]{:S(2)}, u32[]{:S(2)}) %collective-permute-start.6) | collective-permute-done | bytes 131104 | tf_op jit(solution)/shard_map/ppermute | solution.py:105
  35.6 3.4 %collective-permute-done.7.high_ref = bf16[1,64,1024]{2,1,0:T(8,128)(2,1)S(1)} collective-permute-done((bf16[1,64,1024]{2,1,0:T(8,128)(2,1)S(1)}, bf16[1,64,1024]{2,1,0:T(8,128)(2,1)S(1)}, u32[]{:S(2)}, u32[]{:S(2)}) %collective-permute-start.7) | collective-permute-done | bytes 131104 | tf_op jit(solution)/shard_map/ppermute | solution.py:106
  39.0 1.8 norm_ext.1.ext
  41.2 2.6 %collective-permute-done.8 = bf16[1,256,1024]{2,1,0:T(8,128)(2,1)S(1)} collective-permute-done((bf16[1,256,1024]{2,1,0:T(8,128)(2,1)S(1)}, bf16[1,256,1024]{2,1,0:T(8,128)(2,1)S(1)}, u32[]{:S(2)}, u32[]{:S(2)}) %collective-permute-start.8) | collective-permute-done | bytes 524320 | tf_op jit(solution)/shard_map/ppermute | solution.py:112
  46.8 13.3 %collective-permute-done.10 = bf16[2,128,1024]{2,1,0:T(8,128)(2,1)S(1)} collective-permute-done((bf16[2,128,1024]{2,1,0:T(8,128)(2,1)S(1)}, bf16[2,128,1024]{2,1,0:T(8,128)(2,1)S(1)}, u32[]{:S(2)}, u32[]{:S(2)}) %collective-permute-start.10) | collective-permute-done | bytes 524320 | tf_op jit(solution)/shard_map/ppermute | solution.py:84
  60.1 3.7 %collective-permute-done.9 = bf16[4,128,1024]{2,1,0:T(8,128)(2,1)S(1)} collective-permute-done((bf16[4,128,1024]{2,1,0:T(8,128)(2,1)S(1)}, bf16[4,128,1024]{2,1,0:T(8,128)(2,1)S(1)}, u32[]{:S(2)}, u32[]{:S(2)}) %collective-permute-start.9) | collective-permute-done | bytes 1048608 | tf_op jit(solution)/shard_map/ppermute | solution.py:84
  64.1 1.8 collective-permute-start.12
  65.8 2.3 %collective-permute-done.11.other.refs_8_.refs_6_ = bf16[8,128,1024]{2,1,0:T(8,128)(2,1)S(1)} collective-permute-done((bf16[8,128,1024]{2,1,0:T(8,128)(2,1)S(1)}, bf16[8,128,1024]{2,1,0:T(8,128)(2,1)S(1)}, u32[]{:S(2)}, u32[]{:S(2)}) %collective-permute-start.11) | collective-permute-done | bytes 2097184 | tf_op jit(solution)/shard_map/ppermute | solution.py:74
  68.1 3.0 %forward_block.1 = (f32[512,512]{1,0:T(8,128)S(1)}, bf16[512,512]{1,0:T(8,128)(2,1)S(1)}, bf16[1,512,1024]{2,1,0:T(8,128)(2,1)S(1)}, bf16[1,128,1024]{2,1,0:T(8,128)(2,1)S(1)}, bf16[1,128,1024]{2,1,0:T(8,128)(2,1)S(1)}) custom-call(bf16[1,640,1024]{2,1,0:T(8,128)(2,1)S(1)} %norm_ext.1.ext, bf16[1,512,1024]{2,1,0:T(8,128)(2,1)S(1)} %pad_maximum_fusion.1.x_ref.refs_3_, ...), custom_call_target="tpu_custom_call" | custom-call | flops 2147483648 | bytes 8388608 | tf_op jit(solution)/shard_map/forward_block/pallas_call | solution.py:233
  72.4 4.6 %collective-permute-start.13 = (bf16[1,128,1024]{2,1,0:T(8,128)(2,1)S(1)}, bf16[1,128,1024]{2,1,0:T(8,128)(2,1)S(1)}, u32[]{:S(2)}, u32[]{:S(2)}) collective-permute-start(bf16[1,128,1024]{2,1,0:T(8,128)(2,1)S(1)} %get-tuple-element.76.last), channel_id=1, source_target_pairs={{0,4},{2,6},{4,8},{6,10},{8,12},{10,14},{1,5},{3,7},{5,9},{7,11},{... | collective-permute-start | bytes 786440 | tf_op jit(solution)/shard_map/ppermute | solution.py:105
  77.0 4.8 %collective-permute-done.12 = bf16[4,128,1024]{2,1,0:T(8,128)(2,1)S(1)} collective-permute-done((bf16[4,128,1024]{2,1,0:T(8,128)(2,1)S(1)}, bf16[4,128,1024]{2,1,0:T(8,128)(2,1)S(1)}, u32[]{:S(2)}, u32[]{:S(2)}) %collective-permute-start.12) | collective-permute-done | bytes 1048608 | tf_op jit(solution)/shard_map/ppermute | solution.py:84
  81.8 2.8 %collective-permute-done.14.high = bf16[1,128,1024]{2,1,0:T(8,128)(2,1)S(1)} collective-permute-done((bf16[1,128,1024]{2,1,0:T(8,128)(2,1)S(1)}, bf16[1,128,1024]{2,1,0:T(8,128)(2,1)S(1)}, u32[]{:S(2)}, u32[]{:S(2)}) %collective-permute-start.14) | collective-permute-done | bytes 262176 | tf_op jit(solution)/shard_map/ppermute | solution.py:106
  85.1 3.9 %collective-permute-done.15.other.refs_6_ = bf16[8,128,1024]{2,1,0:T(8,128)(2,1)S(1)} collective-permute-done((bf16[8,128,1024]{2,1,0:T(8,128)(2,1)S(1)}, bf16[8,128,1024]{2,1,0:T(8,128)(2,1)S(1)}, u32[]{:S(2)}, u32[]{:S(2)}) %collective-permute-start.15) | collective-permute-done | bytes 2097184 | tf_op jit(solution)/shard_map/ppermute | solution.py:74
  89.0 3.2 %turn_block.1 = (bf16[1,768,1024]{2,1,0:T(8,128)(2,1)S(1)}, bf16[512,512]{1,0:T(8,128)(2,1)S(1)}, bf16[512,512]{1,0:T(8,128)(2,1)S(1)}, bf16[1,128,512]{2,1,0:T(8,128)(2,1)S(1)}, bf16[1,128,512]{2,1,0:T(8,128)(2,1)S(1)}) custom-call(bf16[1,128,1024]{2,1,0:T(8,128)(2,1)S(1)} %get-tuple-element.75.first, bf16[1,128,1024]{2,1,0:T(8,128)(2,1)S(1)} %get-tuple-element.76.last, ...), custom_call_target="tpu_custom_call" | custom-call | flops 2147483648 | bytes 8388608 | tf_op jit(solution)/shard_map/turn_block/pallas_call | solution.py:283
  92.2 3.6 %collective-permute-start.16 = (bf16[1,128,512]{2,1,0:T(8,128)(2,1)S(1)}, bf16[1,128,512]{2,1,0:T(8,128)(2,1)S(1)}, u32[]{:S(2)}, u32[]{:S(2)}) collective-permute-start(bf16[1,128,512]{2,1,0:T(8,128)(2,1)S(1)} %get-tuple-element.87), channel_id=1, source_target_pairs={{0,4},{2,6},{4,8},{6,10},{8,12},{10,14},{1,5},{3,7},{5,9},{7,11},{... | collective-permute-start | bytes 393224 | tf_op jit(solution)/shard_map/ppermute | solution.py:105
  97.1 3.6 %grads_block.2 = (f32[8,128,1024]{2,1,0:T(8,128)S(1)}, bf16[8,128,1024]{2,1,0:T(8,128)(2,1)S(1)}) custom-call(bf16[1,768,1024]{2,1,0:T(8,128)(2,1)S(1)} %get-tuple-element.83.ext, bf16[512,512]{1,0:T(8,128)(2,1)S(1)} %get-tuple-element.84.hid, bf16[1,512,1024]{2,1,0:T(8,128)(2,1)S(1)} %pad_maximum_fusion.4.e_ref.refs_4_, ...), custom_call_target="tpu_custom_call" | custom-call | flops 2147483648 | bytes 8388608 | tf_op jit(solution)/shard_map/grads_block/pallas_call | solution.py:349
  100.7 2.2 %collective-permute-done.17.refs_2_ = bf16[1,128,512]{2,1,0:T(8,128)(2,1)S(1)} collective-permute-done((bf16[1,128,512]{2,1,0:T(8,128)(2,1)S(1)}, bf16[1,128,512]{2,1,0:T(8,128)(2,1)S(1)}, u32[]{:S(2)}, u32[]{:S(2)}) %collective-permute-start.17) | collective-permute-done | bytes 131104 | tf_op jit(solution)/shard_map/ppermute | solution.py:106
  102.9 5.5 %back_block.2 = (bf16[1,512,1024]{2,1,0:T(8,128)(2,1)S(1)}, bf16[512,512]{1,0:T(8,128)(2,1)S(1)}, bf16[1,64,512]{2,1,0:T(8,128)(2,1)S(1)}, bf16[1,64,512]{2,1,0:T(8,128)(2,1)S(1)}) custom-call(bf16[512,512]{1,0:T(8,128)(2,1)S(1)} %get-tuple-element.85.dpre.refs_0_, bf16[1,128,512]{2,1,0:T(8,128)(2,1)S(1)} %collective-permute-done.16.refs_1_, ...), custom_call_target="tpu_custom_call" | custom-call | flops 2147483648 | bytes 8388608 | tf_op jit(solution)/shard_map/back_block/pallas_call | solution.py:428
  109.5 3.4 %grads_block.3 = (f32[8,128,1024]{2,1,0:T(8,128)S(1)}, bf16[8,128,1024]{2,1,0:T(8,128)(2,1)S(1)}) custom-call(bf16[1,640,1024]{2,1,0:T(8,128)(2,1)S(1)} %norm_ext.1.ext, bf16[512,512]{1,0:T(8,128)(2,1)S(1)} %get-tuple-element.100.hid, bf16[1,512,1024]{2,1,0:T(8,128)(2,1)S(1)} %get-tuple-element.101.e_ref.refs_4_, ...), custom_call_target="tpu_custom_call" | custom-call | flops 2147483648 | bytes 8388608 | tf_op jit(solution)/shard_map/grads_block/pallas_call | solution.py:349
  114.3 3.3 %collective-permute-start.21 = (bf16[1,64,512]{2,1,0:T(8,128)(2,1)S(1)}, bf16[1,64,512]{2,1,0:T(8,128)(2,1)S(1)}, u32[]{:S(2)}, u32[]{:S(2)}) collective-permute-start(bf16[1,64,512]{2,1,0:T(8,128)(2,1)S(1)} %get-tuple-element.106), channel_id=1, source_target_pairs={{0,4},{2,6},{4,8},{6,10},{8,12},{10,14},{1,5},{3,7},{5,9},{7,11},{... | collective-permute-start | bytes 196616 | tf_op jit(solution)/shard_map/ppermute | solution.py:105
  120.3 7.8 %collective-permute-done.21.refs_1_ = bf16[1,64,512]{2,1,0:T(8,128)(2,1)S(1)} collective-permute-done((bf16[1,64,512]{2,1,0:T(8,128)(2,1)S(1)}, bf16[1,64,512]{2,1,0:T(8,128)(2,1)S(1)}, u32[]{:S(2)}, u32[]{:S(2)}) %collective-permute-start.21) | collective-permute-done | bytes 65568 | tf_op jit(solution)/shard_map/ppermute | solution.py:105
  128.1 1.9 %collective-permute-done.22.refs_2_ = bf16[1,64,512]{2,1,0:T(8,128)(2,1)S(1)} collective-permute-done((bf16[1,64,512]{2,1,0:T(8,128)(2,1)S(1)}, bf16[1,64,512]{2,1,0:T(8,128)(2,1)S(1)}, u32[]{:S(2)}, u32[]{:S(2)}) %collective-permute-start.22) | collective-permute-done | bytes 65568 | tf_op jit(solution)/shard_map/ppermute | solution.py:106
  131.6 4.3 %back_block.3 = bf16[1,512,1024]{2,1,0:T(8,128)(2,1)S(1)} custom-call(bf16[512,512]{1,0:T(8,128)(2,1)S(1)} %get-tuple-element.98.dpre.refs_0_, bf16[1,64,512]{2,1,0:T(8,128)(2,1)S(1)} %collective-permute-done.21.refs_1_, bf16[1,64,512]{2,1,0:T(8,128)(2,1)S(1)} %collective-permute-done.22.refs_2_, bf16[1,512,1024]{2,1,0:T(8,128)(2,1)S(1)} %pad_maximum_fusion.1.x_ref.refs_3_, ...), custom_call_target="tpu_custom_call" | custom-call | flops 2147483648 | bytes 8388608 | tf_op jit(solution)/shard_map/back_block/pallas_call | solution.py:428
  135.9 10.2 %collective-permute-done.24 = bf16[2,128,1024]{2,1,0:T(8,128)(2,1)S(1)} collective-permute-done((bf16[2,128,1024]{2,1,0:T(8,128)(2,1)S(1)}, bf16[2,128,1024]{2,1,0:T(8,128)(2,1)S(1)}, u32[]{:S(2)}, u32[]{:S(2)}) %collective-permute-start.24) | collective-permute-done | bytes 524320 | tf_op jit(solution)/shard_map/ppermute | solution.py:84
  146.1 4.4 %collective-permute-done.23 = bf16[4,128,1024]{2,1,0:T(8,128)(2,1)S(1)} collective-permute-done((bf16[4,128,1024]{2,1,0:T(8,128)(2,1)S(1)}, bf16[4,128,1024]{2,1,0:T(8,128)(2,1)S(1)}, u32[]{:S(2)}, u32[]{:S(2)}) %collective-permute-start.23) | collective-permute-done | bytes 1048608 | tf_op jit(solution)/shard_map/ppermute | solution.py:84
  151.9 8.5 %collective-permute-done.25 = bf16[1,128,1024]{2,1,0:T(8,128)(2,1)S(1)} collective-permute-done((bf16[1,128,1024]{2,1,0:T(8,128)(2,1)S(1)}, bf16[1,128,1024]{2,1,0:T(8,128)(2,1)S(1)}, u32[]{:S(2)}, u32[]{:S(2)}) %collective-permute-start.25) | collective-permute-done | bytes 262176 | tf_op jit(solution)/shard_map/ppermute | solution.py:84
  162.3 1.7 collective-permute-start.28
  165.5 11.1 %collective-permute-done.28 = bf16[1,128,1024]{2,1,0:T(8,128)(2,1)S(1)} collective-permute-done((bf16[1,128,1024]{2,1,0:T(8,128)(2,1)S(1)}, bf16[1,128,1024]{2,1,0:T(8,128)(2,1)S(1)}, u32[]{:S(2)}, u32[]{:S(2)}) %collective-permute-start.28) | collective-permute-done | bytes 262176 | tf_op jit(solution)/shard_map/ppermute | solution.py:84
  (107 shorter events, 30.0 us)
Async XLA Ops:
  3.3 4.4 %collective-permute-start = (bf16[64,1024]{1,0:T(8,128)(2,1)S(1)}, bf16[64,1024]{1,0:T(8,128)(2,1)S(1)}, u32[]{:S(2)}, u32[]{:S(2)}) collective-permute-start(bf16[64,1024]{1,0:T(8,128)(2,1)S(1)} %broadcast_select_fusion.18), channel_id=1, source_target_pairs={{0,1},{1,0},{2,3},{3,2},{4,5},{5,4},{6,7},{7,6},{8,9},{9,8},{10,11... | collective-permute-start | bytes 393224 | tf_op jit(solution)/shard_map/ppermute | solution.py:74
  5.1 18.7 %copy-start.1 = (bf16[2,256,1024]{2,1,0:T(8,128)(2,1)S(1)}, bf16[2,256,1024]{2,1,0:T(8,128)(2,1)}, u32[]{:S(2)}) copy-start(bf16[2,256,1024]{2,1,0:T(8,128)(2,1)} %param.7) | copy-start | bytes 3145732
  5.1 18.7 %collective-permute-start.5 = (bf16[1,256,1024]{2,1,0:T(8,128)(2,1)S(1)}, bf16[1,256,1024]{2,1,0:T(8,128)(2,1)S(1)}, u32[]{:S(2)}, u32[]{:S(2)}) collective-permute-start(bf16[1,256,1024]{2,1,0:T(8,128)(2,1)S(1)} %broadcast_select_fusion.10), channel_id=1, source_target_pairs={{0,2},{2,0},{4,6},{6,4},{8,10},{10,8},{12,14},{14,12},{1,3},{3,1},... | collective-permute-start | bytes 1572872 | tf_op jit(solution)/shard_map/ppermute | solution.py:112
  8.0 2.9 %collective-permute-start.3 = (bf16[64,1024]{1,0:T(8,128)(2,1)S(1)}, bf16[64,1024]{1,0:T(8,128)(2,1)S(1)}, u32[]{:S(2)}, u32[]{:S(2)}) collective-permute-start(bf16[64,1024]{1,0:T(8,128)(2,1)S(1)} %broadcast_select_fusion.14), channel_id=1, source_target_pairs={{0,1},{1,0},{2,3},{3,2},{4,5},{5,4},{6,7},{7,6},{8,9},{9,8},{10,11... | collective-permute-start | bytes 393224 | tf_op jit(solution)/shard_map/ppermute | solution.py:74
  8.2 15.0 %collective-permute-start.1 = (bf16[1,128,1024]{2,1,0:T(8,128)(2,1)S(1)}, bf16[1,128,1024]{2,1,0:T(8,128)(2,1)S(1)}, u32[]{:S(2)}, u32[]{:S(2)}) collective-permute-start(bf16[1,128,1024]{2,1,0:T(8,128)(2,1)S(1)} %maximum_bitcast_fusion), channel_id=1, source_target_pairs={{0,8},{1,9},{2,10},{3,11},{4,12},{5,13},{6,14},{7,15},{8,0},{9,1},... | collective-permute-start | bytes 786440 | tf_op jit(solution)/shard_map/ppermute | solution.py:84
  23.3 17.9 %collective-permute-start.2 = (bf16[2,128,1024]{2,1,0:T(8,128)(2,1)S(1)}, bf16[2,128,1024]{2,1,0:T(8,128)(2,1)S(1)}, u32[]{:S(2)}, u32[]{:S(2)}) collective-permute-start(bf16[2,128,1024]{2,1,0:T(8,128)(2,1)S(1)} %constant_dynamic-update-slice_fusion), channel_id=1, source_target_pairs={{0,2},{1,5},{2,0},{3,7},{4,6},{5,1},{6,4},{7,3},{8,10},{9,13},{10,... | collective-permute-start | bytes 1572872 | tf_op jit(solution)/shard_map/ppermute | solution.py:84
  23.9 19.9 %collective-permute-start.8 = (bf16[1,256,1024]{2,1,0:T(8,128)(2,1)S(1)}, bf16[1,256,1024]{2,1,0:T(8,128)(2,1)S(1)}, u32[]{:S(2)}, u32[]{:S(2)}) collective-permute-start(bf16[1,256,1024]{2,1,0:T(8,128)(2,1)S(1)} %broadcast_select_fusion.7), channel_id=1, source_target_pairs={{0,2},{2,0},{4,6},{6,4},{8,10},{10,8},{12,14},{14,12},{1,3},{3,1},... | collective-permute-start | bytes 1572872 | tf_op jit(solution)/shard_map/ppermute | solution.py:112
  25.5 15.6 %collective-permute-start.4 = (bf16[1,128,1024]{2,1,0:T(8,128)(2,1)S(1)}, bf16[1,128,1024]{2,1,0:T(8,128)(2,1)S(1)}, u32[]{:S(2)}, u32[]{:S(2)}) collective-permute-start(bf16[1,128,1024]{2,1,0:T(8,128)(2,1)S(1)} %maximum_bitcast_fusion.1), channel_id=1, source_target_pairs={{0,8},{1,9},{2,10},{3,11},{4,12},{5,13},{6,14},{7,15},{8,0},{9,1},... | collective-permute-start | bytes 786440 | tf_op jit(solution)/shard_map/ppermute | solution.py:84
  25.8 9.9 %collective-permute-start.6 = (bf16[1,64,1024]{2,1,0:T(8,128)(2,1)S(1)}, bf16[1,64,1024]{2,1,0:T(8,128)(2,1)S(1)}, u32[]{:S(2)}, u32[]{:S(2)}) collective-permute-start(bf16[1,64,1024]{2,1,0:T(8,128)(2,1)S(1)} %slice.178), channel_id=1, source_target_pairs={{0,4},{2,6},{4,8},{6,10},{8,12},{10,14},{1,5},{3,7},{5,9},{7,11},{... | collective-permute-start | bytes 393224 | tf_op jit(solution)/shard_map/ppermute | solution.py:105
  31.7 7.3 %collective-permute-start.7 = (bf16[1,64,1024]{2,1,0:T(8,128)(2,1)S(1)}, bf16[1,64,1024]{2,1,0:T(8,128)(2,1)S(1)}, u32[]{:S(2)}, u32[]{:S(2)}) collective-permute-start(bf16[1,64,1024]{2,1,0:T(8,128)(2,1)S(1)} %slice.179), channel_id=1, source_target_pairs={{4,0},{6,2},{8,4},{10,6},{12,8},{14,10},{5,1},{7,3},{9,5},{11,7},{... | collective-permute-start | bytes 393224 | tf_op jit(solution)/shard_map/ppermute | solution.py:106
  43.9 20.0 %collective-permute-start.9 = (bf16[4,128,1024]{2,1,0:T(8,128)(2,1)S(1)}, bf16[4,128,1024]{2,1,0:T(8,128)(2,1)S(1)}, u32[]{:S(2)}, u32[]{:S(2)}) collective-permute-start(bf16[4,128,1024]{2,1,0:T(8,128)(2,1)S(1)} %pad_maximum_fusion.2), channel_id=1, source_target_pairs={{0,4},{1,3},{2,6},{3,1},{4,0},{5,7},{6,2},{7,5},{8,12},{9,11},{10,... | collective-permute-start | bytes 3145736 | tf_op jit(solution)/shard_map/ppermute | solution.py:84
  45.1 14.9 %collective-permute-start.10 = (bf16[2,128,1024]{2,1,0:T(8,128)(2,1)S(1)}, bf16[2,128,1024]{2,1,0:T(8,128)(2,1)S(1)}, u32[]{:S(2)}, u32[]{:S(2)}) collective-permute-start(bf16[2,128,1024]{2,1,0:T(8,128)(2,1)S(1)} %pad_maximum_fusion.6), channel_id=1, source_target_pairs={{0,2},{1,5},{2,0},{3,7},{4,6},{5,1},{6,4},{7,3},{8,10},{9,13},{10,... | collective-permute-start | bytes 1572872 | tf_op jit(solution)/shard_map/ppermute | solution.py:84
  63.9 4.2 %collective-permute-start.11 = (bf16[8,128,1024]{2,1,0:T(8,128)(2,1)S(1)}, bf16[8,128,1024]{2,1,0:T(8,128)(2,1)S(1)}, u32[]{:S(2)}, u32[]{:S(2)}) collective-permute-start(bf16[8,128,1024]{2,1,0:T(8,128)(2,1)S(1)} %constant_dynamic-update-slice_fusion.2.own.refs_7_.refs_5_), channel_id=1, source_target_pairs={{0,1},{1,0},{2,3},{3,2},{4,5},{5,4},{6,7},{7,6},{8,9},{9,8},{10,11... | collective-permute-start | bytes 6291464 | tf_op jit(solution)/shard_map/ppermute | solution.py:74
  64.1 17.7 %collective-permute-start.12 = (bf16[4,128,1024]{2,1,0:T(8,128)(2,1)S(1)}, bf16[4,128,1024]{2,1,0:T(8,128)(2,1)S(1)}, u32[]{:S(2)}, u32[]{:S(2)}) collective-permute-start(bf16[4,128,1024]{2,1,0:T(8,128)(2,1)S(1)} %pad_maximum_fusion.3), channel_id=1, source_target_pairs={{0,4},{1,3},{2,6},{3,1},{4,0},{5,7},{6,2},{7,5},{8,12},{9,11},{10,... | collective-permute-start | bytes 3145736 | tf_op jit(solution)/shard_map/ppermute | solution.py:84
  71.1 13.5 %collective-permute-start.14 = (bf16[1,128,1024]{2,1,0:T(8,128)(2,1)S(1)}, bf16[1,128,1024]{2,1,0:T(8,128)(2,1)S(1)}, u32[]{:S(2)}, u32[]{:S(2)}) collective-permute-start(bf16[1,128,1024]{2,1,0:T(8,128)(2,1)S(1)} %get-tuple-element.75.first), channel_id=1, source_target_pairs={{4,0},{6,2},{8,4},{10,6},{12,8},{14,10},{5,1},{7,3},{9,5},{11,7},{... | collective-permute-start | bytes 786440 | tf_op jit(solution)/shard_map/ppermute | solution.py:106
  72.4 12.2 %collective-permute-start.13 = (bf16[1,128,1024]{2,1,0:T(8,128)(2,1)S(1)}, bf16[1,128,1024]{2,1,0:T(8,128)(2,1)S(1)}, u32[]{:S(2)}, u32[]{:S(2)}) collective-permute-start(bf16[1,128,1024]{2,1,0:T(8,128)(2,1)S(1)} %get-tuple-element.76.last), channel_id=1, source_target_pairs={{0,4},{2,6},{4,8},{6,10},{8,12},{10,14},{1,5},{3,7},{5,9},{7,11},{... | collective-permute-start | bytes 786440 | tf_op jit(solution)/shard_map/ppermute | solution.py:105
  84.8 4.2 %collective-permute-start.15 = (bf16[8,128,1024]{2,1,0:T(8,128)(2,1)S(1)}, bf16[8,128,1024]{2,1,0:T(8,128)(2,1)S(1)}, u32[]{:S(2)}, u32[]{:S(2)}) collective-permute-start(bf16[8,128,1024]{2,1,0:T(8,128)(2,1)S(1)} %pad_maximum_fusion.own.refs_5_), channel_id=1, source_target_pairs={{0,1},{1,0},{2,3},{3,2},{4,5},{5,4},{6,7},{7,6},{8,9},{9,8},{10,11... | collective-permute-start | bytes 6291464 | tf_op jit(solution)/shard_map/ppermute | solution.py:74
  92.2 8.5 %collective-permute-start.16 = (bf16[1,128,512]{2,1,0:T(8,128)(2,1)S(1)}, bf16[1,128,512]{2,1,0:T(8,128)(2,1)S(1)}, u32[]{:S(2)}, u32[]{:S(2)}) collective-permute-start(bf16[1,128,512]{2,1,0:T(8,128)(2,1)S(1)} %get-tuple-element.87), channel_id=1, source_target_pairs={{0,4},{2,6},{4,8},{6,10},{8,12},{10,14},{1,5},{3,7},{5,9},{7,11},{... | collective-permute-start | bytes 393224 | tf_op jit(solution)/shard_map/ppermute | solution.py:105
  95.8 7.2 %collective-permute-start.17 = (bf16[1,128,512]{2,1,0:T(8,128)(2,1)S(1)}, bf16[1,128,512]{2,1,0:T(8,128)(2,1)S(1)}, u32[]{:S(2)}, u32[]{:S(2)}) collective-permute-start(bf16[1,128,512]{2,1,0:T(8,128)(2,1)S(1)} %get-tuple-element.88), channel_id=1, source_target_pairs={{4,0},{6,2},{8,4},{10,6},{12,8},{14,10},{5,1},{7,3},{9,5},{11,7},{... | collective-permute-start | bytes 393224 | tf_op jit(solution)/shard_map/ppermute | solution.py:106
  102.9 5.5 %collective-permute-start.18 = (bf16[8,128,1024]{2,1,0:T(8,128)(2,1)S(1)}, bf16[8,128,1024]{2,1,0:T(8,128)(2,1)S(1)}, u32[]{:S(2)}, u32[]{:S(2)}) collective-permute-start(bf16[8,128,1024]{2,1,0:T(8,128)(2,1)S(1)} %get-tuple-element.90), channel_id=1, source_target_pairs={{0,1},{1,0},{2,3},{3,2},{4,5},{5,4},{6,7},{7,6},{8,9},{9,8},{10,11... | collective-permute-start | bytes 6291464 | tf_op jit(solution)/shard_map/ppermute | solution.py:74
  112.9 6.2 %collective-permute-start.20 = (bf16[8,128,1024]{2,1,0:T(8,128)(2,1)S(1)}, bf16[8,128,1024]{2,1,0:T(8,128)(2,1)S(1)}, u32[]{:S(2)}, u32[]{:S(2)}) collective-permute-start(bf16[8,128,1024]{2,1,0:T(8,128)(2,1)S(1)} %get-tuple-element.103), channel_id=1, source_target_pairs={{0,1},{1,0},{2,3},{3,2},{4,5},{5,4},{6,7},{7,6},{8,9},{9,8},{10,11... | collective-permute-start | bytes 6291464 | tf_op jit(solution)/shard_map/ppermute | solution.py:74
  113.7 16.3 %collective-permute-start.19 = (bf16[4,128,1024]{2,1,0:T(8,128)(2,1)S(1)}, bf16[4,128,1024]{2,1,0:T(8,128)(2,1)S(1)}, u32[]{:S(2)}, u32[]{:S(2)}) collective-permute-start(bf16[4,128,1024]{2,1,0:T(8,128)(2,1)S(1)} %slice.275), channel_id=1, source_target_pairs={{0,4},{1,3},{2,6},{3,1},{4,0},{5,7},{6,2},{7,5},{8,12},{9,11},{10,... | collective-permute-start | bytes 3145736 | tf_op jit(solution)/shard_map/ppermute | solution.py:84
  114.3 13.7 %collective-permute-start.21 = (bf16[1,64,512]{2,1,0:T(8,128)(2,1)S(1)}, bf16[1,64,512]{2,1,0:T(8,128)(2,1)S(1)}, u32[]{:S(2)}, u32[]{:S(2)}) collective-permute-start(bf16[1,64,512]{2,1,0:T(8,128)(2,1)S(1)} %get-tuple-element.106), channel_id=1, source_target_pairs={{0,4},{2,6},{4,8},{6,10},{8,12},{10,14},{1,5},{3,7},{5,9},{7,11},{... | collective-permute-start | bytes 196616 | tf_op jit(solution)/shard_map/ppermute | solution.py:105
  117.7 12.3 %collective-permute-start.22 = (bf16[1,64,512]{2,1,0:T(8,128)(2,1)S(1)}, bf16[1,64,512]{2,1,0:T(8,128)(2,1)S(1)}, u32[]{:S(2)}, u32[]{:S(2)}) collective-permute-start(bf16[1,64,512]{2,1,0:T(8,128)(2,1)S(1)} %get-tuple-element.107), channel_id=1, source_target_pairs={{4,0},{6,2},{8,4},{10,6},{12,8},{14,10},{5,1},{7,3},{9,5},{11,7},{... | collective-permute-start | bytes 196616 | tf_op jit(solution)/shard_map/ppermute | solution.py:106
  130.1 20.4 %collective-permute-start.23 = (bf16[4,128,1024]{2,1,0:T(8,128)(2,1)S(1)}, bf16[4,128,1024]{2,1,0:T(8,128)(2,1)S(1)}, u32[]{:S(2)}, u32[]{:S(2)}) collective-permute-start(bf16[4,128,1024]{2,1,0:T(8,128)(2,1)S(1)} %slice.274), channel_id=1, source_target_pairs={{0,4},{1,3},{2,6},{3,1},{4,0},{5,7},{6,2},{7,5},{8,12},{9,11},{10,... | collective-permute-start | bytes 3145736 | tf_op jit(solution)/shard_map/ppermute | solution.py:84
  131.2 14.9 %collective-permute-start.24 = (bf16[2,128,1024]{2,1,0:T(8,128)(2,1)S(1)}, bf16[2,128,1024]{2,1,0:T(8,128)(2,1)S(1)}, u32[]{:S(2)}, u32[]{:S(2)}) collective-permute-start(bf16[2,128,1024]{2,1,0:T(8,128)(2,1)S(1)} %slice.277), channel_id=1, source_target_pairs={{0,2},{1,9},{2,0},{3,11},{4,6},{5,13},{6,4},{7,15},{8,10},{9,1},{1... | collective-permute-start | bytes 1572872 | tf_op jit(solution)/shard_map/ppermute | solution.py:84
  150.7 9.8 %collective-permute-start.25 = (bf16[1,128,1024]{2,1,0:T(8,128)(2,1)S(1)}, bf16[1,128,1024]{2,1,0:T(8,128)(2,1)S(1)}, u32[]{:S(2)}, u32[]{:S(2)}) collective-permute-start(bf16[1,128,1024]{2,1,0:T(8,128)(2,1)S(1)} %slice.279), channel_id=1, source_target_pairs={{0,8},{1,5},{2,10},{3,7},{4,12},{5,1},{6,14},{7,3},{8,0},{9,13},{1... | collective-permute-start | bytes 786440 | tf_op jit(solution)/shard_map/ppermute | solution.py:84
  151.1 9.5 %collective-permute-start.27 = (bf16[2,128,1024]{2,1,0:T(8,128)(2,1)S(1)}, bf16[2,128,1024]{2,1,0:T(8,128)(2,1)S(1)}, u32[]{:S(2)}, u32[]{:S(2)}) collective-permute-start(bf16[2,128,1024]{2,1,0:T(8,128)(2,1)S(1)} %slice.276), channel_id=1, source_target_pairs={{0,2},{1,5},{2,0},{3,7},{4,6},{5,1},{6,4},{7,3},{8,10},{9,13},{10,... | collective-permute-start | bytes 1572872 | tf_op jit(solution)/shard_map/ppermute | solution.py:84
  160.6 1.6 collective-permute-start.26
  160.6 16.0 %collective-permute-start.29 = (bf16[1,256,1024]{2,1,0:T(8,128)(2,1)S(1)}, bf16[1,256,1024]{2,1,0:T(8,128)(2,1)S(1)}, u32[]{:S(2)}, u32[]{:S(2)}) collective-permute-start(bf16[1,256,1024]{2,1,0:T(8,128)(2,1)S(1)} %broadcast_select_fusion.2), channel_id=1, source_target_pairs={{0,2},{2,0},{4,6},{6,4},{8,10},{10,8},{12,14},{14,12},{1,3},{3,1},... | collective-permute-start | bytes 1572872 | tf_op jit(solution)/shard_map/ppermute | solution.py:112
  162.3 14.3 %collective-permute-start.28 = (bf16[1,128,1024]{2,1,0:T(8,128)(2,1)S(1)}, bf16[1,128,1024]{2,1,0:T(8,128)(2,1)S(1)}, u32[]{:S(2)}, u32[]{:S(2)}) collective-permute-start(bf16[1,128,1024]{2,1,0:T(8,128)(2,1)S(1)} %slice.278), channel_id=1, source_target_pairs={{0,8},{1,9},{2,10},{3,11},{4,12},{5,13},{6,14},{7,15},{8,0},{9,1},... | collective-permute-start | bytes 786440 | tf_op jit(solution)/shard_map/ppermute | solution.py:84
  176.7 1.6 collective-permute-start.30
  (3 other events, 31.2 us)

commit v7 on v6

--- a/solution.py
+++ b/solution.py
@@ -556,7 +556,7 @@
             got_g = swap_pair(gives_g)
     total_two = fold(total_two, got_two)
     grads_two = unpack(total_two[0], middle)
-    grads_two, got_one, got_g = tie(grads_two, got_one, got_g)
+    got_one, got_g = tie(got_one, got_g)
     total_one = fold(total_one, got_one)
     input_grad = join_pair(mine_g, got_g, 0)
     return (input_grad, *unpack(total_one[0], middle), *grads_two)

time: 180 us -> 180 us (level)
  transfers between devices with their start and end apart: 31 -> 31, of which waited for: 20 -> 19; matrix products, arithmetic and copies ran while one was open for 4% -> 3% of each run, Pallas kernels for 10% -> 10%
where the time goes in v7:
time: 180 us
  waiting for transfers between devices  99.5 us (55%)
  starting transfers between devices  42.2 us (23%)
  Pallas kernels  24.8 us (14%)
  other arithmetic  8.55 us (5%)
  local copies, waits for them, and re-layouts  3.47 us (2%)
    ppermute x12, waiting for transfers between devices, hop(): return lax.ppermute(value, ('seq', 'dp'), pairs)  69.7 us
    ppermute x4, starting transfers between devices, halo(): low = lax.ppermute(last, 'seq', [(i, i + 2) for i in range(count - 2)])  17.4 us
    ppermute x12, starting transfers between devices, hop(): return lax.ppermute(value, ('seq', 'dp'), pairs)  13 us
    ppermute x4, waiting for transfers between devices, halo(): low = lax.ppermute(last, 'seq', [(i, i + 2) for i in range(count - 2)])  10.4 us
    ppermute x4, waiting for transfers between devices, halo(): high = lax.ppermute(first, 'seq', [(i + 2, i) for i in range(count - 2)])  10.3 us
    pallas_call x2, Pallas kernels, back_block(): pl.pallas_call(functools.partial(back_kernel, orders, dilate, orders_m),...  9.8 us
    pallas_call x2, Pallas kernels, grads_block(): pl.pallas_call(functools.partial(grads_kernel, orders, dilate), out_shape...  7.05 us
    ppermute x8, waiting for transfers between devices, cross(): return lax.ppermute(value, 'dp', [(0, 1), (1, 0)])  6.5 us
  transfers between devices with their start and end apart: 31, of which 19 were waited for; matrix products, arithmetic and copies ran while one was open for 3% of the time, Pallas kernels for 10%

profile of v7, /device:TPU:0, one launch (start us, length us, event | category | flops | bytes accessed | tf_op | source)
XLA Modules:
  0.0 179.6 jit_solution(7758192327855574043)
XLA Ops:
  5.1 2.6 %collective-permute-start.5 = (bf16[1,256,1024]{2,1,0:T(8,128)(2,1)S(1)}, bf16[1,256,1024]{2,1,0:T(8,128)(2,1)S(1)}, u32[]{:S(2)}, u32[]{:S(2)}) collective-permute-start(bf16[1,256,1024]{2,1,0:T(8,128)(2,1)S(1)} %broadcast_select_fusion.10), channel_id=1, source_target_pairs={{0,2},{2,0},{4,6},{6,4},{8,10},{10,8},{12,14},{14,12},{1,3},{3,1},... | collective-permute-start | bytes 1572872 | tf_op jit(solution)/shard_map/ppermute | solution.py:112
  8.2 2.6 %collective-permute-start.1 = (bf16[1,128,1024]{2,1,0:T(8,128)(2,1)S(1)}, bf16[1,128,1024]{2,1,0:T(8,128)(2,1)S(1)}, u32[]{:S(2)}, u32[]{:S(2)}) collective-permute-start(bf16[1,128,1024]{2,1,0:T(8,128)(2,1)S(1)} %maximum_bitcast_fusion), channel_id=1, source_target_pairs={{0,8},{1,9},{2,10},{3,11},{4,12},{5,13},{6,14},{7,15},{8,0},{9,1},... | collective-permute-start | bytes 786440 | tf_op jit(solution)/shard_map/ppermute | solution.py:84
  10.9 12.3 %collective-permute-done.1 = bf16[1,128,1024]{2,1,0:T(8,128)(2,1)S(1)} collective-permute-done((bf16[1,128,1024]{2,1,0:T(8,128)(2,1)S(1)}, bf16[1,128,1024]{2,1,0:T(8,128)(2,1)S(1)}, u32[]{:S(2)}, u32[]{:S(2)}) %collective-permute-start.1) | collective-permute-done | bytes 262176 | tf_op jit(solution)/shard_map/ppermute | solution.py:84
  25.8 5.9 %collective-permute-start.6 = (bf16[1,64,1024]{2,1,0:T(8,128)(2,1)S(1)}, bf16[1,64,1024]{2,1,0:T(8,128)(2,1)S(1)}, u32[]{:S(2)}, u32[]{:S(2)}) collective-permute-start(bf16[1,64,1024]{2,1,0:T(8,128)(2,1)S(1)} %slice.178), channel_id=1, source_target_pairs={{0,4},{2,6},{4,8},{6,10},{8,12},{10,14},{1,5},{3,7},{5,9},{7,11},{... | collective-permute-start | bytes 393224 | tf_op jit(solution)/shard_map/ppermute | solution.py:105
  33.1 2.5 %collective-permute-done.6.low_ref = bf16[1,64,1024]{2,1,0:T(8,128)(2,1)S(1)} collective-permute-done((bf16[1,64,1024]{2,1,0:T(8,128)(2,1)S(1)}, bf16[1,64,1024]{2,1,0:T(8,128)(2,1)S(1)}, u32[]{:S(2)}, u32[]{:S(2)}) %collective-permute-start.6) | collective-permute-done | bytes 131104 | tf_op jit(solution)/shard_map/ppermute | solution.py:105
  35.6 3.4 %collective-permute-done.7.high_ref = bf16[1,64,1024]{2,1,0:T(8,128)(2,1)S(1)} collective-permute-done((bf16[1,64,1024]{2,1,0:T(8,128)(2,1)S(1)}, bf16[1,64,1024]{2,1,0:T(8,128)(2,1)S(1)}, u32[]{:S(2)}, u32[]{:S(2)}) %collective-permute-start.7) | collective-permute-done | bytes 131104 | tf_op jit(solution)/shard_map/ppermute | solution.py:106
  39.0 1.8 norm_ext.1.ext
  41.2 2.6 %collective-permute-done.8 = bf16[1,256,1024]{2,1,0:T(8,128)(2,1)S(1)} collective-permute-done((bf16[1,256,1024]{2,1,0:T(8,128)(2,1)S(1)}, bf16[1,256,1024]{2,1,0:T(8,128)(2,1)S(1)}, u32[]{:S(2)}, u32[]{:S(2)}) %collective-permute-start.8) | collective-permute-done | bytes 524320 | tf_op jit(solution)/shard_map/ppermute | solution.py:112
  46.8 13.3 %collective-permute-done.10 = bf16[2,128,1024]{2,1,0:T(8,128)(2,1)S(1)} collective-permute-done((bf16[2,128,1024]{2,1,0:T(8,128)(2,1)S(1)}, bf16[2,128,1024]{2,1,0:T(8,128)(2,1)S(1)}, u32[]{:S(2)}, u32[]{:S(2)}) %collective-permute-start.10) | collective-permute-done | bytes 524320 | tf_op jit(solution)/shard_map/ppermute | solution.py:84
  60.1 3.7 %collective-permute-done.9 = bf16[4,128,1024]{2,1,0:T(8,128)(2,1)S(1)} collective-permute-done((bf16[4,128,1024]{2,1,0:T(8,128)(2,1)S(1)}, bf16[4,128,1024]{2,1,0:T(8,128)(2,1)S(1)}, u32[]{:S(2)}, u32[]{:S(2)}) %collective-permute-start.9) | collective-permute-done | bytes 1048608 | tf_op jit(solution)/shard_map/ppermute | solution.py:84
  64.1 1.8 collective-permute-start.12
  65.8 2.3 %collective-permute-done.11.other.refs_8_.refs_6_ = bf16[8,128,1024]{2,1,0:T(8,128)(2,1)S(1)} collective-permute-done((bf16[8,128,1024]{2,1,0:T(8,128)(2,1)S(1)}, bf16[8,128,1024]{2,1,0:T(8,128)(2,1)S(1)}, u32[]{:S(2)}, u32[]{:S(2)}) %collective-permute-start.11) | collective-permute-done | bytes 2097184 | tf_op jit(solution)/shard_map/ppermute | solution.py:74
  68.1 3.0 %forward_block.1 = (f32[512,512]{1,0:T(8,128)S(1)}, bf16[512,512]{1,0:T(8,128)(2,1)S(1)}, bf16[1,512,1024]{2,1,0:T(8,128)(2,1)S(1)}, bf16[1,128,1024]{2,1,0:T(8,128)(2,1)S(1)}, bf16[1,128,1024]{2,1,0:T(8,128)(2,1)S(1)}) custom-call(bf16[1,640,1024]{2,1,0:T(8,128)(2,1)S(1)} %norm_ext.1.ext, bf16[1,512,1024]{2,1,0:T(8,128)(2,1)S(1)} %pad_maximum_fusion.1.x_ref.refs_3_, ...), custom_call_target="tpu_custom_call" | custom-call | flops 2147483648 | bytes 8388608 | tf_op jit(solution)/shard_map/forward_block/pallas_call | solution.py:233
  72.4 4.6 %collective-permute-start.13 = (bf16[1,128,1024]{2,1,0:T(8,128)(2,1)S(1)}, bf16[1,128,1024]{2,1,0:T(8,128)(2,1)S(1)}, u32[]{:S(2)}, u32[]{:S(2)}) collective-permute-start(bf16[1,128,1024]{2,1,0:T(8,128)(2,1)S(1)} %get-tuple-element.74.last), channel_id=1, source_target_pairs={{0,4},{2,6},{4,8},{6,10},{8,12},{10,14},{1,5},{3,7},{5,9},{7,11},{... | collective-permute-start | bytes 786440 | tf_op jit(solution)/shard_map/ppermute | solution.py:105
  77.0 4.8 %collective-permute-done.12 = bf16[4,128,1024]{2,1,0:T(8,128)(2,1)S(1)} collective-permute-done((bf16[4,128,1024]{2,1,0:T(8,128)(2,1)S(1)}, bf16[4,128,1024]{2,1,0:T(8,128)(2,1)S(1)}, u32[]{:S(2)}, u32[]{:S(2)}) %collective-permute-start.12) | collective-permute-done | bytes 1048608 | tf_op jit(solution)/shard_map/ppermute | solution.py:84
  81.8 2.8 %collective-permute-done.14.high = bf16[1,128,1024]{2,1,0:T(8,128)(2,1)S(1)} collective-permute-done((bf16[1,128,1024]{2,1,0:T(8,128)(2,1)S(1)}, bf16[1,128,1024]{2,1,0:T(8,128)(2,1)S(1)}, u32[]{:S(2)}, u32[]{:S(2)}) %collective-permute-start.14) | collective-permute-done | bytes 262176 | tf_op jit(solution)/shard_map/ppermute | solution.py:106
  85.1 3.9 %collective-permute-done.15.other.refs_6_ = bf16[8,128,1024]{2,1,0:T(8,128)(2,1)S(1)} collective-permute-done((bf16[8,128,1024]{2,1,0:T(8,128)(2,1)S(1)}, bf16[8,128,1024]{2,1,0:T(8,128)(2,1)S(1)}, u32[]{:S(2)}, u32[]{:S(2)}) %collective-permute-start.15) | collective-permute-done | bytes 2097184 | tf_op jit(solution)/shard_map/ppermute | solution.py:74
  89.0 3.2 %turn_block.1 = (bf16[1,768,1024]{2,1,0:T(8,128)(2,1)S(1)}, bf16[512,512]{1,0:T(8,128)(2,1)S(1)}, bf16[512,512]{1,0:T(8,128)(2,1)S(1)}, bf16[1,128,512]{2,1,0:T(8,128)(2,1)S(1)}, bf16[1,128,512]{2,1,0:T(8,128)(2,1)S(1)}) custom-call(bf16[1,128,1024]{2,1,0:T(8,128)(2,1)S(1)} %get-tuple-element.73.first, bf16[1,128,1024]{2,1,0:T(8,128)(2,1)S(1)} %get-tuple-element.74.last, ...), custom_call_target="tpu_custom_call" | custom-call | flops 2147483648 | bytes 8388608 | tf_op jit(solution)/shard_map/turn_block/pallas_call | solution.py:283
  92.2 3.6 %collective-permute-start.16 = (bf16[1,128,512]{2,1,0:T(8,128)(2,1)S(1)}, bf16[1,128,512]{2,1,0:T(8,128)(2,1)S(1)}, u32[]{:S(2)}, u32[]{:S(2)}) collective-permute-start(bf16[1,128,512]{2,1,0:T(8,128)(2,1)S(1)} %get-tuple-element.85), channel_id=1, source_target_pairs={{0,4},{2,6},{4,8},{6,10},{8,12},{10,14},{1,5},{3,7},{5,9},{7,11},{... | collective-permute-start | bytes 393224 | tf_op jit(solution)/shard_map/ppermute | solution.py:105
  97.1 3.6 %grads_block.2 = (f32[8,128,1024]{2,1,0:T(8,128)S(1)}, bf16[8,128,1024]{2,1,0:T(8,128)(2,1)S(1)}) custom-call(bf16[1,768,1024]{2,1,0:T(8,128)(2,1)S(1)} %get-tuple-element.81.ext, bf16[512,512]{1,0:T(8,128)(2,1)S(1)} %get-tuple-element.82.hid, bf16[1,512,1024]{2,1,0:T(8,128)(2,1)S(1)} %pad_maximum_fusion.4.e_ref.refs_4_, ...), custom_call_target="tpu_custom_call" | custom-call | flops 2147483648 | bytes 8388608 | tf_op jit(solution)/shard_map/grads_block/pallas_call | solution.py:349
  100.7 2.2 %collective-permute-done.17.refs_2_ = bf16[1,128,512]{2,1,0:T(8,128)(2,1)S(1)} collective-permute-done((bf16[1,128,512]{2,1,0:T(8,128)(2,1)S(1)}, bf16[1,128,512]{2,1,0:T(8,128)(2,1)S(1)}, u32[]{:S(2)}, u32[]{:S(2)}) %collective-permute-start.17) | collective-permute-done | bytes 131104 | tf_op jit(solution)/shard_map/ppermute | solution.py:106
  102.9 5.5 %back_block.2 = (bf16[1,512,1024]{2,1,0:T(8,128)(2,1)S(1)}, bf16[512,512]{1,0:T(8,128)(2,1)S(1)}, bf16[1,64,512]{2,1,0:T(8,128)(2,1)S(1)}, bf16[1,64,512]{2,1,0:T(8,128)(2,1)S(1)}) custom-call(bf16[512,512]{1,0:T(8,128)(2,1)S(1)} %get-tuple-element.83.dpre.refs_0_, bf16[1,128,512]{2,1,0:T(8,128)(2,1)S(1)} %collective-permute-done.16.refs_1_, ...), custom_call_target="tpu_custom_call" | custom-call | flops 2147483648 | bytes 8388608 | tf_op jit(solution)/shard_map/back_block/pallas_call | solution.py:428
  109.5 3.4 %grads_block.3 = (f32[8,128,1024]{2,1,0:T(8,128)S(1)}, bf16[8,128,1024]{2,1,0:T(8,128)(2,1)S(1)}) custom-call(bf16[1,640,1024]{2,1,0:T(8,128)(2,1)S(1)} %norm_ext.1.ext, bf16[512,512]{1,0:T(8,128)(2,1)S(1)} %get-tuple-element.98.hid, bf16[1,512,1024]{2,1,0:T(8,128)(2,1)S(1)} %get-tuple-element.99.e_ref.refs_4_, ...), custom_call_target="tpu_custom_call" | custom-call | flops 2147483648 | bytes 8388608 | tf_op jit(solution)/shard_map/grads_block/pallas_call | solution.py:349
  114.3 3.3 %collective-permute-start.21 = (bf16[1,64,512]{2,1,0:T(8,128)(2,1)S(1)}, bf16[1,64,512]{2,1,0:T(8,128)(2,1)S(1)}, u32[]{:S(2)}, u32[]{:S(2)}) collective-permute-start(bf16[1,64,512]{2,1,0:T(8,128)(2,1)S(1)} %get-tuple-element.104), channel_id=1, source_target_pairs={{0,4},{2,6},{4,8},{6,10},{8,12},{10,14},{1,5},{3,7},{5,9},{7,11},{... | collective-permute-start | bytes 196616 | tf_op jit(solution)/shard_map/ppermute | solution.py:105
  120.3 7.8 %collective-permute-done.21.refs_1_ = bf16[1,64,512]{2,1,0:T(8,128)(2,1)S(1)} collective-permute-done((bf16[1,64,512]{2,1,0:T(8,128)(2,1)S(1)}, bf16[1,64,512]{2,1,0:T(8,128)(2,1)S(1)}, u32[]{:S(2)}, u32[]{:S(2)}) %collective-permute-start.21) | collective-permute-done | bytes 65568 | tf_op jit(solution)/shard_map/ppermute | solution.py:105
  128.1 1.9 %collective-permute-done.22.refs_2_ = bf16[1,64,512]{2,1,0:T(8,128)(2,1)S(1)} collective-permute-done((bf16[1,64,512]{2,1,0:T(8,128)(2,1)S(1)}, bf16[1,64,512]{2,1,0:T(8,128)(2,1)S(1)}, u32[]{:S(2)}, u32[]{:S(2)}) %collective-permute-start.22) | collective-permute-done | bytes 65568 | tf_op jit(solution)/shard_map/ppermute | solution.py:106
  131.6 4.3 %back_block.3 = bf16[1,512,1024]{2,1,0:T(8,128)(2,1)S(1)} custom-call(bf16[512,512]{1,0:T(8,128)(2,1)S(1)} %get-tuple-element.96.dpre.refs_0_, bf16[1,64,512]{2,1,0:T(8,128)(2,1)S(1)} %collective-permute-done.21.refs_1_, bf16[1,64,512]{2,1,0:T(8,128)(2,1)S(1)} %collective-permute-done.22.refs_2_, bf16[1,512,1024]{2,1,0:T(8,128)(2,1)S(1)} %pad_maximum_fusion.1.x_ref.refs_3_, ...), custom_call_target="tpu_custom_call" | custom-call | flops 2147483648 | bytes 8388608 | tf_op jit(solution)/shard_map/back_block/pallas_call | solution.py:428
  135.9 10.2 %collective-permute-done.24 = bf16[2,128,1024]{2,1,0:T(8,128)(2,1)S(1)} collective-permute-done((bf16[2,128,1024]{2,1,0:T(8,128)(2,1)S(1)}, bf16[2,128,1024]{2,1,0:T(8,128)(2,1)S(1)}, u32[]{:S(2)}, u32[]{:S(2)}) %collective-permute-start.24) | collective-permute-done | bytes 524320 | tf_op jit(solution)/shard_map/ppermute | solution.py:84
  146.1 4.4 %collective-permute-done.23 = bf16[4,128,1024]{2,1,0:T(8,128)(2,1)S(1)} collective-permute-done((bf16[4,128,1024]{2,1,0:T(8,128)(2,1)S(1)}, bf16[4,128,1024]{2,1,0:T(8,128)(2,1)S(1)}, u32[]{:S(2)}, u32[]{:S(2)}) %collective-permute-start.23) | collective-permute-done | bytes 1048608 | tf_op jit(solution)/shard_map/ppermute | solution.py:84
  151.9 8.5 %collective-permute-done.29 = bf16[1,128,1024]{2,1,0:T(8,128)(2,1)S(1)} collective-permute-done((bf16[1,128,1024]{2,1,0:T(8,128)(2,1)S(1)}, bf16[1,128,1024]{2,1,0:T(8,128)(2,1)S(1)}, u32[]{:S(2)}, u32[]{:S(2)}) %collective-permute-start.29) | collective-permute-done | bytes 262176 | tf_op jit(solution)/shard_map/ppermute | solution.py:84
  160.8 2.7 %collective-permute-start.26 = (bf16[1,128,1024]{2,1,0:T(8,128)(2,1)S(1)}, bf16[1,128,1024]{2,1,0:T(8,128)(2,1)S(1)}, u32[]{:S(2)}, u32[]{:S(2)}) collective-permute-start(bf16[1,128,1024]{2,1,0:T(8,128)(2,1)S(1)} %slice.279), channel_id=1, source_target_pairs={{0,8},{1,9},{2,10},{3,11},{4,12},{5,13},{6,14},{7,15},{8,0},{9,1},... | collective-permute-start | bytes 786440 | tf_op jit(solution)/shard_map/ppermute | solution.py:84
  164.1 12.1 %collective-permute-done.26 = bf16[1,128,1024]{2,1,0:T(8,128)(2,1)S(1)} collective-permute-done((bf16[1,128,1024]{2,1,0:T(8,128)(2,1)S(1)}, bf16[1,128,1024]{2,1,0:T(8,128)(2,1)S(1)}, u32[]{:S(2)}, u32[]{:S(2)}) %collective-permute-start.26) | collective-permute-done | bytes 262176 | tf_op jit(solution)/shard_map/ppermute | solution.py:84
  (105 shorter events, 27.8 us)
Async XLA Ops:
  3.3 4.4 %collective-permute-start = (bf16[64,1024]{1,0:T(8,128)(2,1)S(1)}, bf16[64,1024]{1,0:T(8,128)(2,1)S(1)}, u32[]{:S(2)}, u32[]{:S(2)}) collective-permute-start(bf16[64,1024]{1,0:T(8,128)(2,1)S(1)} %broadcast_select_fusion.18), channel_id=1, source_target_pairs={{0,1},{1,0},{2,3},{3,2},{4,5},{5,4},{6,7},{7,6},{8,9},{9,8},{10,11... | collective-permute-start | bytes 393224 | tf_op jit(solution)/shard_map/ppermute | solution.py:74
  5.1 18.7 %copy-start.1 = (bf16[2,256,1024]{2,1,0:T(8,128)(2,1)S(1)}, bf16[2,256,1024]{2,1,0:T(8,128)(2,1)}, u32[]{:S(2)}) copy-start(bf16[2,256,1024]{2,1,0:T(8,128)(2,1)} %param.7) | copy-start | bytes 3145732
  5.1 18.7 %collective-permute-start.5 = (bf16[1,256,1024]{2,1,0:T(8,128)(2,1)S(1)}, bf16[1,256,1024]{2,1,0:T(8,128)(2,1)S(1)}, u32[]{:S(2)}, u32[]{:S(2)}) collective-permute-start(bf16[1,256,1024]{2,1,0:T(8,128)(2,1)S(1)} %broadcast_select_fusion.10), channel_id=1, source_target_pairs={{0,2},{2,0},{4,6},{6,4},{8,10},{10,8},{12,14},{14,12},{1,3},{3,1},... | collective-permute-start | bytes 1572872 | tf_op jit(solution)/shard_map/ppermute | solution.py:112
  8.0 2.9 %collective-permute-start.3 = (bf16[64,1024]{1,0:T(8,128)(2,1)S(1)}, bf16[64,1024]{1,0:T(8,128)(2,1)S(1)}, u32[]{:S(2)}, u32[]{:S(2)}) collective-permute-start(bf16[64,1024]{1,0:T(8,128)(2,1)S(1)} %broadcast_select_fusion.14), channel_id=1, source_target_pairs={{0,1},{1,0},{2,3},{3,2},{4,5},{5,4},{6,7},{7,6},{8,9},{9,8},{10,11... | collective-permute-start | bytes 393224 | tf_op jit(solution)/shard_map/ppermute | solution.py:74
  8.2 15.0 %collective-permute-start.1 = (bf16[1,128,1024]{2,1,0:T(8,128)(2,1)S(1)}, bf16[1,128,1024]{2,1,0:T(8,128)(2,1)S(1)}, u32[]{:S(2)}, u32[]{:S(2)}) collective-permute-start(bf16[1,128,1024]{2,1,0:T(8,128)(2,1)S(1)} %maximum_bitcast_fusion), channel_id=1, source_target_pairs={{0,8},{1,9},{2,10},{3,11},{4,12},{5,13},{6,14},{7,15},{8,0},{9,1},... | collective-permute-start | bytes 786440 | tf_op jit(solution)/shard_map/ppermute | solution.py:84
  23.3 17.9 %collective-permute-start.2 = (bf16[2,128,1024]{2,1,0:T(8,128)(2,1)S(1)}, bf16[2,128,1024]{2,1,0:T(8,128)(2,1)S(1)}, u32[]{:S(2)}, u32[]{:S(2)}) collective-permute-start(bf16[2,128,1024]{2,1,0:T(8,128)(2,1)S(1)} %constant_dynamic-update-slice_fusion), channel_id=1, source_target_pairs={{0,2},{1,5},{2,0},{3,7},{4,6},{5,1},{6,4},{7,3},{8,10},{9,13},{10,... | collective-permute-start | bytes 1572872 | tf_op jit(solution)/shard_map/ppermute | solution.py:84
  23.9 19.9 %collective-permute-start.8 = (bf16[1,256,1024]{2,1,0:T(8,128)(2,1)S(1)}, bf16[1,256,1024]{2,1,0:T(8,128)(2,1)S(1)}, u32[]{:S(2)}, u32[]{:S(2)}) collective-permute-start(bf16[1,256,1024]{2,1,0:T(8,128)(2,1)S(1)} %broadcast_select_fusion.7), channel_id=1, source_target_pairs={{0,2},{2,0},{4,6},{6,4},{8,10},{10,8},{12,14},{14,12},{1,3},{3,1},... | collective-permute-start | bytes 1572872 | tf_op jit(solution)/shard_map/ppermute | solution.py:112
  25.5 15.6 %collective-permute-start.4 = (bf16[1,128,1024]{2,1,0:T(8,128)(2,1)S(1)}, bf16[1,128,1024]{2,1,0:T(8,128)(2,1)S(1)}, u32[]{:S(2)}, u32[]{:S(2)}) collective-permute-start(bf16[1,128,1024]{2,1,0:T(8,128)(2,1)S(1)} %maximum_bitcast_fusion.1), channel_id=1, source_target_pairs={{0,8},{1,9},{2,10},{3,11},{4,12},{5,13},{6,14},{7,15},{8,0},{9,1},... | collective-permute-start | bytes 786440 | tf_op jit(solution)/shard_map/ppermute | solution.py:84
  25.8 9.9 %collective-permute-start.6 = (bf16[1,64,1024]{2,1,0:T(8,128)(2,1)S(1)}, bf16[1,64,1024]{2,1,0:T(8,128)(2,1)S(1)}, u32[]{:S(2)}, u32[]{:S(2)}) collective-permute-start(bf16[1,64,1024]{2,1,0:T(8,128)(2,1)S(1)} %slice.178), channel_id=1, source_target_pairs={{0,4},{2,6},{4,8},{6,10},{8,12},{10,14},{1,5},{3,7},{5,9},{7,11},{... | collective-permute-start | bytes 393224 | tf_op jit(solution)/shard_map/ppermute | solution.py:105
  31.7 7.3 %collective-permute-start.7 = (bf16[1,64,1024]{2,1,0:T(8,128)(2,1)S(1)}, bf16[1,64,1024]{2,1,0:T(8,128)(2,1)S(1)}, u32[]{:S(2)}, u32[]{:S(2)}) collective-permute-start(bf16[1,64,1024]{2,1,0:T(8,128)(2,1)S(1)} %slice.179), channel_id=1, source_target_pairs={{4,0},{6,2},{8,4},{10,6},{12,8},{14,10},{5,1},{7,3},{9,5},{11,7},{... | collective-permute-start | bytes 393224 | tf_op jit(solution)/shard_map/ppermute | solution.py:106
  43.9 20.0 %collective-permute-start.9 = (bf16[4,128,1024]{2,1,0:T(8,128)(2,1)S(1)}, bf16[4,128,1024]{2,1,0:T(8,128)(2,1)S(1)}, u32[]{:S(2)}, u32[]{:S(2)}) collective-permute-start(bf16[4,128,1024]{2,1,0:T(8,128)(2,1)S(1)} %pad_maximum_fusion.2), channel_id=1, source_target_pairs={{0,4},{1,3},{2,6},{3,1},{4,0},{5,7},{6,2},{7,5},{8,12},{9,11},{10,... | collective-permute-start | bytes 3145736 | tf_op jit(solution)/shard_map/ppermute | solution.py:84
  45.1 14.9 %collective-permute-start.10 = (bf16[2,128,1024]{2,1,0:T(8,128)(2,1)S(1)}, bf16[2,128,1024]{2,1,0:T(8,128)(2,1)S(1)}, u32[]{:S(2)}, u32[]{:S(2)}) collective-permute-start(bf16[2,128,1024]{2,1,0:T(8,128)(2,1)S(1)} %pad_maximum_fusion.6), channel_id=1, source_target_pairs={{0,2},{1,5},{2,0},{3,7},{4,6},{5,1},{6,4},{7,3},{8,10},{9,13},{10,... | collective-permute-start | bytes 1572872 | tf_op jit(solution)/shard_map/ppermute | solution.py:84
  63.9 4.2 %collective-permute-start.11 = (bf16[8,128,1024]{2,1,0:T(8,128)(2,1)S(1)}, bf16[8,128,1024]{2,1,0:T(8,128)(2,1)S(1)}, u32[]{:S(2)}, u32[]{:S(2)}) collective-permute-start(bf16[8,128,1024]{2,1,0:T(8,128)(2,1)S(1)} %constant_dynamic-update-slice_fusion.2.own.refs_7_.refs_5_), channel_id=1, source_target_pairs={{0,1},{1,0},{2,3},{3,2},{4,5},{5,4},{6,7},{7,6},{8,9},{9,8},{10,11... | collective-permute-start | bytes 6291464 | tf_op jit(solution)/shard_map/ppermute | solution.py:74
  64.1 17.7 %collective-permute-start.12 = (bf16[4,128,1024]{2,1,0:T(8,128)(2,1)S(1)}, bf16[4,128,1024]{2,1,0:T(8,128)(2,1)S(1)}, u32[]{:S(2)}, u32[]{:S(2)}) collective-permute-start(bf16[4,128,1024]{2,1,0:T(8,128)(2,1)S(1)} %pad_maximum_fusion.3), channel_id=1, source_target_pairs={{0,4},{1,3},{2,6},{3,1},{4,0},{5,7},{6,2},{7,5},{8,12},{9,11},{10,... | collective-permute-start | bytes 3145736 | tf_op jit(solution)/shard_map/ppermute | solution.py:84
  71.1 13.5 %collective-permute-start.14 = (bf16[1,128,1024]{2,1,0:T(8,128)(2,1)S(1)}, bf16[1,128,1024]{2,1,0:T(8,128)(2,1)S(1)}, u32[]{:S(2)}, u32[]{:S(2)}) collective-permute-start(bf16[1,128,1024]{2,1,0:T(8,128)(2,1)S(1)} %get-tuple-element.73.first), channel_id=1, source_target_pairs={{4,0},{6,2},{8,4},{10,6},{12,8},{14,10},{5,1},{7,3},{9,5},{11,7},{... | collective-permute-start | bytes 786440 | tf_op jit(solution)/shard_map/ppermute | solution.py:106
  72.4 12.2 %collective-permute-start.13 = (bf16[1,128,1024]{2,1,0:T(8,128)(2,1)S(1)}, bf16[1,128,1024]{2,1,0:T(8,128)(2,1)S(1)}, u32[]{:S(2)}, u32[]{:S(2)}) collective-permute-start(bf16[1,128,1024]{2,1,0:T(8,128)(2,1)S(1)} %get-tuple-element.74.last), channel_id=1, source_target_pairs={{0,4},{2,6},{4,8},{6,10},{8,12},{10,14},{1,5},{3,7},{5,9},{7,11},{... | collective-permute-start | bytes 786440 | tf_op jit(solution)/shard_map/ppermute | solution.py:105
  84.8 4.2 %collective-permute-start.15 = (bf16[8,128,1024]{2,1,0:T(8,128)(2,1)S(1)}, bf16[8,128,1024]{2,1,0:T(8,128)(2,1)S(1)}, u32[]{:S(2)}, u32[]{:S(2)}) collective-permute-start(bf16[8,128,1024]{2,1,0:T(8,128)(2,1)S(1)} %pad_maximum_fusion.own.refs_5_), channel_id=1, source_target_pairs={{0,1},{1,0},{2,3},{3,2},{4,5},{5,4},{6,7},{7,6},{8,9},{9,8},{10,11... | collective-permute-start | bytes 6291464 | tf_op jit(solution)/shard_map/ppermute | solution.py:74
  92.2 8.5 %collective-permute-start.16 = (bf16[1,128,512]{2,1,0:T(8,128)(2,1)S(1)}, bf16[1,128,512]{2,1,0:T(8,128)(2,1)S(1)}, u32[]{:S(2)}, u32[]{:S(2)}) collective-permute-start(bf16[1,128,512]{2,1,0:T(8,128)(2,1)S(1)} %get-tuple-element.85), channel_id=1, source_target_pairs={{0,4},{2,6},{4,8},{6,10},{8,12},{10,14},{1,5},{3,7},{5,9},{7,11},{... | collective-permute-start | bytes 393224 | tf_op jit(solution)/shard_map/ppermute | solution.py:105
  95.8 7.2 %collective-permute-start.17 = (bf16[1,128,512]{2,1,0:T(8,128)(2,1)S(1)}, bf16[1,128,512]{2,1,0:T(8,128)(2,1)S(1)}, u32[]{:S(2)}, u32[]{:S(2)}) collective-permute-start(bf16[1,128,512]{2,1,0:T(8,128)(2,1)S(1)} %get-tuple-element.86), channel_id=1, source_target_pairs={{4,0},{6,2},{8,4},{10,6},{12,8},{14,10},{5,1},{7,3},{9,5},{11,7},{... | collective-permute-start | bytes 393224 | tf_op jit(solution)/shard_map/ppermute | solution.py:106
  102.9 5.5 %collective-permute-start.18 = (bf16[8,128,1024]{2,1,0:T(8,128)(2,1)S(1)}, bf16[8,128,1024]{2,1,0:T(8,128)(2,1)S(1)}, u32[]{:S(2)}, u32[]{:S(2)}) collective-permute-start(bf16[8,128,1024]{2,1,0:T(8,128)(2,1)S(1)} %get-tuple-element.88), channel_id=1, source_target_pairs={{0,1},{1,0},{2,3},{3,2},{4,5},{5,4},{6,7},{7,6},{8,9},{9,8},{10,11... | collective-permute-start | bytes 6291464 | tf_op jit(solution)/shard_map/ppermute | solution.py:74
  112.9 6.2 %collective-permute-start.20 = (bf16[8,128,1024]{2,1,0:T(8,128)(2,1)S(1)}, bf16[8,128,1024]{2,1,0:T(8,128)(2,1)S(1)}, u32[]{:S(2)}, u32[]{:S(2)}) collective-permute-start(bf16[8,128,1024]{2,1,0:T(8,128)(2,1)S(1)} %get-tuple-element.101), channel_id=1, source_target_pairs={{0,1},{1,0},{2,3},{3,2},{4,5},{5,4},{6,7},{7,6},{8,9},{9,8},{10,11... | collective-permute-start | bytes 6291464 | tf_op jit(solution)/shard_map/ppermute | solution.py:74
  113.7 16.3 %collective-permute-start.19 = (bf16[4,128,1024]{2,1,0:T(8,128)(2,1)S(1)}, bf16[4,128,1024]{2,1,0:T(8,128)(2,1)S(1)}, u32[]{:S(2)}, u32[]{:S(2)}) collective-permute-start(bf16[4,128,1024]{2,1,0:T(8,128)(2,1)S(1)} %slice.275), channel_id=1, source_target_pairs={{0,4},{1,3},{2,6},{3,1},{4,0},{5,7},{6,2},{7,5},{8,12},{9,11},{10,... | collective-permute-start | bytes 3145736 | tf_op jit(solution)/shard_map/ppermute | solution.py:84
  114.3 13.7 %collective-permute-start.21 = (bf16[1,64,512]{2,1,0:T(8,128)(2,1)S(1)}, bf16[1,64,512]{2,1,0:T(8,128)(2,1)S(1)}, u32[]{:S(2)}, u32[]{:S(2)}) collective-permute-start(bf16[1,64,512]{2,1,0:T(8,128)(2,1)S(1)} %get-tuple-element.104), channel_id=1, source_target_pairs={{0,4},{2,6},{4,8},{6,10},{8,12},{10,14},{1,5},{3,7},{5,9},{7,11},{... | collective-permute-start | bytes 196616 | tf_op jit(solution)/shard_map/ppermute | solution.py:105
  117.7 12.3 %collective-permute-start.22 = (bf16[1,64,512]{2,1,0:T(8,128)(2,1)S(1)}, bf16[1,64,512]{2,1,0:T(8,128)(2,1)S(1)}, u32[]{:S(2)}, u32[]{:S(2)}) collective-permute-start(bf16[1,64,512]{2,1,0:T(8,128)(2,1)S(1)} %get-tuple-element.105), channel_id=1, source_target_pairs={{4,0},{6,2},{8,4},{10,6},{12,8},{14,10},{5,1},{7,3},{9,5},{11,7},{... | collective-permute-start | bytes 196616 | tf_op jit(solution)/shard_map/ppermute | solution.py:106
  130.1 20.4 %collective-permute-start.23 = (bf16[4,128,1024]{2,1,0:T(8,128)(2,1)S(1)}, bf16[4,128,1024]{2,1,0:T(8,128)(2,1)S(1)}, u32[]{:S(2)}, u32[]{:S(2)}) collective-permute-start(bf16[4,128,1024]{2,1,0:T(8,128)(2,1)S(1)} %slice.274), channel_id=1, source_target_pairs={{0,4},{1,3},{2,6},{3,1},{4,0},{5,7},{6,2},{7,5},{8,12},{9,11},{10,... | collective-permute-start | bytes 3145736 | tf_op jit(solution)/shard_map/ppermute | solution.py:84
  131.2 14.9 %collective-permute-start.24 = (bf16[2,128,1024]{2,1,0:T(8,128)(2,1)S(1)}, bf16[2,128,1024]{2,1,0:T(8,128)(2,1)S(1)}, u32[]{:S(2)}, u32[]{:S(2)}) collective-permute-start(bf16[2,128,1024]{2,1,0:T(8,128)(2,1)S(1)} %slice.277), channel_id=1, source_target_pairs={{0,2},{1,9},{2,0},{3,11},{4,6},{5,13},{6,4},{7,15},{8,10},{9,1},{1... | collective-permute-start | bytes 1572872 | tf_op jit(solution)/shard_map/ppermute | solution.py:84
  150.7 9.8 %collective-permute-start.29 = (bf16[1,128,1024]{2,1,0:T(8,128)(2,1)S(1)}, bf16[1,128,1024]{2,1,0:T(8,128)(2,1)S(1)}, u32[]{:S(2)}, u32[]{:S(2)}) collective-permute-start(bf16[1,128,1024]{2,1,0:T(8,128)(2,1)S(1)} %slice.278), channel_id=1, source_target_pairs={{0,8},{1,5},{2,10},{3,7},{4,12},{5,1},{6,14},{7,3},{8,0},{9,13},{1... | collective-permute-start | bytes 786440 | tf_op jit(solution)/shard_map/ppermute | solution.py:84
  151.1 9.5 %collective-permute-start.25 = (bf16[2,128,1024]{2,1,0:T(8,128)(2,1)S(1)}, bf16[2,128,1024]{2,1,0:T(8,128)(2,1)S(1)}, u32[]{:S(2)}, u32[]{:S(2)}) collective-permute-start(bf16[2,128,1024]{2,1,0:T(8,128)(2,1)S(1)} %slice.276), channel_id=1, source_target_pairs={{0,2},{1,5},{2,0},{3,7},{4,6},{5,1},{6,4},{7,3},{8,10},{9,13},{10,... | collective-permute-start | bytes 1572872 | tf_op jit(solution)/shard_map/ppermute | solution.py:84
  160.6 3.4 %collective-permute-start.30 = (f32[64,1024]{1,0:T(8,128)S(1)}, f32[64,1024]{1,0:T(8,128)S(1)}, u32[]{:S(2)}, u32[]{:S(2)}) collective-permute-start(f32[64,1024]{1,0:T(8,128)S(1)} %fusion.4), channel_id=1, source_target_pairs={{0,1},{1,0},{2,3},{3,2},{4,5},{5,4},{6,7},{7,6},{8,9},{9,8},{10,11... | collective-permute-start | bytes 786440 | tf_op jit(solution)/shard_map/ppermute | solution.py:74
  160.8 15.3 %collective-permute-start.26 = (bf16[1,128,1024]{2,1,0:T(8,128)(2,1)S(1)}, bf16[1,128,1024]{2,1,0:T(8,128)(2,1)S(1)}, u32[]{:S(2)}, u32[]{:S(2)}) collective-permute-start(bf16[1,128,1024]{2,1,0:T(8,128)(2,1)S(1)} %slice.279), channel_id=1, source_target_pairs={{0,8},{1,9},{2,10},{3,11},{4,12},{5,13},{6,14},{7,15},{8,0},{9,1},... | collective-permute-start | bytes 786440 | tf_op jit(solution)/shard_map/ppermute | solution.py:84
  163.6 12.6 %collective-permute-start.27 = (bf16[1,256,1024]{2,1,0:T(8,128)(2,1)S(1)}, bf16[1,256,1024]{2,1,0:T(8,128)(2,1)S(1)}, u32[]{:S(2)}, u32[]{:S(2)}) collective-permute-start(bf16[1,256,1024]{2,1,0:T(8,128)(2,1)S(1)} %broadcast_select_fusion.2), channel_id=1, source_target_pairs={{0,2},{2,0},{4,6},{6,4},{8,10},{10,8},{12,14},{14,12},{1,3},{3,1},... | collective-permute-start | bytes 1572872 | tf_op jit(solution)/shard_map/ppermute | solution.py:112
  176.3 1.6 collective-permute-start.28
  (3 other events, 31.2 us)
